TPU v7x, 128 devices: a whole 4x4x4 slice. The times are simulated.
128 devices in a mesh: fsdp: 16 (over z_lo, y, core), tp: 8 (over x, z_hi).
Axes of the slice: x: 4, y: 4, z: 4 (z_hi: 2, z_lo: 2; z = z_hi * 2 + z_lo), core: 2. Of those that a mesh axis runs over, the one named last changes fastest.
Arguments:
- probe_states: bfloat16 [256, 16384], P('fsdp'), may hold values from -6 to 6
- wq_master: float32 [16384, 4096], P(('fsdp', 'tp')), may hold values from -1 to 1
- wq_first: float32 [16384, 4096], P(('fsdp', 'tp')), may hold values from -6 to 6
- wq_second: float32 [16384, 4096], P(('fsdp', 'tp')), may hold values from 0.25 to 4
- wq_grad: float32 [16384, 4096], P('fsdp', 'tp'), may hold values from -6 to 6
- wkv_master: float32 [16384, 512], P(('fsdp', 'tp')), may hold values from -0.046875 to 0.046875
- wkv_first: float32 [16384, 512], P(('fsdp', 'tp')), may hold values from -6 to 6
- wkv_second: float32 [16384, 512], P(('fsdp', 'tp')), may hold values from 0.25 to 4
- wkv_grad: float32 [16384, 512], P(('fsdp', 'tp')), may hold values from -6 to 6
Outputs:
- wq_updated: float32 [16384, 4096], P('fsdp', 'tp')
- wq_first_new: float32 [16384, 4096], P('fsdp', 'tp')
- wq_second_new: float32 [16384, 4096], P('fsdp', 'tp')
- wkv_updated: float32 [16384, 512], P(('fsdp', 'tp'))
- wkv_first_new: float32 [16384, 512], P(('fsdp', 'tp'))
- wkv_second_new: float32 [16384, 512], P(('fsdp', 'tp'))
- probe_query: bfloat16 [256, 4096], P('fsdp', 'tp')
- probe_keyvalue: bfloat16 [256, 512], replicated
All inputs are finite; a program needn't handle non-finite values.
Results may differ from a plain program's by a relative error of at most 0.008.
Values may be sent and summed in bfloat16 or wider, within the bound.
A program may use at most 128 MiB of HBM per device.

v0:
```python
import math

import jax
import jax.numpy as jnp
from jax import lax
from jax.sharding import PartitionSpec as P

BETA_ONE = 0.9
BETA_TWO = 0.95
LEARN_RATE = 0.001
EPSILON = 1e-08
CORRECT_ONE = 1.0 - math.exp(1000.0 * math.log(0.9))
CORRECT_TWO = 1.0 - math.exp(1000.0 * math.log(0.95))


def adam_step(master, first, second, grad):
    first_new = BETA_ONE * first + (1.0 - BETA_ONE) * grad
    second_new = BETA_TWO * second + (1.0 - BETA_TWO) * grad * grad
    update = first_new / CORRECT_ONE / (jnp.sqrt(second_new / CORRECT_TWO) + EPSILON)
    return (master - LEARN_RATE * update, first_new, second_new)


def body(
    probe_states,
    wq_master,
    wq_first,
    wq_second,
    wq_grad,
    wkv_master,
    wkv_first,
    wkv_second,
    wkv_grad,
):
    master, first, second = (
        lax.all_to_all(wq_master, "tp", split_axis=1, concat_axis=0, tiled=True),
        lax.all_to_all(wq_first, "tp", split_axis=1, concat_axis=0, tiled=True),
        lax.all_to_all(wq_second, "tp", split_axis=1, concat_axis=0, tiled=True),
    )
    wq_new, wq_mom, wq_var = adam_step(master, first, second, wq_grad)
    wkv_new, wkv_mom, wkv_var = adam_step(wkv_master, wkv_first, wkv_second, wkv_grad)
    columns = lax.all_to_all(probe_states, "fsdp", split_axis=1, concat_axis=0, tiled=True)
    tp_rank = lax.axis_index("tp")
    kv_rows = wkv_master.shape[0]
    own_columns = lax.dynamic_slice_in_dim(columns, tp_rank * kv_rows, kv_rows, 1)
    kv_term = jnp.dot(own_columns, wkv_new.astype(jnp.bfloat16), preferred_element_type=jnp.float32)
    probe_keyvalue = lax.psum(kv_term, ("fsdp", "tp")).astype(jnp.bfloat16)
    wq_low = wq_new.astype(jnp.bfloat16)
    queries = jnp.dot(
        probe_states,
        lax.all_gather(wq_low, "fsdp", axis=0, tiled=True),
        preferred_element_type=jnp.float32,
    )
    probe_query = queries.astype(jnp.bfloat16)
    return (wq_new, wq_mom, wq_var, wkv_new, wkv_mom, wkv_var, probe_query, probe_keyvalue)


def solution(mesh):
    return jax.shard_map(
        body,
        mesh=mesh,
        in_specs=(
            P("fsdp", None),
            P(("fsdp", "tp"), None),
            P(("fsdp", "tp"), None),
            P(("fsdp", "tp"), None),
            P("fsdp", "tp"),
            P(("fsdp", "tp"), None),
            P(("fsdp", "tp"), None),
            P(("fsdp", "tp"), None),
            P(("fsdp", "tp"), None),
        ),
        out_specs=(
            P("fsdp", "tp"),
            P("fsdp", "tp"),
            P("fsdp", "tp"),
            P(("fsdp", "tp"), None),
            P(("fsdp", "tp"), None),
            P(("fsdp", "tp"), None),
            P("fsdp", "tp"),
            P(),
        ),
        check_vma=False,
    )
```

profile of v0, /device:TPU:1, one launch (start us, length us, event | category | flops | bytes accessed | tf_op | source)
XLA Modules:
  0.0 238.8 jit_solution(16143131540047762686)
XLA Ops:
  7.2 3.1 %copy.39 = f32[16,8,8,512]{3,2,0,1:T(8,128)} copy(f32[16,8,8,512]{3,2,1,0:T(8,128)} %bitcast.42) | data formatting | bytes 4194304 | tf_op jit(solution)/shard_map/all_to_all | solution.py:37
  10.3 8.2 %all-to-all-start.2 = ((f32[128,8,512]{2,0,1:T(8,128)}), f32[128,8,512]{2,0,1:T(8,128)S(1)}, u32[]{:S(2)}, u32[]{:S(2)}) async-start(f32[128,8,512]{2,0,1:T(8,128)} %bitcast.40), calls=%async_computation.2 | async-start | bytes 4194304 | tf_op jit(solution)/shard_map/all_to_all | solution.py:37
  18.5 3.1 %copy.40 = f32[16,8,8,512]{3,2,0,1:T(8,128)} copy(f32[16,8,8,512]{3,2,1,0:T(8,128)} %bitcast.43) | data formatting | bytes 4194304 | tf_op jit(solution)/shard_map/all_to_all | solution.py:36
  21.6 27.5 %all-to-all-done.2 = f32[128,8,512]{2,0,1:T(8,128)S(1)} async-done(((f32[128,8,512]{2,0,1:T(8,128)}), f32[128,8,512]{2,0,1:T(8,128)S(1)}, u32[]{:S(2)}, u32[]{:S(2)}) %all-to-all-start.2) | async-done | bytes 2097184 | tf_op jit(solution)/shard_map/all_to_all | solution.py:37
  49.1 0.0 copy-start
  49.1 1.3 copy-done
  50.4 4.4 %all-to-all-start.1 = ((f32[128,8,512]{2,0,1:T(8,128)}), f32[128,8,512]{2,0,1:T(8,128)}, u32[]{:S(2)}, u32[]{:S(2)}) async-start(f32[128,8,512]{2,0,1:T(8,128)} %bitcast.39), calls=%async_computation.1 | async-start | bytes 4194304 | tf_op jit(solution)/shard_map/all_to_all | solution.py:36
  54.8 3.2 %copy.41 = f32[16,8,8,512]{3,2,0,1:T(8,128)} copy(f32[16,8,8,512]{3,2,1,0:T(8,128)} %bitcast.44) | data formatting | bytes 4194304 | tf_op jit(solution)/shard_map/all_to_all | solution.py:35
  57.9 26.7 %all-to-all-done.1 = f32[128,8,512]{2,0,1:T(8,128)} async-done(((f32[128,8,512]{2,0,1:T(8,128)}), f32[128,8,512]{2,0,1:T(8,128)}, u32[]{:S(2)}, u32[]{:S(2)}) %all-to-all-start.1) | async-done | bytes 2097184 | tf_op jit(solution)/shard_map/all_to_all | solution.py:36
  84.6 3.6 %all-to-all-start = ((f32[128,8,512]{2,0,1:T(8,128)}), f32[128,8,512]{2,0,1:T(8,128)S(1)}, u32[]{:S(2)}, u32[]{:S(2)}) async-start(f32[128,8,512]{2,0,1:T(8,128)} %bitcast.38), calls=%async_computation | async-start | bytes 4194304 | tf_op jit(solution)/shard_map/all_to_all | solution.py:35
  88.2 0.0 all-gather.2.cloned.1.call-start
  88.2 3.3 %broadcast_multiply_fusion = f32[128,8,512]{2,0,1:T(8,128)} fusion(f32[128,8,512]{2,0,1:T(8,128)} %copy-done), kind=kLoop, calls=%fused_computation.9 | loop fusion | flops 524288 | bytes 4194304 | tf_op jit(solution)/shard_map/mul | solution.py:18
  91.5 3.3 %broadcast_multiply_fusion.1 = f32[128,8,512]{2,0,1:T(8,128)} fusion(f32[128,8,512]{2,0,1:T(8,128)} %all-to-all-done.1), kind=kLoop, calls=%fused_computation.10 | loop fusion | flops 524288 | bytes 4194304 | tf_op jit(solution)/shard_map/mul | solution.py:17
  94.8 0.0 copy-start.1
  94.8 22.8 %all-to-all-done = f32[128,8,512]{2,0,1:T(8,128)S(1)} async-done(((f32[128,8,512]{2,0,1:T(8,128)}), f32[128,8,512]{2,0,1:T(8,128)S(1)}, u32[]{:S(2)}, u32[]{:S(2)}) %all-to-all-start) | async-done | bytes 2097184 | tf_op jit(solution)/shard_map/all_to_all | solution.py:35
  117.5 6.7 %fusion.7 = (bf16[1024,512]{1,0:T(8,128)(2,1)}, f32[1024,512]{1,0:T(8,128)}, f32[1024,512]{1,0:T(8,128)}, f32[1024,512]{1,0:T(8,128)}) fusion(f32[128,8,512]{2,0,1:T(8,128)S(1)} %all-to-all-done, f32[1024,512]{1,0:T(8,128)} %param.13, f32[128,8,512]{2,0,1:T(8,128)} %broadcast_multiply_fusion, f32[128,8,512]{2,0,1:T(8,128)} %broadcast_multiply_fusion.1), kind=kLoop, calls=%fused_computation.20 | loop fusion | flops 5242880 | bytes 15728640 | tf_op jit(solution)/shard_map/convert_element_type | solution.py:47
  124.3 0.0 copy-start.3
  124.3 0.0 copy-start.4
  124.3 0.0 copy-start.5
  124.3 0.0 copy-start.6
  124.3 0.0 all-gather.2.cloned.1.call-update
  124.3 0.0 copy-done.1
  124.3 0.9 copy.42
  125.2 7.0 %all-to-all-start.3 = ((bf16[16,16,1024]{2,0,1:T(8,128)(2,1)}), bf16[16,16,1024]{2,0,1:T(8,128)(2,1)S(1)}, u32[]{:S(2)}, u32[]{:S(2)}) async-start(bf16[16,16,1024]{2,0,1:T(8,128)(2,1)} %bitcast.37), calls=%async_computation.3 | async-start | bytes 1048576 | tf_op jit(solution)/shard_map/all_to_all | solution.py:41
  132.2 0.0 copy-done.3
  132.2 0.0 copy-done.4
  132.2 0.0 copy-done.5
  132.2 0.0 copy-done.6
  132.2 0.9 multiply_subtract_fusion
  133.1 0.0 copy-start.2
  133.2 13.5 %all-to-all-done.3 = bf16[16,16,1024]{2,0,1:T(8,128)(2,1)S(1)} async-done(((bf16[16,16,1024]{2,0,1:T(8,128)(2,1)}), bf16[16,16,1024]{2,0,1:T(8,128)(2,1)S(1)}, u32[]{:S(2)}, u32[]{:S(2)}) %all-to-all-start.3) | async-done | bytes 524320 | tf_op jit(solution)/shard_map/all_to_all | solution.py:41
  146.6 0.2 fusion.3
  146.8 68.1 %all-reduce.1 = bf16[256,512]{1,0:T(8,128)(2,1)} all-reduce(f32[256,512]{1,0:T(8,128)S(1)} %fusion.3), channel_id=1, replica_groups=mesh['fsdp'=16,'tp'=8] {'fsdp','tp'}, use_global_device_ids=true, to_apply=%region_0.0 | all-reduce | flops 131072 | bytes 786432 | tf_op jit(solution)/shard_map/psum | solution.py:46
  214.9 8.3 %all-gather.2.cloned.1.call-done = bf16[16384,512]{1,0:T(8,128)(2,1)} async-done(((bf16[1024,512]{1,0:T(8,128)(2,1)}), bf16[16384,512]{1,0:T(8,128)(2,1)}) %all-gather.2.cloned.1.call-update) | async-done | bytes 16777232 | tf_op jit(solution)/shard_map/all_gather | solution.py:50
  223.3 8.6 %fusion.1 = bf16[16,512]{1,0:T(8,128)(2,1)} fusion(bf16[16,16384]{1,0:T(8,128)(2,1)S(1)} %copy-done.1, bf16[16384,512]{1,0:T(8,128)(2,1)} %all-gather.2.cloned.1.call-done), kind=kOutput, calls=%fused_computation.8 | convolution fusion | flops 268443648 | bytes 17317888 | tf_op jit(solution)/shard_map/dot_general | solution.py:48
  231.9 0.0 copy-done.2
Async XLA Ops:
  10.3 38.8 %all-to-all-start.2 = ((f32[128,8,512]{2,0,1:T(8,128)}), f32[128,8,512]{2,0,1:T(8,128)S(1)}, u32[]{:S(2)}, u32[]{:S(2)}) async-start(f32[128,8,512]{2,0,1:T(8,128)} %bitcast.40), calls=%async_computation.2 | async-start | bytes 4194304 | tf_op jit(solution)/shard_map/all_to_all | solution.py:37
  49.1 1.3 copy-start
  50.4 34.2 %all-to-all-start.1 = ((f32[128,8,512]{2,0,1:T(8,128)}), f32[128,8,512]{2,0,1:T(8,128)}, u32[]{:S(2)}, u32[]{:S(2)}) async-start(f32[128,8,512]{2,0,1:T(8,128)} %bitcast.39), calls=%async_computation.1 | async-start | bytes 4194304 | tf_op jit(solution)/shard_map/all_to_all | solution.py:36
  84.6 33.0 %all-to-all-start = ((f32[128,8,512]{2,0,1:T(8,128)}), f32[128,8,512]{2,0,1:T(8,128)S(1)}, u32[]{:S(2)}, u32[]{:S(2)}) async-start(f32[128,8,512]{2,0,1:T(8,128)} %bitcast.38), calls=%async_computation | async-start | bytes 4194304 | tf_op jit(solution)/shard_map/all_to_all | solution.py:35
  88.2 135.1 %all-gather.2.cloned.1.call-start = ((), (), s32[]{:S(2)}) async-start(), calls=%async_computation.4 | async-start | bytes 17825792 | tf_op jit(solution)/shard_map/all_gather | solution.py:50
  94.8 29.5 %copy-start.1 = (bf16[16,16384]{1,0:T(8,128)(2,1)S(1)}, bf16[16,16384]{1,0:T(8,128)(2,1)}, u32[]{:S(2)}) copy-start(bf16[16,16384]{1,0:T(8,128)(2,1)} %param.9) | copy-start | bytes 1572868
  124.3 7.9 %copy-start.3 = (f32[128,512]{1,0:T(8,128)S(1)}, f32[128,512]{1,0:T(8,128)}, u32[]{:S(2)}) copy-start(f32[128,512]{1,0:T(8,128)} %param.14) | copy-start | bytes 786436
  124.3 7.9 %copy-start.4 = (f32[128,512]{1,0:T(8,128)S(1)}, f32[128,512]{1,0:T(8,128)}, u32[]{:S(2)}) copy-start(f32[128,512]{1,0:T(8,128)} %param.17) | copy-start | bytes 786436
  124.3 7.9 %copy-start.5 = (f32[128,512]{1,0:T(8,128)S(1)}, f32[128,512]{1,0:T(8,128)}, u32[]{:S(2)}) copy-start(f32[128,512]{1,0:T(8,128)} %param.16) | copy-start | bytes 786436
  124.3 7.9 %copy-start.6 = (f32[128,512]{1,0:T(8,128)S(1)}, f32[128,512]{1,0:T(8,128)}, u32[]{:S(2)}) copy-start(f32[128,512]{1,0:T(8,128)} %param.15) | copy-start | bytes 786436
  125.2 21.4 %all-to-all-start.3 = ((bf16[16,16,1024]{2,0,1:T(8,128)(2,1)}), bf16[16,16,1024]{2,0,1:T(8,128)(2,1)S(1)}, u32[]{:S(2)}, u32[]{:S(2)}) async-start(bf16[16,16,1024]{2,0,1:T(8,128)(2,1)} %bitcast.37), calls=%async_computation.3 | async-start | bytes 1048576 | tf_op jit(solution)/shard_map/all_to_all | solution.py:41
  133.1 98.8 %copy-start.2 = (f32[128,512]{1,0:T(8,128)}, f32[128,512]{1,0:T(8,128)S(1)}, u32[]{:S(2)}) copy-start(f32[128,512]{1,0:T(8,128)S(1)} %get-tuple-element.12) | copy-start | bytes 786436
Sparse Core Ops, SparseCore 0:
  124.5 98.7 all-gather.1
where the time goes:
time: 239 us
  waiting for transfers between devices  98.7 us (41%)
  blocking collectives  68.1 us (28%)
  starting transfers between devices  23.1 us (10%)
  other arithmetic  14.3 us (6%)
  between operations  14.1 us (6%)
  local copies, waits for them, and re-layouts  11.7 us (5%)
  matrix products  8.86 us (4%)
    psum x1, blocking collectives, body(): probe_keyvalue = lax.psum(kv_term, ('fsdp', 'tp')).astype(jnp.bfloat16)  68.1 us
    all_to_all x1, waiting for transfers between devices, body(): lax.all_to_all(wq_second, 'tp', split_axis=1, concat_axis=0, tiled=True)  27.5 us
    all_to_all x1, waiting for transfers between devices, body(): lax.all_to_all(wq_first, 'tp', split_axis=1, concat_axis=0, tiled=True)  26.7 us
    all_to_all x1, waiting for transfers between devices, body(): lax.all_to_all(wq_master, 'tp', split_axis=1, concat_axis=0, tiled=True)  22.8 us
    all_to_all x1, waiting for transfers between devices, body(): lax.all_to_all(probe_states, 'fsdp', split_axis=1, concat_axis=0, tiled=T...  13.5 us
    dot_general x1, matrix products, body(): jnp.dot(probe_states, lax.all_gather(wq_low, 'fsdp', axis=0, tiled=True),...  8.65 us
    all_gather x1, waiting for transfers between devices, body(): lax.all_gather(wq_low, 'fsdp', axis=0, tiled=True)  8.34 us
    all_to_all x1, starting transfers between devices, body(): lax.all_to_all(wq_second, 'tp', split_axis=1, concat_axis=0, tiled=True)  8.15 us
  transfers between devices with their start and end apart: 5, of which 5 were waited for; matrix products, arithmetic and copies ran while one was open for 6% of the time, Pallas kernels for 0%

commit v1 on v0

--- a/solution.py
+++ b/solution.py
@@ -20,6 +20,16 @@
     return (master - LEARN_RATE * update, first_new, second_new)
 
 
+def gather_rows(x, axis_name, size):
+    copies = jnp.broadcast_to(x[None], (size,) + x.shape).reshape((size * x.shape[0],) + x.shape[1:])
+    return lax.all_to_all(copies, axis_name, split_axis=0, concat_axis=0, tiled=True)
+
+
+def scatter_sum_rows(x, axis_name, size):
+    parts = lax.all_to_all(x, axis_name, split_axis=0, concat_axis=0, tiled=True)
+    return parts.reshape((size, x.shape[0] // size) + x.shape[1:]).sum(axis=0)
+
+
 def body(
     probe_states,
     wq_master,
@@ -31,26 +41,25 @@
     wkv_second,
     wkv_grad,
 ):
+    fsdp = lax.axis_size("fsdp")
+    tp = lax.axis_size("tp")
+    columns = lax.all_to_all(probe_states, "fsdp", split_axis=1, concat_axis=0, tiled=True)
+    wkv_new, wkv_mom, wkv_var = adam_step(wkv_master, wkv_first, wkv_second, wkv_grad)
+    wkv_rows = gather_rows(wkv_new.astype(jnp.bfloat16), "tp", tp)
+    kv_term = jnp.dot(columns, wkv_rows, preferred_element_type=jnp.float32)
+
     master, first, second = (
         lax.all_to_all(wq_master, "tp", split_axis=1, concat_axis=0, tiled=True),
         lax.all_to_all(wq_first, "tp", split_axis=1, concat_axis=0, tiled=True),
         lax.all_to_all(wq_second, "tp", split_axis=1, concat_axis=0, tiled=True),
     )
     wq_new, wq_mom, wq_var = adam_step(master, first, second, wq_grad)
-    wkv_new, wkv_mom, wkv_var = adam_step(wkv_master, wkv_first, wkv_second, wkv_grad)
-    columns = lax.all_to_all(probe_states, "fsdp", split_axis=1, concat_axis=0, tiled=True)
-    tp_rank = lax.axis_index("tp")
-    kv_rows = wkv_master.shape[0]
-    own_columns = lax.dynamic_slice_in_dim(columns, tp_rank * kv_rows, kv_rows, 1)
-    kv_term = jnp.dot(own_columns, wkv_new.astype(jnp.bfloat16), preferred_element_type=jnp.float32)
-    probe_keyvalue = lax.psum(kv_term, ("fsdp", "tp")).astype(jnp.bfloat16)
-    wq_low = wq_new.astype(jnp.bfloat16)
-    queries = jnp.dot(
-        probe_states,
-        lax.all_gather(wq_low, "fsdp", axis=0, tiled=True),
-        preferred_element_type=jnp.float32,
-    )
-    probe_query = queries.astype(jnp.bfloat16)
+    q_term = jnp.dot(columns, wq_new.astype(jnp.bfloat16), preferred_element_type=jnp.float32)
+
+    sums = scatter_sum_rows(jnp.concatenate([q_term, kv_term], axis=1), "fsdp", fsdp)
+    q_cols = q_term.shape[1]
+    probe_query = sums[:, :q_cols].astype(jnp.bfloat16)
+    probe_keyvalue = gather_rows(sums[:, q_cols:].astype(jnp.bfloat16), "fsdp", fsdp)
     return (wq_new, wq_mom, wq_var, wkv_new, wkv_mom, wkv_var, probe_query, probe_keyvalue)
 
 

time: 239 us -> 190 us (0.79)
  blocking collectives: 68.1 us -> 32.9 us
  between operations: 14.1 us -> 0.75 us
  matrix products: 8.86 us -> 3.04 us
  local copies, waits for them, and re-layouts: 11.7 us -> 17 us
  starting transfers between devices: 23.1 us -> 27.3 us
  waiting for transfers between devices: 98.7 us -> 95.6 us
    psum x1 -> x0, blocking collectives: 68.1 us -> none  [body(): probe_keyvalue = lax.psum(kv_term, ('fsdp', 'tp')).astype(jnp.bfloat16)]
    all_to_all x0 -> x2, blocking collectives: none -> 32.9 us  [the longest x1 21.8 us: scatter_sum_rows(): lax.all_to_all(x, axis_name, split_axis=0, concat_axis=0, tiled=True)]
    all_to_all x0 -> x1, waiting for transfers between devices: none -> 12.1 us  [gather_rows(): lax.all_to_all(copies, axis_name, split_axis=0, concat_axis=0, tiled=True)]
    all_gather x1 -> x0, waiting for transfers between devices: 8.34 us -> none  [body(): lax.all_gather(wq_low, 'fsdp', axis=0, tiled=True)]
    all_to_all x0 -> x1, starting transfers between devices: none -> 7.04 us  [gather_rows(): lax.all_to_all(copies, axis_name, split_axis=0, concat_axis=0, tiled=True)]
    dot_general x2, matrix products: 8.86 us -> 3.04 us  [the longest x1 2.55 us: body(): kv_term = jnp.dot(columns, wkv_rows, preferred_element_type=jnp.float32)]
    sub x1, other arithmetic: 0.95 us -> 6.74 us  [adam_step(): return (master - LEARN_RATE * update, first_new, second_new)]
    convert_element_type x1, other arithmetic: 6.74 us -> 0.97 us  [body(): wkv_rows = gather_rows(wkv_new.astype(jnp.bfloat16), 'tp', tp)]
  transfers between devices with their start and end apart: 5 -> 5, of which waited for: 5 -> 5; matrix products, arithmetic and copies ran while one was open for 6% -> 9% of each run, Pallas kernels for 0% -> 0%
where the time goes in v1:
time: 190 us; the launch traced here: 189 us
  waiting for transfers between devices  95.6 us (50%)
  blocking collectives  32.9 us (17%)
  starting transfers between devices  27.3 us (14%)
  local copies, waits for them, and re-layouts  17 us (9%)
  other arithmetic  12.8 us (7%)
  matrix products  3.04 us (2%)
    all_to_all x1, waiting for transfers between devices, body(): lax.all_to_all(wq_second, 'tp', split_axis=1, concat_axis=0, tiled=True)  26.8 us
    all_to_all x1, waiting for transfers between devices, body(): lax.all_to_all(wq_first, 'tp', split_axis=1, concat_axis=0, tiled=True)  26.4 us
    all_to_all x1, blocking collectives, scatter_sum_rows(): lax.all_to_all(x, axis_name, split_axis=0, concat_axis=0, tiled=True)  21.8 us
    all_to_all x1, waiting for transfers between devices, body(): lax.all_to_all(wq_master, 'tp', split_axis=1, concat_axis=0, tiled=True)  21.8 us
    all_to_all x1, waiting for transfers between devices, gather_rows(): lax.all_to_all(copies, axis_name, split_axis=0, concat_axis=0, tiled=True)  12.1 us
    all_to_all x1, blocking collectives, gather_rows(): lax.all_to_all(copies, axis_name, split_axis=0, concat_axis=0, tiled=True)  11.1 us
    all_to_all x1, waiting for transfers between devices, body(): lax.all_to_all(probe_states, 'fsdp', split_axis=1, concat_axis=0, tiled=T...  8.49 us
    all_to_all x1, starting transfers between devices, body(): lax.all_to_all(probe_states, 'fsdp', split_axis=1, concat_axis=0, tiled=T...  7.33 us
  transfers between devices with their start and end apart: 5, of which 5 were waited for; matrix products, arithmetic and copies ran while one was open for 9% of the time, Pallas kernels for 0%

profile of v1, /device:TPU:1, one launch (start us, length us, event | category | flops | bytes accessed | tf_op | source)
XLA Modules:
  0.0 189.5 jit_solution(4943944811190114836)
XLA Ops:
  0.6 0.0 copy-start.3
  0.6 0.0 copy-start.6
  0.7 0.0 copy-start.5
  0.7 0.0 copy-start.4
  0.7 2.0 %copy.45 = bf16[2,16,8,1024]{3,2,0,1:T(8,128)(2,1)} copy(bf16[2,16,8,1024]{3,2,1,0:T(8,128)(2,1)} %bitcast.54) | data formatting | bytes 1048576 | tf_op jit(solution)/shard_map/all_to_all | solution.py:46
  2.6 7.3 %all-to-all-start.3 = ((bf16[16,16,1024]{2,0,1:T(8,128)(2,1)}), bf16[16,16,1024]{2,0,1:T(8,128)(2,1)S(1)}, u32[]{:S(2)}, u32[]{:S(2)}) async-start(bf16[16,16,1024]{2,0,1:T(8,128)(2,1)} %bitcast.42), calls=%async_computation.3 | async-start | bytes 1048576 | tf_op jit(solution)/shard_map/all_to_all | solution.py:46
  10.0 0.0 copy-done.3
  10.0 0.0 copy-done.6
  10.0 0.0 copy-done.5
  10.0 0.0 copy-done.4
  10.0 1.0 fusion.3
  11.0 8.5 %all-to-all-done.3 = bf16[16,16,1024]{2,0,1:T(8,128)(2,1)S(1)} async-done(((bf16[16,16,1024]{2,0,1:T(8,128)(2,1)}), bf16[16,16,1024]{2,0,1:T(8,128)(2,1)S(1)}, u32[]{:S(2)}, u32[]{:S(2)}) %all-to-all-start.3) | async-done | bytes 524320 | tf_op jit(solution)/shard_map/all_to_all | solution.py:46
  19.5 1.1 broadcast_in_dim.4
  20.5 7.0 %all-to-all-start.4 = ((bf16[8,128,512]{2,1,0:T(8,128)(2,1)}), bf16[8,128,512]{2,1,0:T(8,128)(2,1)S(1)}, u32[]{:S(2)}, u32[]{:S(2)}) async-start(bf16[8,128,512]{2,1,0:T(8,128)(2,1)} %broadcast_in_dim.4), calls=%async_computation.4 | async-start | bytes 2097152 | tf_op jit(solution)/shard_map/all_to_all | solution.py:25
  27.6 3.1 %copy.42 = f32[16,8,8,512]{3,2,0,1:T(8,128)} copy(f32[16,8,8,512]{3,2,1,0:T(8,128)} %bitcast.50) | data formatting | bytes 4194304 | tf_op jit(solution)/shard_map/all_to_all | solution.py:54
  30.7 12.1 %all-to-all-done.4 = bf16[8,128,512]{2,1,0:T(8,128)(2,1)S(1)} async-done(((bf16[8,128,512]{2,1,0:T(8,128)(2,1)}), bf16[8,128,512]{2,1,0:T(8,128)(2,1)S(1)}, u32[]{:S(2)}, u32[]{:S(2)}) %all-to-all-start.4) | async-done | bytes 1048608 | tf_op jit(solution)/shard_map/all_to_all | solution.py:25
  42.8 0.0 copy-start.1
  42.9 1.0 copy-done.1
  43.8 4.2 %all-to-all-start.2 = ((f32[128,8,512]{2,0,1:T(8,128)}), f32[128,8,512]{2,0,1:T(8,128)S(1)}, u32[]{:S(2)}, u32[]{:S(2)}) async-start(f32[128,8,512]{2,0,1:T(8,128)} %bitcast.44), calls=%async_computation.2 | async-start | bytes 4194304 | tf_op jit(solution)/shard_map/all_to_all | solution.py:54
  48.0 3.1 %copy.43 = f32[16,8,8,512]{3,2,0,1:T(8,128)} copy(f32[16,8,8,512]{3,2,1,0:T(8,128)} %bitcast.51) | data formatting | bytes 4194304 | tf_op jit(solution)/shard_map/all_to_all | solution.py:53
  51.2 26.8 %all-to-all-done.2 = f32[128,8,512]{2,0,1:T(8,128)S(1)} async-done(((f32[128,8,512]{2,0,1:T(8,128)}), f32[128,8,512]{2,0,1:T(8,128)S(1)}, u32[]{:S(2)}, u32[]{:S(2)}) %all-to-all-start.2) | async-done | bytes 2097184 | tf_op jit(solution)/shard_map/all_to_all | solution.py:54
  78.0 4.4 %all-to-all-start.1 = ((f32[128,8,512]{2,0,1:T(8,128)}), f32[128,8,512]{2,0,1:T(8,128)}, u32[]{:S(2)}, u32[]{:S(2)}) async-start(f32[128,8,512]{2,0,1:T(8,128)} %bitcast.45), calls=%async_computation.1 | async-start | bytes 4194304 | tf_op jit(solution)/shard_map/all_to_all | solution.py:53
  82.4 3.2 %copy.44 = f32[16,8,8,512]{3,2,0,1:T(8,128)} copy(f32[16,8,8,512]{3,2,1,0:T(8,128)} %bitcast.52) | data formatting | bytes 4194304 | tf_op jit(solution)/shard_map/all_to_all | solution.py:52
  85.6 26.4 %all-to-all-done.1 = f32[128,8,512]{2,0,1:T(8,128)} async-done(((f32[128,8,512]{2,0,1:T(8,128)}), f32[128,8,512]{2,0,1:T(8,128)}, u32[]{:S(2)}, u32[]{:S(2)}) %all-to-all-start.1) | async-done | bytes 2097184 | tf_op jit(solution)/shard_map/all_to_all | solution.py:53
  111.9 4.3 %all-to-all-start = ((f32[128,8,512]{2,0,1:T(8,128)}), f32[128,8,512]{2,0,1:T(8,128)}, u32[]{:S(2)}, u32[]{:S(2)}) async-start(f32[128,8,512]{2,0,1:T(8,128)} %bitcast.43), calls=%async_computation | async-start | bytes 4194304 | tf_op jit(solution)/shard_map/all_to_all | solution.py:52
  116.3 2.6 %convolution_bitcast_fusion = f32[256,512]{0,1:T(8,128)} fusion(bf16[1024,512]{1,0:T(8,128)(2,1)} %bitcast.48, bf16[256,1024]{1,0:T(8,128)(2,1)S(1)} %bitcast.46), kind=kOutput, calls=%fused_computation.7 | convolution fusion | flops 268435456 | bytes 2097152 | tf_op jit(solution)/shard_map/dot_general | solution.py:49
  118.8 1.7 broadcast_multiply_fusion
  120.5 3.3 %broadcast_multiply_fusion.1 = f32[128,8,512]{2,0,1:T(8,128)} fusion(f32[128,8,512]{2,0,1:T(8,128)} %all-to-all-done.1), kind=kLoop, calls=%fused_computation.12 | loop fusion | flops 524288 | bytes 4194304 | tf_op jit(solution)/shard_map/mul | solution.py:17
  123.8 21.8 %all-to-all-done = f32[128,8,512]{2,0,1:T(8,128)} async-done(((f32[128,8,512]{2,0,1:T(8,128)}), f32[128,8,512]{2,0,1:T(8,128)}, u32[]{:S(2)}, u32[]{:S(2)}) %all-to-all-start) | async-done | bytes 2097184 | tf_op jit(solution)/shard_map/all_to_all | solution.py:52
  145.6 6.7 %bitcast_subtract_fusion = (f32[1024,512]{1,0:T(8,128)S(1)}, f32[1024,512]{1,0:T(8,128)}, f32[1024,512]{1,0:T(8,128)}) fusion(f32[128,8,512]{2,0,1:T(8,128)} %all-to-all-done, f32[1024,512]{1,0:T(8,128)} %param.13, f32[128,8,512]{2,0,1:T(8,128)} %broadcast_multiply_fusion, f32[128,8,512]{2,0,1:T(8,128)} %broadcast_multiply_fusion.1), kind=kLoop, calls=%fused_computation.6 | loop fusion | flops 4718592 | bytes 14680064 | tf_op jit(solution)/shard_map/sub | solution.py:20
  152.3 0.0 copy-start
  152.3 0.0 copy-start.2
  152.3 0.5 convolution_bitcast_fusion.1
  152.8 0.9 copy-done.2
  153.7 0.1 pad_maximum_fusion
  153.8 0.0 copy-done
  153.8 1.3 copy.33
  155.1 21.8 %all_to_all.91 = f32[16,16,1024]{2,1,0:T(8,128)S(1)} all-to-all(f32[16,16,1024]{2,1,0:T(8,128)} %bitcast.49), channel_id=1, replica_groups=mesh['fsdp'=16,'tp'=8] {'fsdp'}, dimensions={0} | all-to-all | bytes 2097152 | tf_op jit(solution)/shard_map/all_to_all | solution.py:29
  176.9 0.1 reduce_sum.9
  177.0 0.6 fusion.6
  177.6 11.1 %all_to_all.92 = bf16[16,16,512]{2,1,0:T(8,128)(2,1)S(1)} all-to-all(bf16[16,16,512]{2,1,0:T(8,128)(2,1)S(1)} %broadcast_in_dim.5), channel_id=1, replica_groups=mesh['fsdp'=16,'tp'=8] {'fsdp'}, dimensions={0} | all-to-all | bytes 524288 | tf_op jit(solution)/shard_map/all_to_all | solution.py:25
  188.8 0.7 copy.47
  (1 shorter events, 0.0 us)
Async XLA Ops:
  0.6 9.3 %copy-start.3 = (f32[128,512]{1,0:T(8,128)S(1)}, f32[128,512]{1,0:T(8,128)}, u32[]{:S(2)}) copy-start(f32[128,512]{1,0:T(8,128)} %param.14) | copy-start | bytes 786436
  0.6 9.3 %copy-start.6 = (f32[128,512]{1,0:T(8,128)S(1)}, f32[128,512]{1,0:T(8,128)}, u32[]{:S(2)}) copy-start(f32[128,512]{1,0:T(8,128)} %param.15) | copy-start | bytes 786436
  0.7 9.3 %copy-start.5 = (f32[128,512]{1,0:T(8,128)S(1)}, f32[128,512]{1,0:T(8,128)}, u32[]{:S(2)}) copy-start(f32[128,512]{1,0:T(8,128)} %param.16) | copy-start | bytes 786436
  0.7 9.3 %copy-start.4 = (f32[128,512]{1,0:T(8,128)S(1)}, f32[128,512]{1,0:T(8,128)}, u32[]{:S(2)}) copy-start(f32[128,512]{1,0:T(8,128)} %param.17) | copy-start | bytes 786436
  2.6 16.8 %all-to-all-start.3 = ((bf16[16,16,1024]{2,0,1:T(8,128)(2,1)}), bf16[16,16,1024]{2,0,1:T(8,128)(2,1)S(1)}, u32[]{:S(2)}, u32[]{:S(2)}) async-start(bf16[16,16,1024]{2,0,1:T(8,128)(2,1)} %bitcast.42), calls=%async_computation.3 | async-start | bytes 1048576 | tf_op jit(solution)/shard_map/all_to_all | solution.py:46
  20.5 22.3 %all-to-all-start.4 = ((bf16[8,128,512]{2,1,0:T(8,128)(2,1)}), bf16[8,128,512]{2,1,0:T(8,128)(2,1)S(1)}, u32[]{:S(2)}, u32[]{:S(2)}) async-start(bf16[8,128,512]{2,1,0:T(8,128)(2,1)} %broadcast_in_dim.4), calls=%async_computation.4 | async-start | bytes 2097152 | tf_op jit(solution)/shard_map/all_to_all | solution.py:25
  42.8 1.0 copy-start.1
  43.8 34.2 %all-to-all-start.2 = ((f32[128,8,512]{2,0,1:T(8,128)}), f32[128,8,512]{2,0,1:T(8,128)S(1)}, u32[]{:S(2)}, u32[]{:S(2)}) async-start(f32[128,8,512]{2,0,1:T(8,128)} %bitcast.44), calls=%async_computation.2 | async-start | bytes 4194304 | tf_op jit(solution)/shard_map/all_to_all | solution.py:54
  78.0 33.9 %all-to-all-start.1 = ((f32[128,8,512]{2,0,1:T(8,128)}), f32[128,8,512]{2,0,1:T(8,128)}, u32[]{:S(2)}, u32[]{:S(2)}) async-start(f32[128,8,512]{2,0,1:T(8,128)} %bitcast.45), calls=%async_computation.1 | async-start | bytes 4194304 | tf_op jit(solution)/shard_map/all_to_all | solution.py:53
  111.9 33.7 %all-to-all-start = ((f32[128,8,512]{2,0,1:T(8,128)}), f32[128,8,512]{2,0,1:T(8,128)}, u32[]{:S(2)}, u32[]{:S(2)}) async-start(f32[128,8,512]{2,0,1:T(8,128)} %bitcast.43), calls=%async_computation | async-start | bytes 4194304 | tf_op jit(solution)/shard_map/all_to_all | solution.py:52
  152.3 1.5 copy-start
  152.3 1.4 copy-start.2

commit v2 on v1

--- a/solution.py
+++ b/solution.py
@@ -42,17 +42,16 @@
     wkv_grad,
 ):
     fsdp = lax.axis_size("fsdp")
-    tp = lax.axis_size("tp")
     columns = lax.all_to_all(probe_states, "fsdp", split_axis=1, concat_axis=0, tiled=True)
     wkv_new, wkv_mom, wkv_var = adam_step(wkv_master, wkv_first, wkv_second, wkv_grad)
-    wkv_rows = gather_rows(wkv_new.astype(jnp.bfloat16), "tp", tp)
+    wkv_rows = lax.all_gather(wkv_new.astype(jnp.bfloat16), "tp", axis=0, tiled=True)
     kv_term = jnp.dot(columns, wkv_rows, preferred_element_type=jnp.float32)
 
-    master, first, second = (
-        lax.all_to_all(wq_master, "tp", split_axis=1, concat_axis=0, tiled=True),
-        lax.all_to_all(wq_first, "tp", split_axis=1, concat_axis=0, tiled=True),
-        lax.all_to_all(wq_second, "tp", split_axis=1, concat_axis=0, tiled=True),
-    )
+    tp = lax.axis_size("tp")
+    rows, cols = wq_master.shape
+    pieces = [x.reshape(rows, tp, cols // tp).transpose(1, 0, 2) for x in (wq_master, wq_first, wq_second)]
+    state = lax.all_to_all(jnp.concatenate(pieces, axis=1), "tp", split_axis=0, concat_axis=0, tiled=True)
+    master, first, second = (state[:, k * rows:(k + 1) * rows].reshape(tp * rows, cols // tp) for k in range(3))
     wq_new, wq_mom, wq_var = adam_step(master, first, second, wq_grad)
     q_term = jnp.dot(columns, wq_new.astype(jnp.bfloat16), preferred_element_type=jnp.float32)
 

time: 190 us -> 178 us (0.937)
  between operations: 0.75 us -> 14.2 us
  starting transfers between devices: 27.3 us -> 14.4 us
  local copies, waits for them, and re-layouts: 17 us -> 8.42 us
  waiting for transfers between devices: 95.6 us -> 92.2 us
    all_gather x0 -> x1, waiting for transfers between devices: none -> 88.8 us  [body(): lax.all_gather(wkv_new.astype(jnp.bfloat16), 'tp', axis=0, tiled=True)]
    all_to_all x4 -> x1, waiting for transfers between devices: 87.2 us -> 0.01 us  [body(): lax.all_to_all(jnp.concatenate(pieces, axis=1), 'tp', split_axis=0, conca...]
    all_to_all x4 -> x1, starting transfers between devices: 20 us -> 7.04 us  [body(): lax.all_to_all(jnp.concatenate(pieces, axis=1), 'tp', split_axis=0, conca...]
    all_to_all x3 -> x0, local copies, waits for them, and re-layouts: 9.45 us -> none  [the longest x1 3.15 us: body(): lax.all_to_all(wq_master, 'tp', split_axis=1, concat_axis=0, tiled=True)]
    all_to_all x1, waiting for transfers between devices: 8.49 us -> 3.3 us  [body(): lax.all_to_all(probe_states, 'fsdp', split_axis=1, concat_axis=0, tiled=T...]
    sub x1, other arithmetic: 6.74 us -> 3.26 us  [adam_step(): return (master - LEARN_RATE * update, first_new, second_new)]
    concatenate x0 -> x1, other arithmetic: none -> 3.33 us  [body(): jnp.concatenate(pieces, axis=1)]
  transfers between devices with their start and end apart: 5 -> 3, of which waited for: 5 -> 2; matrix products, arithmetic and copies ran while one was open for 9% -> 4% of each run, Pallas kernels for 0% -> 0%
where the time goes in v2:
time: 178 us; the launch traced here: 177 us
  waiting for transfers between devices  92.2 us (52%)
  blocking collectives  33.1 us (19%)
  starting transfers between devices  14.4 us (8%)
  between operations  14.2 us (8%)
  other arithmetic  12 us (7%)
  local copies, waits for them, and re-layouts  8.42 us (5%)
  matrix products  3.01 us (2%)
    all_gather x1, waiting for transfers between devices, body(): lax.all_gather(wkv_new.astype(jnp.bfloat16), 'tp', axis=0, tiled=True)  88.8 us
    all_to_all x1, blocking collectives, scatter_sum_rows(): lax.all_to_all(x, axis_name, split_axis=0, concat_axis=0, tiled=True)  22 us
    all_to_all x1, blocking collectives, gather_rows(): lax.all_to_all(copies, axis_name, split_axis=0, concat_axis=0, tiled=True)  11.1 us
    all_to_all x1, starting transfers between devices, body(): lax.all_to_all(probe_states, 'fsdp', split_axis=1, concat_axis=0, tiled=T...  7.33 us
    all_to_all x1, starting transfers between devices, body(): lax.all_to_all(jnp.concatenate(pieces, axis=1), 'tp', split_axis=0, conca...  7.04 us
    mul x1, other arithmetic, adam_step(): first_new = BETA_ONE * first + (1.0 - BETA_ONE) * grad  4.27 us
    unnamed x21, local copies, waits for them, and re-layouts  3.66 us
  transfers between devices with their start and end apart: 3, of which 2 were waited for; matrix products, arithmetic and copies ran while one was open for 4% of the time, Pallas kernels for 0%

profile of v2, /device:TPU:1, one launch (start us, length us, event | category | flops | bytes accessed | tf_op | source)
XLA Modules:
  0.0 177.2 jit_solution(8441982506671339834)
XLA Ops:
  7.2 0.0 copy-start.2
  7.2 2.0 %copy.43 = bf16[2,16,8,1024]{3,2,0,1:T(8,128)(2,1)} copy(bf16[2,16,8,1024]{3,2,1,0:T(8,128)(2,1)} %bitcast.49) | data formatting | bytes 1048576 | tf_op jit(solution)/shard_map/all_to_all | solution.py:45
  9.2 7.3 %all-to-all-start.1 = ((bf16[16,16,1024]{2,0,1:T(8,128)(2,1)}), bf16[16,16,1024]{2,0,1:T(8,128)(2,1)S(1)}, u32[]{:S(2)}, u32[]{:S(2)}) async-start(bf16[16,16,1024]{2,0,1:T(8,128)(2,1)} %bitcast.40), calls=%async_computation.1 | async-start | bytes 1048576 | tf_op jit(solution)/shard_map/all_to_all | solution.py:45
  16.5 0.0 copy-done.2
  16.5 0.0 copy-start.3
  16.6 0.0 copy-start.4
  16.6 0.2 copy.42
  16.7 1.4 copy-done.3
  18.1 0.6 copy-done.4
  18.8 0.6 bitcast_bitcast_fusion
  19.4 3.3 %pad_maximum_fusion = f32[8,384,512]{2,1,0:T(8,128)} fusion(f32[8,128,512]{2,1,0:T(8,128)S(1)} %get-tuple-element.20, f32[8,128,512]{2,1,0:T(8,128)S(1)} %get-tuple-element.21, f32[8,128,512]{2,1,0:T(8,128)S(1)} %bitcast.41), kind=kLoop, calls=%fused_computation | loop fusion | flops 3145728 | bytes 12582912 | tf_op jit(solution)/shard_map/concatenate | solution.py:53
  22.7 0.0 copy-start.6
  22.7 0.0 copy-start.7
  22.7 0.0 copy-start.8
  22.7 0.0 copy-start.9
  22.7 3.3 %all-to-all-done.1 = bf16[16,16,1024]{2,0,1:T(8,128)(2,1)S(1)} async-done(((bf16[16,16,1024]{2,0,1:T(8,128)(2,1)}), bf16[16,16,1024]{2,0,1:T(8,128)(2,1)S(1)}, u32[]{:S(2)}, u32[]{:S(2)}) %all-to-all-start.1) | async-done | bytes 524320 | tf_op jit(solution)/shard_map/all_to_all | solution.py:45
  26.0 7.0 %all-to-all-start = ((f32[8,384,512]{2,1,0:T(8,128)}), f32[8,384,512]{2,1,0:T(8,128)}, u32[]{:S(2)}, u32[]{:S(2)}) async-start(f32[8,384,512]{2,1,0:T(8,128)} %pad_maximum_fusion), calls=%async_computation | async-start | bytes 12582912 | tf_op jit(solution)/shard_map/all_to_all | solution.py:53
  33.1 0.0 all-gather.2.cloned.1.call-start
  33.1 0.0 copy-done.6
  33.1 0.0 copy-done.7
  33.1 0.0 copy-done.8
  33.1 0.0 copy-done.9
  33.1 1.0 fusion.3
  34.2 0.0 all-gather.2.cloned.1.call-update
  34.2 88.8 %all-gather.2.cloned.1.call-done = bf16[1024,512]{1,0:T(8,128)(2,1)} async-done(((bf16[128,512]{1,0:T(8,128)(2,1)}), bf16[1024,512]{1,0:T(8,128)(2,1)}) %all-gather.2.cloned.1.call-update) | async-done | bytes 1048592 | tf_op jit(solution)/shard_map/all_gather | solution.py:47
  123.0 2.5 %convolution_bitcast_fusion = f32[256,512]{0,1:T(8,128)} fusion(bf16[1024,512]{1,0:T(8,128)(2,1)} %all-gather.2.cloned.1.call-done, bf16[256,1024]{1,0:T(8,128)(2,1)S(1)} %bitcast.42), kind=kOutput, calls=%fused_computation.10 | convolution fusion | flops 268435456 | bytes 2097152 | tf_op jit(solution)/shard_map/dot_general | solution.py:48
  125.6 0.0 all-to-all-done
  125.6 0.0 copy-start.1
  125.6 4.3 %slice_multiply_fusion.1 = (f32[8,128,512]{2,1,0:T(8,128)S(1)}, f32[8,128,512]{2,1,0:T(8,128)S(1)}, f32[8,128,512]{2,1,0:T(8,128)S(1)}) fusion(f32[8,384,512]{2,1,0:T(8,128)} %all-to-all-done), kind=kLoop, calls=%fused_computation.7 | loop fusion | flops 1048576 | bytes 12582912 | tf_op jit(solution)/shard_map/mul | solution.py:17
  129.8 0.0 copy-done.1
  129.8 3.3 %bitcast_subtract_fusion = (f32[1024,512]{1,0:T(8,128)S(1)}, f32[1024,512]{1,0:T(8,128)}, f32[1024,512]{1,0:T(8,128)}) fusion(f32[8,128,512]{2,1,0:T(8,128)S(1)} %get-tuple-element.17, f32[1024,512]{1,0:T(8,128)S(1)} %copy-done.1, f32[8,128,512]{2,1,0:T(8,128)S(1)} %get-tuple-element.16, f32[8,128,512]{2,1,0:T(8,128)S(1)} %get-tuple-element.15), kind=kLoop, calls=%fused_computation.9 | loop fusion | flops 4718592 | bytes 14680064 | tf_op jit(solution)/shard_map/sub | solution.py:20
  133.1 0.0 copy-start
  133.1 0.0 copy-start.5
  133.1 0.5 convolution_bitcast_fusion.1
  133.6 0.9 copy-done.5
  134.5 0.1 pad_maximum_fusion.1
  134.6 0.0 copy-done
  134.6 1.3 copy.33
  135.9 22.0 %all_to_all.42 = f32[16,16,1024]{2,1,0:T(8,128)S(1)} all-to-all(f32[16,16,1024]{2,1,0:T(8,128)} %bitcast.44), channel_id=1, replica_groups=mesh['fsdp'=16,'tp'=8] {'fsdp'}, dimensions={0} | all-to-all | bytes 2097152 | tf_op jit(solution)/shard_map/all_to_all | solution.py:29
  157.9 0.1 reduce_sum.9
  157.9 0.6 fusion.6
  158.6 11.1 %all_to_all.43 = bf16[16,16,512]{2,1,0:T(8,128)(2,1)S(1)} all-to-all(bf16[16,16,512]{2,1,0:T(8,128)(2,1)S(1)} %broadcast_in_dim.2), channel_id=1, replica_groups=mesh['fsdp'=16,'tp'=8] {'fsdp'}, dimensions={0} | all-to-all | bytes 524288 | tf_op jit(solution)/shard_map/all_to_all | solution.py:25
  169.7 0.7 copy.45
  (1 shorter events, 0.0 us)
Async XLA Ops:
  7.2 9.4 %copy-start.2 = (f32[128,4096]{1,0:T(8,128)S(1)}, f32[128,4096]{1,0:T(8,128)}, u32[]{:S(2)}) copy-start(f32[128,4096]{1,0:T(8,128)} %param.10) | copy-start | bytes 6291460
  9.2 16.8 %all-to-all-start.1 = ((bf16[16,16,1024]{2,0,1:T(8,128)(2,1)}), bf16[16,16,1024]{2,0,1:T(8,128)(2,1)S(1)}, u32[]{:S(2)}, u32[]{:S(2)}) async-start(bf16[16,16,1024]{2,0,1:T(8,128)(2,1)} %bitcast.40), calls=%async_computation.1 | async-start | bytes 1048576 | tf_op jit(solution)/shard_map/all_to_all | solution.py:45
  16.5 1.6 copy-start.3
  16.6 2.2 %copy-start.4 = (f32[128,4096]{1,0:T(8,128)S(1)}, f32[128,4096]{1,0:T(8,128)}, u32[]{:S(2)}) copy-start(f32[128,4096]{1,0:T(8,128)} %param.11) | copy-start | bytes 6291460
  22.7 10.4 %copy-start.6 = (f32[128,512]{1,0:T(8,128)S(1)}, f32[128,512]{1,0:T(8,128)}, u32[]{:S(2)}) copy-start(f32[128,512]{1,0:T(8,128)} %param.14) | copy-start | bytes 786436
  22.7 10.4 %copy-start.7 = (f32[128,512]{1,0:T(8,128)S(1)}, f32[128,512]{1,0:T(8,128)}, u32[]{:S(2)}) copy-start(f32[128,512]{1,0:T(8,128)} %param.17) | copy-start | bytes 786436
  22.7 10.4 %copy-start.8 = (f32[128,512]{1,0:T(8,128)S(1)}, f32[128,512]{1,0:T(8,128)}, u32[]{:S(2)}) copy-start(f32[128,512]{1,0:T(8,128)} %param.16) | copy-start | bytes 786436
  22.7 10.4 %copy-start.9 = (f32[128,512]{1,0:T(8,128)S(1)}, f32[128,512]{1,0:T(8,128)}, u32[]{:S(2)}) copy-start(f32[128,512]{1,0:T(8,128)} %param.15) | copy-start | bytes 786436
  26.0 99.5 %all-to-all-start = ((f32[8,384,512]{2,1,0:T(8,128)}), f32[8,384,512]{2,1,0:T(8,128)}, u32[]{:S(2)}, u32[]{:S(2)}) async-start(f32[8,384,512]{2,1,0:T(8,128)} %pad_maximum_fusion), calls=%async_computation | async-start | bytes 12582912 | tf_op jit(solution)/shard_map/all_to_all | solution.py:53
  33.1 90.0 %all-gather.2.cloned.1.call-start = ((), (), s32[]{:S(2)}) async-start(), calls=%async_computation.4 | async-start | bytes 1179648 | tf_op jit(solution)/shard_map/all_gather | solution.py:47
  125.6 4.3 %copy-start.1 = (f32[1024,512]{1,0:T(8,128)S(1)}, f32[1024,512]{1,0:T(8,128)}, u32[]{:S(2)}) copy-start(f32[1024,512]{1,0:T(8,128)} %param.13) | copy-start | bytes 6291460
  133.1 1.5 copy-start
  133.1 1.4 copy-start.5
Sparse Core Ops, SparseCore 0:
  36.8 86.2 all-gather.1

commit v3 on v2

--- a/solution.py
+++ b/solution.py
@@ -4,6 +4,7 @@
 import jax.numpy as jnp
 from jax import lax
 from jax.sharding import PartitionSpec as P
+
 
 BETA_ONE = 0.9
 BETA_TWO = 0.95
@@ -30,7 +31,7 @@
     return parts.reshape((size, x.shape[0] // size) + x.shape[1:]).sum(axis=0)
 
 
-def body(
+def step(
     probe_states,
     wq_master,
     wq_first,
@@ -50,7 +51,14 @@
     tp = lax.axis_size("tp")
     rows, cols = wq_master.shape
     pieces = [x.reshape(rows, tp, cols // tp).transpose(1, 0, 2) for x in (wq_master, wq_first, wq_second)]
-    state = lax.all_to_all(jnp.concatenate(pieces, axis=1), "tp", split_axis=0, concat_axis=0, tiled=True)
+    send = jnp.concatenate(pieces, axis=1)
+    me = lax.axis_index("tp")
+    got = [send[me]]
+    for k in range(1, tp):
+        block = lax.dynamic_index_in_dim(send, (me + k) % tp, 0, keepdims=False)
+        got.append(lax.ppermute(block, "tp", [(i, (i + k) % tp) for i in range(tp)]))
+    got = jnp.stack(got[::-1])
+    state = lax.dynamic_slice_in_dim(jnp.concatenate([got, got]), tp - 1 - me, tp, 0)
     master, first, second = (state[:, k * rows:(k + 1) * rows].reshape(tp * rows, cols // tp) for k in range(3))
     wq_new, wq_mom, wq_var = adam_step(master, first, second, wq_grad)
     q_term = jnp.dot(columns, wq_new.astype(jnp.bfloat16), preferred_element_type=jnp.float32)
@@ -64,7 +72,7 @@
 
 def solution(mesh):
     return jax.shard_map(
-        body,
+        step,
         mesh=mesh,
         in_specs=(
             P("fsdp", None),

time: 178 us -> 197 us (1.11)
  the two profiles are of different devices: /device:TPU:1 before, /device:TPU:2 now
where the time goes in v3:
time: 197 us
  waiting for transfers between devices  100 us (51%)
  blocking collectives  32.2 us (16%)
  local copies, waits for them, and re-layouts  21.2 us (11%)
  starting transfers between devices  16.9 us (9%)
  between operations  14.4 us (7%)
  other arithmetic  8.57 us (4%)
  matrix products  3.19 us (2%)
    ppermute x7, waiting for transfers between devices, step(): lax.ppermute(block, 'tp', [(i, (i + k) % tp) for i in range(tp)])  100 us
    all_to_all x1, blocking collectives, scatter_sum_rows(): lax.all_to_all(x, axis_name, split_axis=0, concat_axis=0, tiled=True)  21.8 us
    ppermute x7, starting transfers between devices, step(): lax.ppermute(block, 'tp', [(i, (i + k) % tp) for i in range(tp)])  11.8 us
    all_to_all x1, blocking collectives, gather_rows(): lax.all_to_all(copies, axis_name, split_axis=0, concat_axis=0, tiled=True)  10.4 us
    unnamed x24, local copies, waits for them, and re-layouts  10.2 us
    all_to_all x1, starting transfers between devices, step(): lax.all_to_all(probe_states, 'fsdp', split_axis=1, concat_axis=0, tiled=T...  5.03 us
  transfers between devices with their start and end apart: 9, of which 4 were waited for; matrix products, arithmetic and copies ran while one was open for 8% of the time, Pallas kernels for 0%

profile of v3, /device:TPU:2, one launch (start us, length us, event | category | flops | bytes accessed | tf_op | source)
XLA Modules:
  0.0 196.5 jit_solution(15100824501590401734)
XLA Ops:
  7.3 1.8 copy.42
  9.1 2.7 %bitcast_bitcast_fusion = (f32[8,128,512]{2,1,0:T(8,128)S(1)}, f32[8,128,512]{2,1,0:T(8,128)S(1)}) fusion(f32[16,8,8,512]{3,2,1,0:T(8,128)} %bitcast.81, f32[16,8,8,512]{3,2,1,0:T(8,128)} %bitcast.82), kind=kLoop, calls=%fused_computation.3 | loop fusion | bytes 8388608 | tf_op jit(solution)/shard_map/transpose | solution.py:53
  11.8 0.7 pad_maximum_fusion
  12.5 2.7 %copy-done = f32[8,384,512]{2,1,0:T(8,128)} copy-done((f32[8,384,512]{2,1,0:T(8,128)}, f32[8,384,512]{2,1,0:T(8,128)S(1)}, u32[]{:S(2)}) %copy-start) | copy-done | bytes 6291480
  15.2 2.5 %dynamic-slice_bitcast_fusion = (f32[384,512]{1,0:T(8,128)}, f32[384,512]{1,0:T(8,128)}, f32[384,512]{1,0:T(8,128)}, f32[384,512]{1,0:T(8,128)}, f32[384,512]{1,...) fusion(f32[8,384,512]{2,1,0:T(8,128)S(1)} %pad_maximum_fusion, s32[]{:T(128)S(6)} %select_n.72, s32[]{:T(128)S(6)} %select_n.70, ...), kind=kLoop, calls=%fused_computation.28 | loop fusion | bytes 11010076 | tf_op jit(solution)/shard_map/jit(dynamic_index_in_dim)/squeeze | solution.py:58
  17.7 3.8 %collective-permute-start = (f32[384,512]{1,0:T(8,128)}, f32[384,512]{1,0:T(8,128)S(1)}, u32[]{:S(2)}, u32[]{:S(2)}) collective-permute-start(f32[384,512]{1,0:T(8,128)} %get-tuple-element.24), channel_id=1, source_target_pairs={{0,7},{1,0},{2,1},{3,2},{4,3},{5,4},{6,5},{7,6},{8,15},{9,8},{10,9... | collective-permute-start | bytes 2359304 | tf_op jit(solution)/shard_map/ppermute | solution.py:59
  21.5 2.8 %collective-permute-start.1 = (f32[384,512]{1,0:T(8,128)}, f32[384,512]{1,0:T(8,128)S(1)}, u32[]{:S(2)}, u32[]{:S(2)}) collective-permute-start(f32[384,512]{1,0:T(8,128)} %get-tuple-element.23), channel_id=1, source_target_pairs={{0,6},{1,7},{2,0},{3,1},{4,2},{5,3},{6,4},{7,5},{8,14},{9,15},{10,... | collective-permute-start | bytes 2359304 | tf_op jit(solution)/shard_map/ppermute | solution.py:59
  24.3 0.0 collective-permute-start.2
  24.3 0.8 collective-permute-start.3
  25.1 4.5 %collective-permute-start.4 = (f32[384,512]{1,0:T(8,128)}, f32[384,512]{1,0:T(8,128)}, u32[]{:S(2)}, u32[]{:S(2)}) collective-permute-start(f32[384,512]{1,0:T(8,128)} %get-tuple-element.20), channel_id=1, source_target_pairs={{0,3},{1,4},{2,5},{3,6},{4,7},{5,0},{6,1},{7,2},{8,11},{9,12},{10,... | collective-permute-start | bytes 2359304 | tf_op jit(solution)/shard_map/ppermute | solution.py:59
  29.5 0.8 copy.43
  30.4 5.0 %all-to-all-start = ((bf16[16,16,1024]{2,0,1:T(8,128)(2,1)}), bf16[16,16,1024]{2,0,1:T(8,128)(2,1)S(1)}, u32[]{:S(2)}, u32[]{:S(2)}) async-start(bf16[16,16,1024]{2,0,1:T(8,128)(2,1)} %bitcast.75), calls=%async_computation | async-start | bytes 1048576 | tf_op jit(solution)/shard_map/all_to_all | solution.py:46
  35.4 0.0 all-gather.2.cloned.1.call-start
  35.5 2.2 %fusion.3 = (bf16[128,512]{1,0:T(8,128)(2,1)}, f32[128,512]{1,0:T(8,128)}, f32[128,512]{1,0:T(8,128)}, f32[128,512]{1,0:T(8,128)}) fusion(f32[128,512]{1,0:T(8,128)} %param.14, f32[128,512]{1,0:T(8,128)} %param.17, f32[128,512]{1,0:T(8,128)} %param.16, f32[128,512]{1,0:T(8,128)} %param.15), kind=kLoop, calls=%fused_computation.43 | loop fusion | flops 786432 | bytes 1966080 | tf_op jit(solution)/shard_map/convert_element_type | solution.py:48
  37.7 0.0 all-gather.2.cloned.1.call-update
  37.7 23.6 %collective-permute-done = f32[384,512]{1,0:T(8,128)S(1)} collective-permute-done((f32[384,512]{1,0:T(8,128)}, f32[384,512]{1,0:T(8,128)S(1)}, u32[]{:S(2)}, u32[]{:S(2)}) %collective-permute-start) | collective-permute-done | bytes 786464 | tf_op jit(solution)/shard_map/ppermute | solution.py:59
  61.2 0.1 bitcast_dynamic-update-slice_fusion.12
  61.3 17.3 %collective-permute-done.1 = f32[384,512]{1,0:T(8,128)S(1)} collective-permute-done((f32[384,512]{1,0:T(8,128)}, f32[384,512]{1,0:T(8,128)S(1)}, u32[]{:S(2)}, u32[]{:S(2)}) %collective-permute-start.1) | collective-permute-done | bytes 786464 | tf_op jit(solution)/shard_map/ppermute | solution.py:59
  78.6 0.1 bitcast_dynamic-update-slice_fusion.10
  78.7 25.8 %collective-permute-done.2 = f32[384,512]{1,0:T(8,128)S(1)} collective-permute-done((f32[384,512]{1,0:T(8,128)}, f32[384,512]{1,0:T(8,128)S(1)}, u32[]{:S(2)}, u32[]{:S(2)}) %collective-permute-start.2) | collective-permute-done | bytes 786464 | tf_op jit(solution)/shard_map/ppermute | solution.py:59
  104.5 0.1 bitcast_dynamic-update-slice_fusion.8
  104.6 33.4 %collective-permute-done.3 = f32[384,512]{1,0:T(8,128)} collective-permute-done((f32[384,512]{1,0:T(8,128)}, f32[384,512]{1,0:T(8,128)}, u32[]{:S(2)}, u32[]{:S(2)}) %collective-permute-start.3) | collective-permute-done | bytes 786464 | tf_op jit(solution)/shard_map/ppermute | solution.py:59
  137.9 1.2 bitcast_dynamic-update-slice_fusion.6
  139.1 1.2 bitcast_dynamic-update-slice_fusion.4
  140.3 0.1 bitcast_dynamic-update-slice_fusion.2
  140.4 0.1 bitcast_dynamic-update-slice_fusion
  140.5 1.2 dynamic-slice_dynamic-update-slice_fusion
  141.7 0.1 bitcast_dynamic-update-slice_fusion.13
  141.7 0.1 bitcast_dynamic-update-slice_fusion.11
  141.8 0.1 bitcast_dynamic-update-slice_fusion.9
  141.8 1.2 bitcast_dynamic-update-slice_fusion.7
  143.0 1.2 bitcast_dynamic-update-slice_fusion.5
  144.2 0.1 bitcast_dynamic-update-slice_fusion.3
  144.3 0.1 bitcast_dynamic-update-slice_fusion.1
  144.3 1.2 dynamic-slice_dynamic-update-slice_fusion.1
  145.5 0.0 copy-start.2
  145.6 1.2 dynamic-slice_multiply_fusion.1
  146.8 0.3 copy-done.2
  147.1 3.3 %bitcast_subtract_fusion = (f32[1024,512]{1,0:T(8,128)S(1)}, f32[1024,512]{1,0:T(8,128)}, f32[1024,512]{1,0:T(8,128)}) fusion(f32[8,128,512]{2,1,0:T(8,128)S(1)} %get-tuple-element.16, f32[1024,512]{1,0:T(8,128)S(1)} %copy-done.2, f32[8,128,512]{2,1,0:T(8,128)S(1)} %get-tuple-element.17, f32[8,128,512]{2,1,0:T(8,128)S(1)} %get-tuple-element.15), kind=kLoop, calls=%fused_computation.9 | loop fusion | flops 4718592 | bytes 14680064 | tf_op jit(solution)/shard_map/sub | solution.py:21
  150.4 1.5 convolution_bitcast_fusion.1
  151.9 1.7 convolution_bitcast_fusion
  153.6 1.1 pad_maximum_fusion.1
  154.7 1.3 copy.33
  156.0 21.8 %all_to_all.37 = f32[16,16,1024]{2,1,0:T(8,128)S(1)} all-to-all(f32[16,16,1024]{2,1,0:T(8,128)} %bitcast.79), channel_id=1, replica_groups=mesh['fsdp'=16,'tp'=8] {'fsdp'}, dimensions={0} | all-to-all | bytes 2097152 | tf_op jit(solution)/shard_map/all_to_all | solution.py:30
  177.8 0.1 reduce_sum.9
  177.9 0.6 fusion.6
  178.5 10.4 %all_to_all.38 = bf16[16,16,512]{2,1,0:T(8,128)(2,1)S(1)} all-to-all(bf16[16,16,512]{2,1,0:T(8,128)(2,1)S(1)} %broadcast_in_dim.2), channel_id=1, replica_groups=mesh['fsdp'=16,'tp'=8] {'fsdp'}, dimensions={0} | all-to-all | bytes 524288 | tf_op jit(solution)/shard_map/all_to_all | solution.py:26
  189.0 0.7 copy.60
  (13 shorter events, 0.0 us)
Async XLA Ops:
  12.5 2.7 %copy-start = (f32[8,384,512]{2,1,0:T(8,128)}, f32[8,384,512]{2,1,0:T(8,128)S(1)}, u32[]{:S(2)}) copy-start(f32[8,384,512]{2,1,0:T(8,128)S(1)} %pad_maximum_fusion) | copy-start | bytes 18874372
  15.2 14.3 %copy-start.3 = (bf16[16,16384]{1,0:T(8,128)(2,1)S(1)}, bf16[16,16384]{1,0:T(8,128)(2,1)}, u32[]{:S(2)}) copy-start(bf16[16,16384]{1,0:T(8,128)(2,1)} %param.9) | copy-start | bytes 1572868
  17.7 43.6 %collective-permute-start = (f32[384,512]{1,0:T(8,128)}, f32[384,512]{1,0:T(8,128)S(1)}, u32[]{:S(2)}, u32[]{:S(2)}) collective-permute-start(f32[384,512]{1,0:T(8,128)} %get-tuple-element.24), channel_id=1, source_target_pairs={{0,7},{1,0},{2,1},{3,2},{4,3},{5,4},{6,5},{7,6},{8,15},{9,8},{10,9... | collective-permute-start | bytes 2359304 | tf_op jit(solution)/shard_map/ppermute | solution.py:59
  21.5 57.1 %collective-permute-start.1 = (f32[384,512]{1,0:T(8,128)}, f32[384,512]{1,0:T(8,128)S(1)}, u32[]{:S(2)}, u32[]{:S(2)}) collective-permute-start(f32[384,512]{1,0:T(8,128)} %get-tuple-element.23), channel_id=1, source_target_pairs={{0,6},{1,7},{2,0},{3,1},{4,2},{5,3},{6,4},{7,5},{8,14},{9,15},{10,... | collective-permute-start | bytes 2359304 | tf_op jit(solution)/shard_map/ppermute | solution.py:59
  24.3 80.2 %collective-permute-start.2 = (f32[384,512]{1,0:T(8,128)}, f32[384,512]{1,0:T(8,128)S(1)}, u32[]{:S(2)}, u32[]{:S(2)}) collective-permute-start(f32[384,512]{1,0:T(8,128)} %get-tuple-element.22), channel_id=1, source_target_pairs={{0,5},{1,6},{2,7},{3,0},{4,1},{5,2},{6,3},{7,4},{8,13},{9,14},{10,... | collective-permute-start | bytes 2359304 | tf_op jit(solution)/shard_map/ppermute | solution.py:59
  24.3 113.6 %collective-permute-start.3 = (f32[384,512]{1,0:T(8,128)}, f32[384,512]{1,0:T(8,128)}, u32[]{:S(2)}, u32[]{:S(2)}) collective-permute-start(f32[384,512]{1,0:T(8,128)} %get-tuple-element.21), channel_id=1, source_target_pairs={{0,4},{1,5},{2,6},{3,7},{4,0},{5,1},{6,2},{7,3},{8,12},{9,13},{10,... | collective-permute-start | bytes 2359304 | tf_op jit(solution)/shard_map/ppermute | solution.py:59
  25.1 114.1 %collective-permute-start.4 = (f32[384,512]{1,0:T(8,128)}, f32[384,512]{1,0:T(8,128)}, u32[]{:S(2)}, u32[]{:S(2)}) collective-permute-start(f32[384,512]{1,0:T(8,128)} %get-tuple-element.20), channel_id=1, source_target_pairs={{0,3},{1,4},{2,5},{3,6},{4,7},{5,0},{6,1},{7,2},{8,11},{9,12},{10,... | collective-permute-start | bytes 2359304 | tf_op jit(solution)/shard_map/ppermute | solution.py:59
  30.4 120.0 %all-to-all-start = ((bf16[16,16,1024]{2,0,1:T(8,128)(2,1)}), bf16[16,16,1024]{2,0,1:T(8,128)(2,1)S(1)}, u32[]{:S(2)}, u32[]{:S(2)}) async-start(bf16[16,16,1024]{2,0,1:T(8,128)(2,1)} %bitcast.75), calls=%async_computation | async-start | bytes 1048576 | tf_op jit(solution)/shard_map/all_to_all | solution.py:46
  35.4 116.5 %all-gather.2.cloned.1.call-start = ((), (), s32[]{:S(2)}) async-start(), calls=%async_computation.3 | async-start | bytes 1179648 | tf_op jit(solution)/shard_map/all_gather | solution.py:48
  61.2 79.1 %collective-permute-start.5 = (f32[384,512]{1,0:T(8,128)}, f32[384,512]{1,0:T(8,128)S(1)}, u32[]{:S(2)}, u32[]{:S(2)}) collective-permute-start(f32[384,512]{1,0:T(8,128)} %get-tuple-element.19), channel_id=1, source_target_pairs={{0,2},{1,3},{2,4},{3,5},{4,6},{5,7},{6,0},{7,1},{8,10},{9,11},{10,... | collective-permute-start | bytes 2359304 | tf_op jit(solution)/shard_map/ppermute | solution.py:59
  78.6 61.8 %collective-permute-start.6 = (f32[384,512]{1,0:T(8,128)}, f32[384,512]{1,0:T(8,128)S(1)}, u32[]{:S(2)}, u32[]{:S(2)}) collective-permute-start(f32[384,512]{1,0:T(8,128)} %get-tuple-element.18), channel_id=1, source_target_pairs={{0,1},{1,2},{2,3},{3,4},{4,5},{5,6},{6,7},{7,0},{8,9},{9,10},{10,1... | collective-permute-start | bytes 2359304 | tf_op jit(solution)/shard_map/ppermute | solution.py:59
  145.5 1.6 copy-start.2
  150.4 27.5 %copy-start.1 = (f32[1024,512]{1,0:T(8,128)}, f32[1024,512]{1,0:T(8,128)S(1)}, u32[]{:S(2)}) copy-start(f32[1024,512]{1,0:T(8,128)S(1)} %get-tuple-element.37) | copy-start | bytes 6291460
Sparse Core Ops, SparseCore 0:
  39.1 101.1 all-gather.1

commit v4 on v2

--- a/solution.py
+++ b/solution.py
@@ -4,6 +4,7 @@
 import jax.numpy as jnp
 from jax import lax
 from jax.sharding import PartitionSpec as P
+
 
 BETA_ONE = 0.9
 BETA_TWO = 0.95
@@ -30,7 +31,7 @@
     return parts.reshape((size, x.shape[0] // size) + x.shape[1:]).sum(axis=0)
 
 
-def body(
+def step(
     probe_states,
     wq_master,
     wq_first,
@@ -42,7 +43,15 @@
     wkv_grad,
 ):
     fsdp = lax.axis_size("fsdp")
-    columns = lax.all_to_all(probe_states, "fsdp", split_axis=1, concat_axis=0, tiled=True)
+    me = lax.axis_index("fsdp")
+    width = probe_states.shape[1] // fsdp
+    got = [lax.dynamic_slice_in_dim(probe_states, me * width, width, 1)]
+    for k in range(1, fsdp):
+        block = lax.dynamic_slice_in_dim(probe_states, ((me + k) % fsdp) * width, width, 1)
+        got.append(lax.ppermute(block, "fsdp", [(i, (i + k) % fsdp) for i in range(fsdp)]))
+    got = jnp.stack(got[::-1])
+    columns = lax.dynamic_slice_in_dim(jnp.concatenate([got, got]), fsdp - 1 - me, fsdp, 0)
+    columns = columns.reshape(fsdp * probe_states.shape[0], width)
     wkv_new, wkv_mom, wkv_var = adam_step(wkv_master, wkv_first, wkv_second, wkv_grad)
     wkv_rows = lax.all_gather(wkv_new.astype(jnp.bfloat16), "tp", axis=0, tiled=True)
     kv_term = jnp.dot(columns, wkv_rows, preferred_element_type=jnp.float32)
@@ -64,7 +73,7 @@
 
 def solution(mesh):
     return jax.shard_map(
-        body,
+        step,
         mesh=mesh,
         in_specs=(
             P("fsdp", None),

time: 178 us -> 170 us (0.955)
  waiting for transfers between devices: 92.2 us -> 55.5 us
  starting transfers between devices: 14.4 us -> 43.5 us
  blocking collectives: 33.1 us -> 36.1 us
  local copies, waits for them, and re-layouts: 8.42 us -> 5.7 us
    all_gather x1, waiting for transfers between devices: 88.8 us -> 5.17 us  [step(): lax.all_gather(wkv_new.astype(jnp.bfloat16), 'tp', axis=0, tiled=True)]
    ppermute x0 -> x15, waiting for transfers between devices: none -> 48.3 us  [step(): lax.ppermute(block, 'fsdp', [(i, (i + k) % fsdp) for i in range(fsdp)])]
    ppermute x0 -> x15, starting transfers between devices: none -> 35.1 us  [step(): lax.ppermute(block, 'fsdp', [(i, (i + k) % fsdp) for i in range(fsdp)])]
    all_to_all x2 -> x1, starting transfers between devices: 14.4 us -> 8.29 us  [step(): lax.all_to_all(jnp.concatenate(pieces, axis=1), 'tp', split_axis=0, conca...]
    all_to_all x1, blocking collectives: 22 us -> 24.9 us  [scatter_sum_rows(): lax.all_to_all(x, axis_name, split_axis=0, concat_axis=0, tiled=True)]
    all_to_all x1 -> x0, local copies, waits for them, and re-layouts: 2.03 us -> none  [body(): lax.all_to_all(probe_states, 'fsdp', split_axis=1, concat_axis=0, tiled=T...]
    unnamed x21 -> x50, local copies, waits for them, and re-layouts: 3.66 us -> 2.57 us
  transfers between devices with their start and end apart: 3 -> 17, of which waited for: 2 -> 5; matrix products, arithmetic and copies ran while one was open for 4% -> 2% of each run, Pallas kernels for 0% -> 0%
where the time goes in v4:
time: 170 us; the launch traced here: 169 us
  waiting for transfers between devices  55.5 us (33%)
  starting transfers between devices  43.5 us (26%)
  blocking collectives  36.1 us (21%)
  between operations  14.6 us (9%)
  other arithmetic  12 us (7%)
  local copies, waits for them, and re-layouts  5.7 us (3%)
  matrix products  2.08 us (1%)
    ppermute x15, waiting for transfers between devices, step(): lax.ppermute(block, 'fsdp', [(i, (i + k) % fsdp) for i in range(fsdp)])  48.3 us
    ppermute x15, starting transfers between devices, step(): lax.ppermute(block, 'fsdp', [(i, (i + k) % fsdp) for i in range(fsdp)])  35.1 us
    all_to_all x1, blocking collectives, scatter_sum_rows(): lax.all_to_all(x, axis_name, split_axis=0, concat_axis=0, tiled=True)  24.9 us
    all_to_all x1, blocking collectives, gather_rows(): lax.all_to_all(copies, axis_name, split_axis=0, concat_axis=0, tiled=True)  11.1 us
    all_to_all x1, starting transfers between devices, step(): lax.all_to_all(jnp.concatenate(pieces, axis=1), 'tp', split_axis=0, conca...  8.29 us
    all_gather x1, waiting for transfers between devices, step(): lax.all_gather(wkv_new.astype(jnp.bfloat16), 'tp', axis=0, tiled=True)  5.17 us
    mul x1, other arithmetic, adam_step(): first_new = BETA_ONE * first + (1.0 - BETA_ONE) * grad  4.27 us
  transfers between devices with their start and end apart: 17, of which 5 were waited for; matrix products, arithmetic and copies ran while one was open for 2% of the time, Pallas kernels for 0%

profile of v4, /device:TPU:1, one launch (start us, length us, event | category | flops | bytes accessed | tf_op | source)
XLA Modules:
  0.0 169.4 jit_solution(9238858279612781275)
XLA Ops:
  7.2 1.9 %copy.26 = f32[16,8,8,512]{3,2,0,1:T(8,128)S(1)} copy(f32[16,8,8,512]{3,2,1,0:T(8,128)} %bitcast.83) | data formatting | bytes 4194304 | tf_op jit(solution)/shard_map/reshape | solution.py:61
  9.1 0.3 copy-done.2
  9.4 0.6 copy-done.3
  10.0 0.4 bitcast_bitcast_fusion
  10.5 3.3 %pad_maximum_fusion = f32[8,384,512]{2,1,0:T(8,128)} fusion(f32[8,128,512]{2,1,0:T(8,128)S(1)} %get-tuple-element.35, f32[8,128,512]{2,1,0:T(8,128)S(1)} %get-tuple-element.36, f32[8,128,512]{2,1,0:T(8,128)S(1)} %bitcast.79), kind=kLoop, calls=%fused_computation | loop fusion | flops 3145728 | bytes 12582912 | tf_op jit(solution)/shard_map/concatenate | solution.py:62
  13.8 0.0 copy-start.8
  13.8 8.3 %all-to-all-start = ((f32[8,384,512]{2,1,0:T(8,128)}), f32[8,384,512]{2,1,0:T(8,128)}, u32[]{:S(2)}, u32[]{:S(2)}) async-start(f32[8,384,512]{2,1,0:T(8,128)} %pad_maximum_fusion), calls=%async_computation | async-start | bytes 12582912 | tf_op jit(solution)/shard_map/all_to_all | solution.py:62
  22.1 0.0 all-gather.2.cloned.1.call-start
  22.4 0.1 constant_dynamic-slice_fusion.1
  22.5 1.0 collective-permute-start
  23.5 3.2 %collective-permute-start.1 = (bf16[16,1024]{1,0:T(8,128)(2,1)S(1)}, bf16[16,1024]{1,0:T(8,128)(2,1)S(1)}, u32[]{:S(2)}, u32[]{:S(2)}) collective-permute-start(bf16[16,1024]{1,0:T(8,128)(2,1)S(1)} %get-tuple-element.31), channel_id=1, source_target_pairs={{0,112},{8,120},{16,0},{24,8},{32,16},{40,24},{48,32},{56,40},{64,... | collective-permute-start | bytes 98312 | tf_op jit(solution)/shard_map/ppermute | solution.py:51
  26.7 0.7 collective-permute-start.2
  27.4 2.6 %collective-permute-start.3 = (bf16[16,1024]{1,0:T(8,128)(2,1)S(1)}, bf16[16,1024]{1,0:T(8,128)(2,1)S(1)}, u32[]{:S(2)}, u32[]{:S(2)}) collective-permute-start(bf16[16,1024]{1,0:T(8,128)(2,1)S(1)} %get-tuple-element.29), channel_id=1, source_target_pairs={{0,96},{8,104},{16,112},{24,120},{32,0},{40,8},{48,16},{56,24},{64... | collective-permute-start | bytes 98312 | tf_op jit(solution)/shard_map/ppermute | solution.py:51
  30.0 1.0 collective-permute-start.4
  31.0 1.0 fusion.4
  32.1 0.0 all-gather.2.cloned.1.call-update
  32.1 0.0 collective-permute-done
  32.1 1.2 collective-permute-start.5
  33.3 1.4 collective-permute-start.6
  34.7 0.0 collective-permute-done.2
  34.7 0.7 collective-permute-start.7
  35.5 0.6 collective-permute-start.8
  36.1 0.0 collective-permute-done.4
  36.1 2.8 %collective-permute-start.9 = (bf16[16,1024]{1,0:T(8,128)(2,1)S(1)}, bf16[16,1024]{1,0:T(8,128)(2,1)S(1)}, u32[]{:S(2)}, u32[]{:S(2)}) collective-permute-start(bf16[16,1024]{1,0:T(8,128)(2,1)S(1)} %get-tuple-element.23), channel_id=1, source_target_pairs={{0,48},{8,56},{16,64},{24,72},{32,80},{40,88},{48,96},{56,104},{64... | collective-permute-start | bytes 98312 | tf_op jit(solution)/shard_map/ppermute | solution.py:51
  38.9 0.0 collective-permute-done.5
  38.9 4.0 %collective-permute-start.10 = (bf16[16,1024]{1,0:T(8,128)(2,1)S(1)}, bf16[16,1024]{1,0:T(8,128)(2,1)S(1)}, u32[]{:S(2)}, u32[]{:S(2)}) collective-permute-start(bf16[16,1024]{1,0:T(8,128)(2,1)S(1)} %get-tuple-element.22), channel_id=1, source_target_pairs={{0,40},{8,48},{16,56},{24,64},{32,72},{40,80},{48,88},{56,96},{64,... | collective-permute-start | bytes 98312 | tf_op jit(solution)/shard_map/ppermute | solution.py:51
  42.9 43.7 %collective-permute-done.6 = bf16[16,1024]{1,0:T(8,128)(2,1)S(1)} collective-permute-done((bf16[16,1024]{1,0:T(8,128)(2,1)S(1)}, bf16[16,1024]{1,0:T(8,128)(2,1)S(1)}, u32[]{:S(2)}, u32[]{:S(2)}) %collective-permute-start.6) | collective-permute-done | bytes 32800 | tf_op jit(solution)/shard_map/ppermute | solution.py:51
  86.6 2.7 %collective-permute-start.11 = (bf16[16,1024]{1,0:T(8,128)(2,1)S(1)}, bf16[16,1024]{1,0:T(8,128)(2,1)S(1)}, u32[]{:S(2)}, u32[]{:S(2)}) collective-permute-start(bf16[16,1024]{1,0:T(8,128)(2,1)S(1)} %get-tuple-element.21), channel_id=1, source_target_pairs={{0,32},{8,40},{16,48},{24,56},{32,64},{40,72},{48,80},{56,88},{64,... | collective-permute-start | bytes 98312 | tf_op jit(solution)/shard_map/ppermute | solution.py:51
  89.3 0.0 collective-permute-done.7
  89.3 12.5 %collective-permute-start.12 = (bf16[16,1024]{1,0:T(8,128)(2,1)S(1)}, bf16[16,1024]{1,0:T(8,128)(2,1)S(1)}, u32[]{:S(2)}, u32[]{:S(2)}) collective-permute-start(bf16[16,1024]{1,0:T(8,128)(2,1)S(1)} %get-tuple-element.20), channel_id=1, source_target_pairs={{0,24},{8,32},{16,40},{24,48},{32,56},{40,64},{48,72},{56,80},{64,... | collective-permute-start | bytes 98312 | tf_op jit(solution)/shard_map/ppermute | solution.py:51
  101.8 0.6 collective-permute-start.13
  102.4 0.0 collective-permute-done.10
  102.5 0.0 collective-permute-done.11
  102.5 2.6 %collective-permute-done.12 = bf16[16,1024]{1,0:T(8,128)(2,1)S(1)} collective-permute-done((bf16[16,1024]{1,0:T(8,128)(2,1)S(1)}, bf16[16,1024]{1,0:T(8,128)(2,1)S(1)}, u32[]{:S(2)}, u32[]{:S(2)}) %collective-permute-start.12) | collective-permute-done | bytes 32800 | tf_op jit(solution)/shard_map/ppermute | solution.py:51
  105.1 2.0 %collective-permute-done.13 = bf16[16,1024]{1,0:T(8,128)(2,1)S(1)} collective-permute-done((bf16[16,1024]{1,0:T(8,128)(2,1)S(1)}, bf16[16,1024]{1,0:T(8,128)(2,1)S(1)}, u32[]{:S(2)}, u32[]{:S(2)}) %collective-permute-start.13) | collective-permute-done | bytes 32800 | tf_op jit(solution)/shard_map/ppermute | solution.py:51
  107.4 5.2 %all-gather.2.cloned.1.call-done = bf16[1024,512]{1,0:T(8,128)(2,1)} async-done(((bf16[128,512]{1,0:T(8,128)(2,1)}), bf16[1024,512]{1,0:T(8,128)(2,1)}) %all-gather.2.cloned.1.call-update) | async-done | bytes 1048592 | tf_op jit(solution)/shard_map/all_gather | solution.py:56
  112.6 1.7 fusion.8
  114.2 2.0 %all-to-all-done = f32[8,384,512]{2,1,0:T(8,128)} async-done(((f32[8,384,512]{2,1,0:T(8,128)}), f32[8,384,512]{2,1,0:T(8,128)}, u32[]{:S(2)}, u32[]{:S(2)}) %all-to-all-start) | async-done | bytes 6291488 | tf_op jit(solution)/shard_map/all_to_all | solution.py:62
  116.3 4.3 %slice_multiply_fusion.1 = (f32[8,128,512]{2,1,0:T(8,128)S(1)}, f32[8,128,512]{2,1,0:T(8,128)S(1)}, f32[8,128,512]{2,1,0:T(8,128)S(1)}) fusion(f32[8,384,512]{2,1,0:T(8,128)} %all-to-all-done), kind=kLoop, calls=%fused_computation.7 | loop fusion | flops 1048576 | bytes 12582912 | tf_op jit(solution)/shard_map/mul | solution.py:18
  120.6 3.3 %bitcast_subtract_fusion = (f32[1024,512]{1,0:T(8,128)S(1)}, f32[1024,512]{1,0:T(8,128)}, f32[1024,512]{1,0:T(8,128)}) fusion(f32[8,128,512]{2,1,0:T(8,128)S(1)} %get-tuple-element.17, f32[1024,512]{1,0:T(8,128)S(1)} %copy-done.1, f32[8,128,512]{2,1,0:T(8,128)S(1)} %get-tuple-element.16, f32[8,128,512]{2,1,0:T(8,128)S(1)} %get-tuple-element.15), kind=kLoop, calls=%fused_computation.9 | loop fusion | flops 4718592 | bytes 14680064 | tf_op jit(solution)/shard_map/sub | solution.py:21
  123.8 0.4 fusion.1
  124.3 0.1 pad_maximum_fusion.1
  124.4 0.8 copy-done
  125.1 24.9 %all_to_all.23 = f32[16,16,1024]{2,1,0:T(8,128)S(1)} all-to-all(f32[16,16,1024]{2,1,0:T(8,128)S(1)} %bitcast.82), channel_id=1, replica_groups=mesh['fsdp'=16,'tp'=8] {'fsdp'}, dimensions={0} | all-to-all | bytes 2097152 | tf_op jit(solution)/shard_map/all_to_all | solution.py:30
  150.1 0.1 reduce_sum.9
  150.1 0.6 fusion.7
  150.8 11.1 %all_to_all.24 = bf16[16,16,512]{2,1,0:T(8,128)(2,1)S(1)} all-to-all(bf16[16,16,512]{2,1,0:T(8,128)(2,1)S(1)} %broadcast_in_dim.2), channel_id=1, replica_groups=mesh['fsdp'=16,'tp'=8] {'fsdp'}, dimensions={0} | all-to-all | bytes 524288 | tf_op jit(solution)/shard_map/all_to_all | solution.py:26
  161.9 0.7 copy.59
  (54 shorter events, 0.3 us)
Async XLA Ops:
  7.2 2.2 %copy-start.2 = (f32[128,4096]{1,0:T(8,128)S(1)}, f32[128,4096]{1,0:T(8,128)}, u32[]{:S(2)}) copy-start(f32[128,4096]{1,0:T(8,128)} %param.12) | copy-start | bytes 6291460
  7.2 2.8 %copy-start.3 = (f32[128,4096]{1,0:T(8,128)S(1)}, f32[128,4096]{1,0:T(8,128)}, u32[]{:S(2)}) copy-start(f32[128,4096]{1,0:T(8,128)} %param.11) | copy-start | bytes 6291460
  13.8 8.6 %copy-start.4 = (bf16[16,16384]{1,0:T(8,128)(2,1)S(1)}, bf16[16,16384]{1,0:T(8,128)(2,1)}, u32[]{:S(2)}) copy-start(bf16[16,16384]{1,0:T(8,128)(2,1)} %param.9) | copy-start | bytes 1572868
  13.8 17.2 %copy-start.5 = (f32[128,512]{1,0:T(8,128)S(1)}, f32[128,512]{1,0:T(8,128)}, u32[]{:S(2)}) copy-start(f32[128,512]{1,0:T(8,128)} %param.14) | copy-start | bytes 786436
  13.8 17.2 %copy-start.6 = (f32[128,512]{1,0:T(8,128)S(1)}, f32[128,512]{1,0:T(8,128)}, u32[]{:S(2)}) copy-start(f32[128,512]{1,0:T(8,128)} %param.17) | copy-start | bytes 786436
  13.8 17.2 %copy-start.7 = (f32[128,512]{1,0:T(8,128)S(1)}, f32[128,512]{1,0:T(8,128)}, u32[]{:S(2)}) copy-start(f32[128,512]{1,0:T(8,128)} %param.16) | copy-start | bytes 786436
  13.8 17.2 %copy-start.8 = (f32[128,512]{1,0:T(8,128)S(1)}, f32[128,512]{1,0:T(8,128)}, u32[]{:S(2)}) copy-start(f32[128,512]{1,0:T(8,128)} %param.15) | copy-start | bytes 786436
  13.8 102.4 %all-to-all-start = ((f32[8,384,512]{2,1,0:T(8,128)}), f32[8,384,512]{2,1,0:T(8,128)}, u32[]{:S(2)}, u32[]{:S(2)}) async-start(f32[8,384,512]{2,1,0:T(8,128)} %pad_maximum_fusion), calls=%async_computation | async-start | bytes 12582912 | tf_op jit(solution)/shard_map/all_to_all | solution.py:62
  22.1 90.4 %all-gather.2.cloned.1.call-start = ((), (), s32[]{:S(2)}) async-start(), calls=%async_computation.3 | async-start | bytes 1179648 | tf_op jit(solution)/shard_map/all_gather | solution.py:56
  22.5 9.6 %collective-permute-start = (bf16[16,1024]{1,0:T(8,128)(2,1)S(1)}, bf16[16,1024]{1,0:T(8,128)(2,1)S(1)}, u32[]{:S(2)}, u32[]{:S(2)}) collective-permute-start(bf16[16,1024]{1,0:T(8,128)(2,1)S(1)} %get-tuple-element.32), channel_id=1, source_target_pairs={{0,120},{8,0},{16,8},{24,16},{32,24},{40,32},{48,40},{56,48},{64,5... | collective-permute-start | bytes 98312 | tf_op jit(solution)/shard_map/ppermute | solution.py:51
  23.5 9.8 %collective-permute-start.1 = (bf16[16,1024]{1,0:T(8,128)(2,1)S(1)}, bf16[16,1024]{1,0:T(8,128)(2,1)S(1)}, u32[]{:S(2)}, u32[]{:S(2)}) collective-permute-start(bf16[16,1024]{1,0:T(8,128)(2,1)S(1)} %get-tuple-element.31), channel_id=1, source_target_pairs={{0,112},{8,120},{16,0},{24,8},{32,16},{40,24},{48,32},{56,40},{64,... | collective-permute-start | bytes 98312 | tf_op jit(solution)/shard_map/ppermute | solution.py:51
  26.7 8.0 %collective-permute-start.2 = (bf16[16,1024]{1,0:T(8,128)(2,1)S(1)}, bf16[16,1024]{1,0:T(8,128)(2,1)S(1)}, u32[]{:S(2)}, u32[]{:S(2)}) collective-permute-start(bf16[16,1024]{1,0:T(8,128)(2,1)S(1)} %get-tuple-element.30), channel_id=1, source_target_pairs={{0,104},{8,112},{16,120},{24,0},{32,8},{40,16},{48,24},{56,32},{64... | collective-permute-start | bytes 98312 | tf_op jit(solution)/shard_map/ppermute | solution.py:51
  27.4 8.1 %collective-permute-start.3 = (bf16[16,1024]{1,0:T(8,128)(2,1)S(1)}, bf16[16,1024]{1,0:T(8,128)(2,1)S(1)}, u32[]{:S(2)}, u32[]{:S(2)}) collective-permute-start(bf16[16,1024]{1,0:T(8,128)(2,1)S(1)} %get-tuple-element.29), channel_id=1, source_target_pairs={{0,96},{8,104},{16,112},{24,120},{32,0},{40,8},{48,16},{56,24},{64... | collective-permute-start | bytes 98312 | tf_op jit(solution)/shard_map/ppermute | solution.py:51
  30.0 6.1 %collective-permute-start.4 = (bf16[16,1024]{1,0:T(8,128)(2,1)S(1)}, bf16[16,1024]{1,0:T(8,128)(2,1)S(1)}, u32[]{:S(2)}, u32[]{:S(2)}) collective-permute-start(bf16[16,1024]{1,0:T(8,128)(2,1)S(1)} %get-tuple-element.28), channel_id=1, source_target_pairs={{0,88},{8,96},{16,104},{24,112},{32,120},{40,0},{48,8},{56,16},{64... | collective-permute-start | bytes 98312 | tf_op jit(solution)/shard_map/ppermute | solution.py:51
  32.1 6.8 %collective-permute-start.5 = (bf16[16,1024]{1,0:T(8,128)(2,1)S(1)}, bf16[16,1024]{1,0:T(8,128)(2,1)S(1)}, u32[]{:S(2)}, u32[]{:S(2)}) collective-permute-start(bf16[16,1024]{1,0:T(8,128)(2,1)S(1)} %get-tuple-element.27), channel_id=1, source_target_pairs={{0,80},{8,88},{16,96},{24,104},{32,112},{40,120},{48,0},{56,8},{64... | collective-permute-start | bytes 98312 | tf_op jit(solution)/shard_map/ppermute | solution.py:51
  33.3 53.2 %collective-permute-start.6 = (bf16[16,1024]{1,0:T(8,128)(2,1)S(1)}, bf16[16,1024]{1,0:T(8,128)(2,1)S(1)}, u32[]{:S(2)}, u32[]{:S(2)}) collective-permute-start(bf16[16,1024]{1,0:T(8,128)(2,1)S(1)} %get-tuple-element.26), channel_id=1, source_target_pairs={{0,72},{8,80},{16,88},{24,96},{32,104},{40,112},{48,120},{56,0},{6... | collective-permute-start | bytes 98312 | tf_op jit(solution)/shard_map/ppermute | solution.py:51
  34.7 54.6 %collective-permute-start.7 = (bf16[16,1024]{1,0:T(8,128)(2,1)S(1)}, bf16[16,1024]{1,0:T(8,128)(2,1)S(1)}, u32[]{:S(2)}, u32[]{:S(2)}) collective-permute-start(bf16[16,1024]{1,0:T(8,128)(2,1)S(1)} %get-tuple-element.25), channel_id=1, source_target_pairs={{0,64},{8,72},{16,80},{24,88},{32,96},{40,104},{48,112},{56,120},{... | collective-permute-start | bytes 98312 | tf_op jit(solution)/shard_map/ppermute | solution.py:51
  35.5 66.4 %collective-permute-start.8 = (bf16[16,1024]{1,0:T(8,128)(2,1)S(1)}, bf16[16,1024]{1,0:T(8,128)(2,1)S(1)}, u32[]{:S(2)}, u32[]{:S(2)}) collective-permute-start(bf16[16,1024]{1,0:T(8,128)(2,1)S(1)} %get-tuple-element.24), channel_id=1, source_target_pairs={{0,56},{8,64},{16,72},{24,80},{32,88},{40,96},{48,104},{56,112},{6... | collective-permute-start | bytes 98312 | tf_op jit(solution)/shard_map/ppermute | solution.py:51
  36.1 66.3 %collective-permute-start.9 = (bf16[16,1024]{1,0:T(8,128)(2,1)S(1)}, bf16[16,1024]{1,0:T(8,128)(2,1)S(1)}, u32[]{:S(2)}, u32[]{:S(2)}) collective-permute-start(bf16[16,1024]{1,0:T(8,128)(2,1)S(1)} %get-tuple-element.23), channel_id=1, source_target_pairs={{0,48},{8,56},{16,64},{24,72},{32,80},{40,88},{48,96},{56,104},{64... | collective-permute-start | bytes 98312 | tf_op jit(solution)/shard_map/ppermute | solution.py:51
  38.9 63.5 %collective-permute-start.10 = (bf16[16,1024]{1,0:T(8,128)(2,1)S(1)}, bf16[16,1024]{1,0:T(8,128)(2,1)S(1)}, u32[]{:S(2)}, u32[]{:S(2)}) collective-permute-start(bf16[16,1024]{1,0:T(8,128)(2,1)S(1)} %get-tuple-element.22), channel_id=1, source_target_pairs={{0,40},{8,48},{16,56},{24,64},{32,72},{40,80},{48,88},{56,96},{64,... | collective-permute-start | bytes 98312 | tf_op jit(solution)/shard_map/ppermute | solution.py:51
  86.6 15.9 %collective-permute-start.11 = (bf16[16,1024]{1,0:T(8,128)(2,1)S(1)}, bf16[16,1024]{1,0:T(8,128)(2,1)S(1)}, u32[]{:S(2)}, u32[]{:S(2)}) collective-permute-start(bf16[16,1024]{1,0:T(8,128)(2,1)S(1)} %get-tuple-element.21), channel_id=1, source_target_pairs={{0,32},{8,40},{16,48},{24,56},{32,64},{40,72},{48,80},{56,88},{64,... | collective-permute-start | bytes 98312 | tf_op jit(solution)/shard_map/ppermute | solution.py:51
  89.3 15.8 %collective-permute-start.12 = (bf16[16,1024]{1,0:T(8,128)(2,1)S(1)}, bf16[16,1024]{1,0:T(8,128)(2,1)S(1)}, u32[]{:S(2)}, u32[]{:S(2)}) collective-permute-start(bf16[16,1024]{1,0:T(8,128)(2,1)S(1)} %get-tuple-element.20), channel_id=1, source_target_pairs={{0,24},{8,32},{16,40},{24,48},{32,56},{40,64},{48,72},{56,80},{64,... | collective-permute-start | bytes 98312 | tf_op jit(solution)/shard_map/ppermute | solution.py:51
  101.8 5.3 %collective-permute-start.13 = (bf16[16,1024]{1,0:T(8,128)(2,1)S(1)}, bf16[16,1024]{1,0:T(8,128)(2,1)S(1)}, u32[]{:S(2)}, u32[]{:S(2)}) collective-permute-start(bf16[16,1024]{1,0:T(8,128)(2,1)S(1)} %get-tuple-element.19), channel_id=1, source_target_pairs={{0,16},{8,24},{16,32},{24,40},{32,48},{40,56},{48,64},{56,72},{64,... | collective-permute-start | bytes 98312 | tf_op jit(solution)/shard_map/ppermute | solution.py:51
  102.4 4.7 %collective-permute-start.14 = (bf16[16,1024]{1,0:T(8,128)(2,1)S(1)}, bf16[16,1024]{1,0:T(8,128)(2,1)S(1)}, u32[]{:S(2)}, u32[]{:S(2)}) collective-permute-start(bf16[16,1024]{1,0:T(8,128)(2,1)S(1)} %get-tuple-element.18), channel_id=1, source_target_pairs={{0,8},{8,16},{16,24},{24,32},{32,40},{40,48},{48,56},{56,64},{64,7... | collective-permute-start | bytes 98312 | tf_op jit(solution)/shard_map/ppermute | solution.py:51
  116.3 4.3 %copy-start.1 = (f32[1024,512]{1,0:T(8,128)S(1)}, f32[1024,512]{1,0:T(8,128)}, u32[]{:S(2)}) copy-start(f32[1024,512]{1,0:T(8,128)} %param.13) | copy-start | bytes 6291460
  123.8 1.3 copy-start
Sparse Core Ops, SparseCore 0:
  32.2 80.3 all-gather.1

commit v5 on v4

--- a/solution.py
+++ b/solution.py
@@ -53,10 +53,17 @@
     columns = lax.dynamic_slice_in_dim(jnp.concatenate([got, got]), fsdp - 1 - me, fsdp, 0)
     columns = columns.reshape(fsdp * probe_states.shape[0], width)
     wkv_new, wkv_mom, wkv_var = adam_step(wkv_master, wkv_first, wkv_second, wkv_grad)
-    wkv_rows = lax.all_gather(wkv_new.astype(jnp.bfloat16), "tp", axis=0, tiled=True)
+    tp = lax.axis_size("tp")
+    me_tp = lax.axis_index("tp")
+    wkv_low = wkv_new.astype(jnp.bfloat16)
+    rows_kv = [wkv_low]
+    for k in range(1, tp):
+        rows_kv.append(lax.ppermute(wkv_low, "tp", [(i, (i + k) % tp) for i in range(tp)]))
+    rows_kv = jnp.stack(rows_kv[::-1])
+    wkv_rows = lax.dynamic_slice_in_dim(jnp.concatenate([rows_kv, rows_kv]), tp - 1 - me_tp, tp, 0)
+    wkv_rows = wkv_rows.reshape(tp * wkv_low.shape[0], wkv_low.shape[1])
     kv_term = jnp.dot(columns, wkv_rows, preferred_element_type=jnp.float32)
 
-    tp = lax.axis_size("tp")
     rows, cols = wq_master.shape
     pieces = [x.reshape(rows, tp, cols // tp).transpose(1, 0, 2) for x in (wq_master, wq_first, wq_second)]
     state = lax.all_to_all(jnp.concatenate(pieces, axis=1), "tp", split_axis=0, concat_axis=0, tiled=True)

time: 170 us -> 197 us (1.16)
  waiting for transfers between devices: 55.5 us -> 88.3 us
  between operations: 14.6 us -> 1.08 us
  starting transfers between devices: 43.5 us -> 52.5 us
    ppermute x15, waiting for transfers between devices: 48.3 us -> 80 us  [step(): lax.ppermute(block, 'fsdp', [(i, (i + k) % fsdp) for i in range(fsdp)])]
    ppermute x0 -> x7, starting transfers between devices: none -> 16.7 us  [step(): lax.ppermute(wkv_low, 'tp', [(i, (i + k) % tp) for i in range(tp)])]
    ppermute x0 -> x7, waiting for transfers between devices: none -> 8.28 us  [step(): lax.ppermute(wkv_low, 'tp', [(i, (i + k) % tp) for i in range(tp)])]
    all_gather x1 -> x0, waiting for transfers between devices: 5.17 us -> none  [step(): lax.all_gather(wkv_new.astype(jnp.bfloat16), 'tp', axis=0, tiled=True)]
    ppermute x15, starting transfers between devices: 35.1 us -> 30.2 us  [step(): lax.ppermute(block, 'fsdp', [(i, (i + k) % fsdp) for i in range(fsdp)])]
    all_to_all x1, starting transfers between devices: 8.29 us -> 5.54 us  [step(): lax.all_to_all(jnp.concatenate(pieces, axis=1), 'tp', split_axis=0, conca...]
    all_to_all x1, waiting for transfers between devices: 2.04 us -> 0.01 us  [step(): lax.all_to_all(jnp.concatenate(pieces, axis=1), 'tp', split_axis=0, conca...]
  transfers between devices with their start and end apart: 17 -> 23, of which waited for: 5 -> 17; matrix products, arithmetic and copies ran while one was open for 2% -> 3% of each run, Pallas kernels for 0% -> 0%
where the time goes in v5:
time: 197 us; the launch traced here: 196 us
  waiting for transfers between devices  88.3 us (45%)
  starting transfers between devices  52.5 us (27%)
  blocking collectives  34.3 us (17%)
  other arithmetic  13.3 us (7%)
  local copies, waits for them, and re-layouts  6.12 us (3%)
    ppermute x15, waiting for transfers between devices, step(): lax.ppermute(block, 'fsdp', [(i, (i + k) % fsdp) for i in range(fsdp)])  80 us
    ppermute x15, starting transfers between devices, step(): lax.ppermute(block, 'fsdp', [(i, (i + k) % fsdp) for i in range(fsdp)])  30.2 us
    all_to_all x1, blocking collectives, scatter_sum_rows(): lax.all_to_all(x, axis_name, split_axis=0, concat_axis=0, tiled=True)  23.1 us
    ppermute x7, starting transfers between devices, step(): lax.ppermute(wkv_low, 'tp', [(i, (i + k) % tp) for i in range(tp)])  16.7 us
    all_to_all x1, blocking collectives, gather_rows(): lax.all_to_all(copies, axis_name, split_axis=0, concat_axis=0, tiled=True)  11.1 us
    ppermute x7, waiting for transfers between devices, step(): lax.ppermute(wkv_low, 'tp', [(i, (i + k) % tp) for i in range(tp)])  8.28 us
    all_to_all x1, starting transfers between devices, step(): lax.all_to_all(jnp.concatenate(pieces, axis=1), 'tp', split_axis=0, conca...  5.54 us
    mul x1, other arithmetic, adam_step(): first_new = BETA_ONE * first + (1.0 - BETA_ONE) * grad  4.27 us
  transfers between devices with their start and end apart: 23, of which 17 were waited for; matrix products, arithmetic and copies ran while one was open for 3% of the time, Pallas kernels for 0%

profile of v5, /device:TPU:1, one launch (start us, length us, event | category | flops | bytes accessed | tf_op | source)
XLA Modules:
  0.0 196.4 jit_solution(16281123637898398142)
XLA Ops:
  0.7 2.3 %fusion.4 = (bf16[128,512]{1,0:T(8,128)(2,1)S(1)}, f32[128,512]{1,0:T(8,128)}, f32[128,512]{1,0:T(8,128)}, f32[128,512]{1,0:T(8,128)}) fusion(f32[128,512]{1,0:T(8,128)} %param.14, f32[128,512]{1,0:T(8,128)} %param.17, f32[128,512]{1,0:T(8,128)} %param.16, f32[128,512]{1,0:T(8,128)} %param.15), kind=kLoop, calls=%fused_computation.82 | loop fusion | flops 786432 | bytes 1966080 | tf_op jit(solution)/shard_map/convert_element_type | solution.py:58
  3.0 6.6 %collective-permute-start.15 = (bf16[128,512]{1,0:T(8,128)(2,1)S(1)}, bf16[128,512]{1,0:T(8,128)(2,1)S(1)}, u32[]{:S(2)}, u32[]{:S(2)}) collective-permute-start(bf16[128,512]{1,0:T(8,128)(2,1)S(1)} %get-tuple-element.8), channel_id=1, source_target_pairs={{0,7},{1,0},{2,1},{3,2},{4,3},{5,4},{6,5},{7,6},{8,15},{9,8},{10,9... | collective-permute-start | bytes 393224 | tf_op jit(solution)/shard_map/ppermute | solution.py:61
  9.6 0.5 collective-permute-start.16
  10.1 2.4 %collective-permute-start.18 = (bf16[128,512]{1,0:T(8,128)(2,1)S(1)}, bf16[128,512]{1,0:T(8,128)(2,1)S(1)}, u32[]{:S(2)}, u32[]{:S(2)}) collective-permute-start(bf16[128,512]{1,0:T(8,128)(2,1)S(1)} %get-tuple-element.8), channel_id=1, source_target_pairs={{0,4},{1,5},{2,6},{3,7},{4,0},{5,1},{6,2},{7,3},{8,12},{9,13},{10,... | collective-permute-start | bytes 393224 | tf_op jit(solution)/shard_map/ppermute | solution.py:61
  12.5 0.7 constant_dynamic-slice_fusion.2
  13.2 1.5 collective-permute-start
  14.9 1.4 copy-done.3
  16.4 0.6 copy-done.4
  17.0 0.6 bitcast_bitcast_fusion
  17.6 3.4 %pad_maximum_fusion = f32[8,384,512]{2,1,0:T(8,128)} fusion(f32[8,128,512]{2,1,0:T(8,128)S(1)} %get-tuple-element.35, f32[8,128,512]{2,1,0:T(8,128)S(1)} %get-tuple-element.36, f32[8,128,512]{2,1,0:T(8,128)S(1)} %bitcast.104), kind=kLoop, calls=%fused_computation | loop fusion | flops 3145728 | bytes 12582912 | tf_op jit(solution)/shard_map/concatenate | solution.py:69
  21.0 5.5 %all-to-all-start = ((f32[8,384,512]{2,1,0:T(8,128)}), f32[8,384,512]{2,1,0:T(8,128)}, u32[]{:S(2)}, u32[]{:S(2)}) async-start(f32[8,384,512]{2,1,0:T(8,128)} %pad_maximum_fusion), calls=%async_computation | async-start | bytes 12582912 | tf_op jit(solution)/shard_map/all_to_all | solution.py:69
  26.6 3.3 %collective-permute-start.1 = (bf16[16,1024]{1,0:T(8,128)(2,1)S(1)}, bf16[16,1024]{1,0:T(8,128)(2,1)S(1)}, u32[]{:S(2)}, u32[]{:S(2)}) collective-permute-start(bf16[16,1024]{1,0:T(8,128)(2,1)S(1)} %copy-done.12), channel_id=1, source_target_pairs={{0,112},{8,120},{16,0},{24,8},{32,16},{40,24},{48,32},{56,40},{64,... | collective-permute-start | bytes 98312 | tf_op jit(solution)/shard_map/ppermute | solution.py:51
  29.8 1.0 collective-permute-done.1
  30.9 7.1 %collective-permute-start.2 = (bf16[16,1024]{1,0:T(8,128)(2,1)S(1)}, bf16[16,1024]{1,0:T(8,128)(2,1)S(1)}, u32[]{:S(2)}, u32[]{:S(2)}) collective-permute-start(bf16[16,1024]{1,0:T(8,128)(2,1)S(1)} %copy-done.11), channel_id=1, source_target_pairs={{0,104},{8,112},{16,120},{24,0},{32,8},{40,16},{48,24},{56,32},{64... | collective-permute-start | bytes 98312 | tf_op jit(solution)/shard_map/ppermute | solution.py:51
  38.0 1.0 collective-permute-done.2
  39.0 1.3 collective-permute-start.3
  40.4 3.3 %collective-permute-done.3 = bf16[16,1024]{1,0:T(8,128)(2,1)S(1)} collective-permute-done((bf16[16,1024]{1,0:T(8,128)(2,1)S(1)}, bf16[16,1024]{1,0:T(8,128)(2,1)S(1)}, u32[]{:S(2)}, u32[]{:S(2)}) %collective-permute-start.3) | collective-permute-done | bytes 32800 | tf_op jit(solution)/shard_map/ppermute | solution.py:51
  43.7 3.3 %collective-permute-start.4 = (bf16[16,1024]{1,0:T(8,128)(2,1)S(1)}, bf16[16,1024]{1,0:T(8,128)(2,1)S(1)}, u32[]{:S(2)}, u32[]{:S(2)}) collective-permute-start(bf16[16,1024]{1,0:T(8,128)(2,1)S(1)} %copy-done.9), channel_id=1, source_target_pairs={{0,88},{8,96},{16,104},{24,112},{32,120},{40,0},{48,8},{56,16},{64... | collective-permute-start | bytes 98312 | tf_op jit(solution)/shard_map/ppermute | solution.py:51
  47.0 8.6 %collective-permute-done.4 = bf16[16,1024]{1,0:T(8,128)(2,1)S(1)} collective-permute-done((bf16[16,1024]{1,0:T(8,128)(2,1)S(1)}, bf16[16,1024]{1,0:T(8,128)(2,1)S(1)}, u32[]{:S(2)}, u32[]{:S(2)}) %collective-permute-start.4) | collective-permute-done | bytes 32800 | tf_op jit(solution)/shard_map/ppermute | solution.py:51
  55.5 0.5 collective-permute-start.5
  56.0 3.9 %collective-permute-done.5 = bf16[16,1024]{1,0:T(8,128)(2,1)S(1)} collective-permute-done((bf16[16,1024]{1,0:T(8,128)(2,1)S(1)}, bf16[16,1024]{1,0:T(8,128)(2,1)S(1)}, u32[]{:S(2)}, u32[]{:S(2)}) %collective-permute-start.5) | collective-permute-done | bytes 32800 | tf_op jit(solution)/shard_map/ppermute | solution.py:51
  60.0 19.7 %collective-permute-done.6 = bf16[16,1024]{1,0:T(8,128)(2,1)S(1)} collective-permute-done((bf16[16,1024]{1,0:T(8,128)(2,1)S(1)}, bf16[16,1024]{1,0:T(8,128)(2,1)S(1)}, u32[]{:S(2)}, u32[]{:S(2)}) %collective-permute-start.6) | collective-permute-done | bytes 32800 | tf_op jit(solution)/shard_map/ppermute | solution.py:51
  79.8 0.9 collective-permute-start.7
  80.7 16.6 %collective-permute-done.7 = bf16[16,1024]{1,0:T(8,128)(2,1)S(1)} collective-permute-done((bf16[16,1024]{1,0:T(8,128)(2,1)S(1)}, bf16[16,1024]{1,0:T(8,128)(2,1)S(1)}, u32[]{:S(2)}, u32[]{:S(2)}) %collective-permute-start.7) | collective-permute-done | bytes 32800 | tf_op jit(solution)/shard_map/ppermute | solution.py:51
  97.3 6.3 %collective-permute-done.8 = bf16[16,1024]{1,0:T(8,128)(2,1)S(1)} collective-permute-done((bf16[16,1024]{1,0:T(8,128)(2,1)S(1)}, bf16[16,1024]{1,0:T(8,128)(2,1)S(1)}, u32[]{:S(2)}, u32[]{:S(2)}) %collective-permute-start.8) | collective-permute-done | bytes 32800 | tf_op jit(solution)/shard_map/ppermute | solution.py:51
  103.6 6.5 %collective-permute-start.9 = (bf16[16,1024]{1,0:T(8,128)(2,1)S(1)}, bf16[16,1024]{1,0:T(8,128)(2,1)S(1)}, u32[]{:S(2)}, u32[]{:S(2)}) collective-permute-start(bf16[16,1024]{1,0:T(8,128)(2,1)S(1)} %get-tuple-element.23), channel_id=1, source_target_pairs={{0,48},{8,56},{16,64},{24,72},{32,80},{40,88},{48,96},{56,104},{64... | collective-permute-start | bytes 98312 | tf_op jit(solution)/shard_map/ppermute | solution.py:51
  110.1 1.0 collective-permute-done.9
  111.1 2.4 %collective-permute-start.10 = (bf16[16,1024]{1,0:T(8,128)(2,1)S(1)}, bf16[16,1024]{1,0:T(8,128)(2,1)S(1)}, u32[]{:S(2)}, u32[]{:S(2)}) collective-permute-start(bf16[16,1024]{1,0:T(8,128)(2,1)S(1)} %get-tuple-element.22), channel_id=1, source_target_pairs={{0,40},{8,48},{16,56},{24,64},{32,72},{40,80},{48,88},{56,96},{64,... | collective-permute-start | bytes 98312 | tf_op jit(solution)/shard_map/ppermute | solution.py:51
  113.5 3.4 %collective-permute-done.10 = bf16[16,1024]{1,0:T(8,128)(2,1)S(1)} collective-permute-done((bf16[16,1024]{1,0:T(8,128)(2,1)S(1)}, bf16[16,1024]{1,0:T(8,128)(2,1)S(1)}, u32[]{:S(2)}, u32[]{:S(2)}) %collective-permute-start.10) | collective-permute-done | bytes 32800 | tf_op jit(solution)/shard_map/ppermute | solution.py:51
  116.9 1.8 collective-permute-start.11
  118.7 3.6 %collective-permute-done.11 = bf16[16,1024]{1,0:T(8,128)(2,1)S(1)} collective-permute-done((bf16[16,1024]{1,0:T(8,128)(2,1)S(1)}, bf16[16,1024]{1,0:T(8,128)(2,1)S(1)}, u32[]{:S(2)}, u32[]{:S(2)}) %collective-permute-start.11) | collective-permute-done | bytes 32800 | tf_op jit(solution)/shard_map/ppermute | solution.py:51
  122.3 1.5 collective-permute-start.12
  123.7 4.4 %collective-permute-done.12 = bf16[16,1024]{1,0:T(8,128)(2,1)S(1)} collective-permute-done((bf16[16,1024]{1,0:T(8,128)(2,1)S(1)}, bf16[16,1024]{1,0:T(8,128)(2,1)S(1)}, u32[]{:S(2)}, u32[]{:S(2)}) %collective-permute-start.12) | collective-permute-done | bytes 32800 | tf_op jit(solution)/shard_map/ppermute | solution.py:51
  128.2 4.9 %collective-permute-done.13 = bf16[16,1024]{1,0:T(8,128)(2,1)S(1)} collective-permute-done((bf16[16,1024]{1,0:T(8,128)(2,1)S(1)}, bf16[16,1024]{1,0:T(8,128)(2,1)S(1)}, u32[]{:S(2)}, u32[]{:S(2)}) %collective-permute-start.13) | collective-permute-done | bytes 32800 | tf_op jit(solution)/shard_map/ppermute | solution.py:51
  133.0 2.3 %collective-permute-done.14 = bf16[16,1024]{1,0:T(8,128)(2,1)S(1)} collective-permute-done((bf16[16,1024]{1,0:T(8,128)(2,1)S(1)}, bf16[16,1024]{1,0:T(8,128)(2,1)S(1)}, u32[]{:S(2)}, u32[]{:S(2)}) %collective-permute-start.14) | collective-permute-done | bytes 32800 | tf_op jit(solution)/shard_map/ppermute | solution.py:51
  135.4 5.6 %collective-permute-start.19 = (bf16[128,512]{1,0:T(8,128)(2,1)S(1)}, bf16[128,512]{1,0:T(8,128)(2,1)S(1)}, u32[]{:S(2)}, u32[]{:S(2)}) collective-permute-start(bf16[128,512]{1,0:T(8,128)(2,1)S(1)} %get-tuple-element.8), channel_id=1, source_target_pairs={{0,3},{1,4},{2,5},{3,6},{4,7},{5,0},{6,1},{7,2},{8,11},{9,12},{10,... | collective-permute-start | bytes 393224 | tf_op jit(solution)/shard_map/ppermute | solution.py:61
  141.3 1.3 collective-permute-start.20
  142.9 2.0 collective-permute-done.19
  144.9 1.5 collective-permute-done.20
  146.4 4.8 %collective-permute-done.21 = bf16[128,512]{1,0:T(8,128)(2,1)S(1)} collective-permute-done((bf16[128,512]{1,0:T(8,128)(2,1)S(1)}, bf16[128,512]{1,0:T(8,128)(2,1)S(1)}, u32[]{:S(2)}, u32[]{:S(2)}) %collective-permute-start.21) | collective-permute-done | bytes 131104 | tf_op jit(solution)/shard_map/ppermute | solution.py:61
  151.9 4.3 %slice_multiply_fusion.1 = (f32[8,128,512]{2,1,0:T(8,128)S(1)}, f32[8,128,512]{2,1,0:T(8,128)S(1)}, f32[8,128,512]{2,1,0:T(8,128)S(1)}) fusion(f32[8,384,512]{2,1,0:T(8,128)} %all-to-all-done), kind=kLoop, calls=%fused_computation.7 | loop fusion | flops 1048576 | bytes 12582912 | tf_op jit(solution)/shard_map/mul | solution.py:18
  156.2 3.3 %bitcast_subtract_fusion = (f32[1024,512]{1,0:T(8,128)S(1)}, f32[1024,512]{1,0:T(8,128)}, f32[1024,512]{1,0:T(8,128)}) fusion(f32[8,128,512]{2,1,0:T(8,128)S(1)} %get-tuple-element.17, f32[1024,512]{1,0:T(8,128)S(1)} %copy-done.1, f32[8,128,512]{2,1,0:T(8,128)S(1)} %get-tuple-element.16, f32[8,128,512]{2,1,0:T(8,128)S(1)} %get-tuple-element.15), kind=kLoop, calls=%fused_computation.9 | loop fusion | flops 4718592 | bytes 14680064 | tf_op jit(solution)/shard_map/sub | solution.py:21
  159.5 0.4 fusion.1
  160.0 0.8 copy-done
  160.8 23.1 %all_to_all.23 = f32[16,16,1024]{2,1,0:T(8,128)S(1)} all-to-all(f32[16,16,1024]{2,1,0:T(8,128)S(1)} %bitcast.108), channel_id=1, replica_groups=mesh['fsdp'=16,'tp'=8] {'fsdp'}, dimensions={0} | all-to-all | bytes 2097152 | tf_op jit(solution)/shard_map/all_to_all | solution.py:30
  184.0 0.6 fusion.7
  184.6 11.1 %all_to_all.24 = bf16[16,16,512]{2,1,0:T(8,128)(2,1)S(1)} all-to-all(bf16[16,16,512]{2,1,0:T(8,128)(2,1)S(1)} %broadcast_in_dim.2), channel_id=1, replica_groups=mesh['fsdp'=16,'tp'=8] {'fsdp'}, dimensions={0} | all-to-all | bytes 524288 | tf_op jit(solution)/shard_map/all_to_all | solution.py:26
  195.7 0.7 copy.74
  (90 shorter events, 1.6 us)
Async XLA Ops:
  0.6 11.9 %copy-start.5 = (bf16[16,16384]{1,0:T(8,128)(2,1)S(1)}, bf16[16,16384]{1,0:T(8,128)(2,1)}, u32[]{:S(2)}) copy-start(bf16[16,16384]{1,0:T(8,128)(2,1)} %param.9) | copy-start | bytes 1572868
  0.6 14.1 %copy-start.2 = (f32[128,4096]{1,0:T(8,128)S(1)}, f32[128,4096]{1,0:T(8,128)}, u32[]{:S(2)}) copy-start(f32[128,4096]{1,0:T(8,128)} %param.10) | copy-start | bytes 6291460
  3.0 138.3 %collective-permute-start.15 = (bf16[128,512]{1,0:T(8,128)(2,1)S(1)}, bf16[128,512]{1,0:T(8,128)(2,1)S(1)}, u32[]{:S(2)}, u32[]{:S(2)}) collective-permute-start(bf16[128,512]{1,0:T(8,128)(2,1)S(1)} %get-tuple-element.8), channel_id=1, source_target_pairs={{0,7},{1,0},{2,1},{3,2},{4,3},{5,4},{6,5},{7,6},{8,15},{9,8},{10,9... | collective-permute-start | bytes 393224 | tf_op jit(solution)/shard_map/ppermute | solution.py:61
  9.6 133.0 %collective-permute-start.16 = (bf16[128,512]{1,0:T(8,128)(2,1)S(1)}, bf16[128,512]{1,0:T(8,128)(2,1)S(1)}, u32[]{:S(2)}, u32[]{:S(2)}) collective-permute-start(bf16[128,512]{1,0:T(8,128)(2,1)S(1)} %get-tuple-element.8), channel_id=1, source_target_pairs={{0,6},{1,7},{2,0},{3,1},{4,2},{5,3},{6,4},{7,5},{8,14},{9,15},{10,... | collective-permute-start | bytes 393224 | tf_op jit(solution)/shard_map/ppermute | solution.py:61
  10.1 132.7 %collective-permute-start.17 = (bf16[128,512]{1,0:T(8,128)(2,1)S(1)}, bf16[128,512]{1,0:T(8,128)(2,1)S(1)}, u32[]{:S(2)}, u32[]{:S(2)}) collective-permute-start(bf16[128,512]{1,0:T(8,128)(2,1)S(1)} %get-tuple-element.8), channel_id=1, source_target_pairs={{0,5},{1,6},{2,7},{3,0},{4,1},{5,2},{6,3},{7,4},{8,13},{9,14},{10,... | collective-permute-start | bytes 393224 | tf_op jit(solution)/shard_map/ppermute | solution.py:61
  10.1 132.8 %collective-permute-start.18 = (bf16[128,512]{1,0:T(8,128)(2,1)S(1)}, bf16[128,512]{1,0:T(8,128)(2,1)S(1)}, u32[]{:S(2)}, u32[]{:S(2)}) collective-permute-start(bf16[128,512]{1,0:T(8,128)(2,1)S(1)} %get-tuple-element.8), channel_id=1, source_target_pairs={{0,4},{1,5},{2,6},{3,7},{4,0},{5,1},{6,2},{7,3},{8,12},{9,13},{10,... | collective-permute-start | bytes 393224 | tf_op jit(solution)/shard_map/ppermute | solution.py:61
  13.2 13.3 %collective-permute-start = (bf16[16,1024]{1,0:T(8,128)(2,1)}, bf16[16,1024]{1,0:T(8,128)(2,1)S(1)}, u32[]{:S(2)}, u32[]{:S(2)}) collective-permute-start(bf16[16,1024]{1,0:T(8,128)(2,1)} %get-tuple-element.32), channel_id=1, source_target_pairs={{0,120},{8,0},{16,8},{24,16},{32,24},{40,32},{48,40},{56,48},{64,5... | collective-permute-start | bytes 98312 | tf_op jit(solution)/shard_map/ppermute | solution.py:51
  14.8 1.6 copy-start.3
  14.8 2.2 %copy-start.4 = (f32[128,4096]{1,0:T(8,128)S(1)}, f32[128,4096]{1,0:T(8,128)}, u32[]{:S(2)}) copy-start(f32[128,4096]{1,0:T(8,128)} %param.11) | copy-start | bytes 6291460
  21.0 5.6 %copy-start.12 = (bf16[16,1024]{1,0:T(8,128)(2,1)S(1)}, bf16[16,1024]{1,0:T(8,128)(2,1)}, u32[]{:S(2)}) copy-start(bf16[16,1024]{1,0:T(8,128)(2,1)} %get-tuple-element.31) | copy-start | bytes 98308
  21.0 9.9 %copy-start.11 = (bf16[16,1024]{1,0:T(8,128)(2,1)S(1)}, bf16[16,1024]{1,0:T(8,128)(2,1)}, u32[]{:S(2)}) copy-start(bf16[16,1024]{1,0:T(8,128)(2,1)} %get-tuple-element.30) | copy-start | bytes 98308
  21.0 18.0 %copy-start.10 = (bf16[16,1024]{1,0:T(8,128)(2,1)S(1)}, bf16[16,1024]{1,0:T(8,128)(2,1)}, u32[]{:S(2)}) copy-start(bf16[16,1024]{1,0:T(8,128)(2,1)} %get-tuple-element.29) | copy-start | bytes 98308
  21.0 22.7 %copy-start.9 = (bf16[16,1024]{1,0:T(8,128)(2,1)S(1)}, bf16[16,1024]{1,0:T(8,128)(2,1)}, u32[]{:S(2)}) copy-start(bf16[16,1024]{1,0:T(8,128)(2,1)} %get-tuple-element.28) | copy-start | bytes 98308
  21.0 34.6 %copy-start.8 = (bf16[16,1024]{1,0:T(8,128)(2,1)S(1)}, bf16[16,1024]{1,0:T(8,128)(2,1)}, u32[]{:S(2)}) copy-start(bf16[16,1024]{1,0:T(8,128)(2,1)} %get-tuple-element.27) | copy-start | bytes 98308
  21.0 38.9 %copy-start.7 = (bf16[16,1024]{1,0:T(8,128)(2,1)S(1)}, bf16[16,1024]{1,0:T(8,128)(2,1)}, u32[]{:S(2)}) copy-start(bf16[16,1024]{1,0:T(8,128)(2,1)} %get-tuple-element.26) | copy-start | bytes 98308
  21.0 58.8 %copy-start.6 = (bf16[16,1024]{1,0:T(8,128)(2,1)S(1)}, bf16[16,1024]{1,0:T(8,128)(2,1)}, u32[]{:S(2)}) copy-start(bf16[16,1024]{1,0:T(8,128)(2,1)} %get-tuple-element.25) | copy-start | bytes 98308
  21.0 130.9 %all-to-all-start = ((f32[8,384,512]{2,1,0:T(8,128)}), f32[8,384,512]{2,1,0:T(8,128)}, u32[]{:S(2)}, u32[]{:S(2)}) async-start(f32[8,384,512]{2,1,0:T(8,128)} %pad_maximum_fusion), calls=%async_computation | async-start | bytes 12582912 | tf_op jit(solution)/shard_map/all_to_all | solution.py:69
  26.6 4.3 %collective-permute-start.1 = (bf16[16,1024]{1,0:T(8,128)(2,1)S(1)}, bf16[16,1024]{1,0:T(8,128)(2,1)S(1)}, u32[]{:S(2)}, u32[]{:S(2)}) collective-permute-start(bf16[16,1024]{1,0:T(8,128)(2,1)S(1)} %copy-done.12), channel_id=1, source_target_pairs={{0,112},{8,120},{16,0},{24,8},{32,16},{40,24},{48,32},{56,40},{64,... | collective-permute-start | bytes 98312 | tf_op jit(solution)/shard_map/ppermute | solution.py:51
  30.9 8.1 %collective-permute-start.2 = (bf16[16,1024]{1,0:T(8,128)(2,1)S(1)}, bf16[16,1024]{1,0:T(8,128)(2,1)S(1)}, u32[]{:S(2)}, u32[]{:S(2)}) collective-permute-start(bf16[16,1024]{1,0:T(8,128)(2,1)S(1)} %copy-done.11), channel_id=1, source_target_pairs={{0,104},{8,112},{16,120},{24,0},{32,8},{40,16},{48,24},{56,32},{64... | collective-permute-start | bytes 98312 | tf_op jit(solution)/shard_map/ppermute | solution.py:51
  39.0 4.7 %collective-permute-start.3 = (bf16[16,1024]{1,0:T(8,128)(2,1)S(1)}, bf16[16,1024]{1,0:T(8,128)(2,1)S(1)}, u32[]{:S(2)}, u32[]{:S(2)}) collective-permute-start(bf16[16,1024]{1,0:T(8,128)(2,1)S(1)} %copy-done.10), channel_id=1, source_target_pairs={{0,96},{8,104},{16,112},{24,120},{32,0},{40,8},{48,16},{56,24},{64... | collective-permute-start | bytes 98312 | tf_op jit(solution)/shard_map/ppermute | solution.py:51
  43.7 11.9 %collective-permute-start.4 = (bf16[16,1024]{1,0:T(8,128)(2,1)S(1)}, bf16[16,1024]{1,0:T(8,128)(2,1)S(1)}, u32[]{:S(2)}, u32[]{:S(2)}) collective-permute-start(bf16[16,1024]{1,0:T(8,128)(2,1)S(1)} %copy-done.9), channel_id=1, source_target_pairs={{0,88},{8,96},{16,104},{24,112},{32,120},{40,0},{48,8},{56,16},{64... | collective-permute-start | bytes 98312 | tf_op jit(solution)/shard_map/ppermute | solution.py:51
  55.5 4.4 %collective-permute-start.5 = (bf16[16,1024]{1,0:T(8,128)(2,1)S(1)}, bf16[16,1024]{1,0:T(8,128)(2,1)S(1)}, u32[]{:S(2)}, u32[]{:S(2)}) collective-permute-start(bf16[16,1024]{1,0:T(8,128)(2,1)S(1)} %copy-done.8), channel_id=1, source_target_pairs={{0,80},{8,88},{16,96},{24,104},{32,112},{40,120},{48,0},{56,8},{64... | collective-permute-start | bytes 98312 | tf_op jit(solution)/shard_map/ppermute | solution.py:51
  59.9 19.8 %collective-permute-start.6 = (bf16[16,1024]{1,0:T(8,128)(2,1)S(1)}, bf16[16,1024]{1,0:T(8,128)(2,1)S(1)}, u32[]{:S(2)}, u32[]{:S(2)}) collective-permute-start(bf16[16,1024]{1,0:T(8,128)(2,1)S(1)} %copy-done.7), channel_id=1, source_target_pairs={{0,72},{8,80},{16,88},{24,96},{32,104},{40,112},{48,120},{56,0},{6... | collective-permute-start | bytes 98312 | tf_op jit(solution)/shard_map/ppermute | solution.py:51
  79.8 17.5 %collective-permute-start.7 = (bf16[16,1024]{1,0:T(8,128)(2,1)S(1)}, bf16[16,1024]{1,0:T(8,128)(2,1)S(1)}, u32[]{:S(2)}, u32[]{:S(2)}) collective-permute-start(bf16[16,1024]{1,0:T(8,128)(2,1)S(1)} %copy-done.6), channel_id=1, source_target_pairs={{0,64},{8,72},{16,80},{24,88},{32,96},{40,104},{48,112},{56,120},{... | collective-permute-start | bytes 98312 | tf_op jit(solution)/shard_map/ppermute | solution.py:51
  97.3 6.3 %collective-permute-start.8 = (bf16[16,1024]{1,0:T(8,128)(2,1)S(1)}, bf16[16,1024]{1,0:T(8,128)(2,1)S(1)}, u32[]{:S(2)}, u32[]{:S(2)}) collective-permute-start(bf16[16,1024]{1,0:T(8,128)(2,1)S(1)} %get-tuple-element.24), channel_id=1, source_target_pairs={{0,56},{8,64},{16,72},{24,80},{32,88},{40,96},{48,104},{56,112},{6... | collective-permute-start | bytes 98312 | tf_op jit(solution)/shard_map/ppermute | solution.py:51
  103.6 7.5 %collective-permute-start.9 = (bf16[16,1024]{1,0:T(8,128)(2,1)S(1)}, bf16[16,1024]{1,0:T(8,128)(2,1)S(1)}, u32[]{:S(2)}, u32[]{:S(2)}) collective-permute-start(bf16[16,1024]{1,0:T(8,128)(2,1)S(1)} %get-tuple-element.23), channel_id=1, source_target_pairs={{0,48},{8,56},{16,64},{24,72},{32,80},{40,88},{48,96},{56,104},{64... | collective-permute-start | bytes 98312 | tf_op jit(solution)/shard_map/ppermute | solution.py:51
  111.1 5.7 %collective-permute-start.10 = (bf16[16,1024]{1,0:T(8,128)(2,1)S(1)}, bf16[16,1024]{1,0:T(8,128)(2,1)S(1)}, u32[]{:S(2)}, u32[]{:S(2)}) collective-permute-start(bf16[16,1024]{1,0:T(8,128)(2,1)S(1)} %get-tuple-element.22), channel_id=1, source_target_pairs={{0,40},{8,48},{16,56},{24,64},{32,72},{40,80},{48,88},{56,96},{64,... | collective-permute-start | bytes 98312 | tf_op jit(solution)/shard_map/ppermute | solution.py:51
  116.9 5.4 %collective-permute-start.11 = (bf16[16,1024]{1,0:T(8,128)(2,1)S(1)}, bf16[16,1024]{1,0:T(8,128)(2,1)S(1)}, u32[]{:S(2)}, u32[]{:S(2)}) collective-permute-start(bf16[16,1024]{1,0:T(8,128)(2,1)S(1)} %get-tuple-element.21), channel_id=1, source_target_pairs={{0,32},{8,40},{16,48},{24,56},{32,64},{40,72},{48,80},{56,88},{64,... | collective-permute-start | bytes 98312 | tf_op jit(solution)/shard_map/ppermute | solution.py:51
  122.3 5.9 %collective-permute-start.12 = (bf16[16,1024]{1,0:T(8,128)(2,1)S(1)}, bf16[16,1024]{1,0:T(8,128)(2,1)S(1)}, u32[]{:S(2)}, u32[]{:S(2)}) collective-permute-start(bf16[16,1024]{1,0:T(8,128)(2,1)S(1)} %get-tuple-element.20), channel_id=1, source_target_pairs={{0,24},{8,32},{16,40},{24,48},{32,56},{40,64},{48,72},{56,80},{64,... | collective-permute-start | bytes 98312 | tf_op jit(solution)/shard_map/ppermute | solution.py:51
  128.2 4.9 %collective-permute-start.13 = (bf16[16,1024]{1,0:T(8,128)(2,1)S(1)}, bf16[16,1024]{1,0:T(8,128)(2,1)S(1)}, u32[]{:S(2)}, u32[]{:S(2)}) collective-permute-start(bf16[16,1024]{1,0:T(8,128)(2,1)S(1)} %get-tuple-element.19), channel_id=1, source_target_pairs={{0,16},{8,24},{16,32},{24,40},{32,48},{40,56},{48,64},{56,72},{64,... | collective-permute-start | bytes 98312 | tf_op jit(solution)/shard_map/ppermute | solution.py:51
  133.0 2.3 %collective-permute-start.14 = (bf16[16,1024]{1,0:T(8,128)(2,1)S(1)}, bf16[16,1024]{1,0:T(8,128)(2,1)S(1)}, u32[]{:S(2)}, u32[]{:S(2)}) collective-permute-start(bf16[16,1024]{1,0:T(8,128)(2,1)S(1)} %get-tuple-element.18), channel_id=1, source_target_pairs={{0,8},{8,16},{16,24},{24,32},{32,40},{40,48},{48,56},{56,64},{64,7... | collective-permute-start | bytes 98312 | tf_op jit(solution)/shard_map/ppermute | solution.py:51
  135.4 9.5 %collective-permute-start.19 = (bf16[128,512]{1,0:T(8,128)(2,1)S(1)}, bf16[128,512]{1,0:T(8,128)(2,1)S(1)}, u32[]{:S(2)}, u32[]{:S(2)}) collective-permute-start(bf16[128,512]{1,0:T(8,128)(2,1)S(1)} %get-tuple-element.8), channel_id=1, source_target_pairs={{0,3},{1,4},{2,5},{3,6},{4,7},{5,0},{6,1},{7,2},{8,11},{9,12},{10,... | collective-permute-start | bytes 393224 | tf_op jit(solution)/shard_map/ppermute | solution.py:61
  141.3 5.1 %collective-permute-start.20 = (bf16[128,512]{1,0:T(8,128)(2,1)S(1)}, bf16[128,512]{1,0:T(8,128)(2,1)S(1)}, u32[]{:S(2)}, u32[]{:S(2)}) collective-permute-start(bf16[128,512]{1,0:T(8,128)(2,1)S(1)} %get-tuple-element.8), channel_id=1, source_target_pairs={{0,2},{1,3},{2,4},{3,5},{4,6},{5,7},{6,0},{7,1},{8,10},{9,11},{10,... | collective-permute-start | bytes 393224 | tf_op jit(solution)/shard_map/ppermute | solution.py:61
  142.6 8.6 %collective-permute-start.21 = (bf16[128,512]{1,0:T(8,128)(2,1)S(1)}, bf16[128,512]{1,0:T(8,128)(2,1)S(1)}, u32[]{:S(2)}, u32[]{:S(2)}) collective-permute-start(bf16[128,512]{1,0:T(8,128)(2,1)S(1)} %get-tuple-element.8), channel_id=1, source_target_pairs={{0,1},{1,2},{2,3},{3,4},{4,5},{5,6},{6,7},{7,0},{8,9},{9,10},{10,1... | collective-permute-start | bytes 393224 | tf_op jit(solution)/shard_map/ppermute | solution.py:61
  151.9 4.3 %copy-start.1 = (f32[1024,512]{1,0:T(8,128)S(1)}, f32[1024,512]{1,0:T(8,128)}, u32[]{:S(2)}) copy-start(f32[1024,512]{1,0:T(8,128)} %param.13) | copy-start | bytes 6291460
  159.5 1.3 copy-start

commit v6 on v5

--- a/solution.py
+++ b/solution.py
@@ -63,6 +63,8 @@
     wkv_rows = lax.dynamic_slice_in_dim(jnp.concatenate([rows_kv, rows_kv]), tp - 1 - me_tp, tp, 0)
     wkv_rows = wkv_rows.reshape(tp * wkv_low.shape[0], wkv_low.shape[1])
     kv_term = jnp.dot(columns, wkv_rows, preferred_element_type=jnp.float32)
+    kv_sums = scatter_sum_rows(kv_term, "fsdp", fsdp)
+    probe_keyvalue = gather_rows(kv_sums.astype(jnp.bfloat16), "fsdp", fsdp)
 
     rows, cols = wq_master.shape
     pieces = [x.reshape(rows, tp, cols // tp).transpose(1, 0, 2) for x in (wq_master, wq_first, wq_second)]
@@ -71,10 +73,7 @@
     wq_new, wq_mom, wq_var = adam_step(master, first, second, wq_grad)
     q_term = jnp.dot(columns, wq_new.astype(jnp.bfloat16), preferred_element_type=jnp.float32)
 
-    sums = scatter_sum_rows(jnp.concatenate([q_term, kv_term], axis=1), "fsdp", fsdp)
-    q_cols = q_term.shape[1]
-    probe_query = sums[:, :q_cols].astype(jnp.bfloat16)
-    probe_keyvalue = gather_rows(sums[:, q_cols:].astype(jnp.bfloat16), "fsdp", fsdp)
+    probe_query = scatter_sum_rows(q_term, "fsdp", fsdp).astype(jnp.bfloat16)
     return (wq_new, wq_mom, wq_var, wkv_new, wkv_mom, wkv_var, probe_query, probe_keyvalue)
 
 

time: 197 us -> 243 us (1.23)
  waiting for transfers between devices: 88.3 us -> 143 us
  blocking collectives: 34.3 us -> 0 us
  starting transfers between devices: 52.5 us -> 72.3 us
  local copies, waits for them, and re-layouts: 6.12 us -> 8.9 us
    all_to_all x1, waiting for transfers between devices: 0.01 us -> 86.7 us  [step(): lax.all_to_all(jnp.concatenate(pieces, axis=1), 'tp', split_axis=0, conca...]
    ppermute x15, waiting for transfers between devices: 80 us -> 35.7 us  [step(): lax.ppermute(block, 'fsdp', [(i, (i + k) % fsdp) for i in range(fsdp)])]
    all_to_all x2 -> x0, blocking collectives: 34.3 us -> none  [the longest x1 23.1 us: scatter_sum_rows(): lax.all_to_all(x, axis_name, split_axis=0, concat_axis=0, tiled=True)]
    all_to_all x0 -> x3, starting transfers between devices: none -> 19.2 us  [the longest x2 13.9 us: scatter_sum_rows(): lax.all_to_all(x, axis_name, split_axis=0, concat_axis=0, tiled=True)]
    all_to_all x0 -> x3, waiting for transfers between devices: none -> 12.9 us  [the longest x2 12.9 us: scatter_sum_rows(): lax.all_to_all(x, axis_name, split_axis=0, concat_axis=0, tiled=True)]
    ppermute x15, starting transfers between devices: 30.2 us -> 35.4 us  [step(): lax.ppermute(block, 'fsdp', [(i, (i + k) % fsdp) for i in range(fsdp)])]
    ppermute x7, starting transfers between devices: 16.7 us -> 12.9 us  [step(): lax.ppermute(wkv_low, 'tp', [(i, (i + k) % tp) for i in range(tp)])]
  transfers between devices with their start and end apart: 23 -> 26, of which waited for: 17 -> 20; matrix products, arithmetic and copies ran while one was open for 3% -> 9% of each run, Pallas kernels for 0% -> 0%
where the time goes in v6:
time: 243 us; the launch traced here: 242 us
  waiting for transfers between devices  143 us (59%)
  starting transfers between devices  72.3 us (30%)
  other arithmetic  13.9 us (6%)
  local copies, waits for them, and re-layouts  8.9 us (4%)
  matrix products  2.71 us (1%)
    all_to_all x1, waiting for transfers between devices, step(): lax.all_to_all(jnp.concatenate(pieces, axis=1), 'tp', split_axis=0, conca...  86.7 us
    ppermute x15, waiting for transfers between devices, step(): lax.ppermute(block, 'fsdp', [(i, (i + k) % fsdp) for i in range(fsdp)])  35.7 us
    ppermute x15, starting transfers between devices, step(): lax.ppermute(block, 'fsdp', [(i, (i + k) % fsdp) for i in range(fsdp)])  35.4 us
    all_to_all x2, starting transfers between devices, scatter_sum_rows(): lax.all_to_all(x, axis_name, split_axis=0, concat_axis=0, tiled=True)  13.9 us
    ppermute x7, starting transfers between devices, step(): lax.ppermute(wkv_low, 'tp', [(i, (i + k) % tp) for i in range(tp)])  12.9 us
    all_to_all x2, waiting for transfers between devices, scatter_sum_rows(): lax.all_to_all(x, axis_name, split_axis=0, concat_axis=0, tiled=True)  12.9 us
    ppermute x7, waiting for transfers between devices, step(): lax.ppermute(wkv_low, 'tp', [(i, (i + k) % tp) for i in range(tp)])  8.09 us
    all_to_all x1, starting transfers between devices, gather_rows(): lax.all_to_all(copies, axis_name, split_axis=0, concat_axis=0, tiled=True)  5.27 us
  transfers between devices with their start and end apart: 26, of which 20 were waited for; matrix products, arithmetic and copies ran while one was open for 9% of the time, Pallas kernels for 0%

profile of v6, /device:TPU:1, one launch (start us, length us, event | category | flops | bytes accessed | tf_op | source)
XLA Modules:
  0.0 242.4 jit_solution(16942355029050362270)
XLA Ops:
  0.8 1.1 constant_dynamic-slice_fusion.1
  1.9 1.5 collective-permute-start
  3.4 2.2 fusion.10
  5.5 5.9 %collective-permute-start.15 = (bf16[128,512]{1,0:T(8,128)(2,1)S(1)}, bf16[128,512]{1,0:T(8,128)(2,1)S(1)}, u32[]{:S(2)}, u32[]{:S(2)}) collective-permute-start(bf16[128,512]{1,0:T(8,128)(2,1)S(1)} %get-tuple-element.8), channel_id=1, source_target_pairs={{0,7},{1,0},{2,1},{3,2},{4,3},{5,4},{6,5},{7,6},{8,15},{9,8},{10,9... | collective-permute-start | bytes 393224 | tf_op jit(solution)/shard_map/ppermute | solution.py:61
  12.0 2.4 collective-permute-start.18
  14.4 1.8 copy.26
  16.3 3.5 %collective-permute-start.1 = (bf16[16,1024]{1,0:T(8,128)(2,1)S(1)}, bf16[16,1024]{1,0:T(8,128)(2,1)S(1)}, u32[]{:S(2)}, u32[]{:S(2)}) collective-permute-start(bf16[16,1024]{1,0:T(8,128)(2,1)S(1)} %get-tuple-element.31), channel_id=1, source_target_pairs={{0,112},{8,120},{16,0},{24,8},{32,16},{40,24},{48,32},{56,40},{64,... | collective-permute-start | bytes 98312 | tf_op jit(solution)/shard_map/ppermute | solution.py:51
  19.8 1.0 collective-permute-done.1
  20.8 6.2 %collective-permute-start.2 = (bf16[16,1024]{1,0:T(8,128)(2,1)S(1)}, bf16[16,1024]{1,0:T(8,128)(2,1)S(1)}, u32[]{:S(2)}, u32[]{:S(2)}) collective-permute-start(bf16[16,1024]{1,0:T(8,128)(2,1)S(1)} %get-tuple-element.30), channel_id=1, source_target_pairs={{0,104},{8,112},{16,120},{24,0},{32,8},{40,16},{48,24},{56,32},{64... | collective-permute-start | bytes 98312 | tf_op jit(solution)/shard_map/ppermute | solution.py:51
  27.0 1.0 collective-permute-done.2
  28.0 1.9 collective-permute-start.3
  30.0 2.3 collective-permute-done.3
  32.3 2.3 collective-permute-start.4
  34.6 4.8 %collective-permute-done.4 = bf16[16,1024]{1,0:T(8,128)(2,1)S(1)} collective-permute-done((bf16[16,1024]{1,0:T(8,128)(2,1)S(1)}, bf16[16,1024]{1,0:T(8,128)(2,1)S(1)}, u32[]{:S(2)}, u32[]{:S(2)}) %collective-permute-start.4) | collective-permute-done | bytes 32800 | tf_op jit(solution)/shard_map/ppermute | solution.py:51
  40.3 3.1 %collective-permute-done.5 = bf16[16,1024]{1,0:T(8,128)(2,1)S(1)} collective-permute-done((bf16[16,1024]{1,0:T(8,128)(2,1)S(1)}, bf16[16,1024]{1,0:T(8,128)(2,1)S(1)}, u32[]{:S(2)}, u32[]{:S(2)}) %collective-permute-start.5) | collective-permute-done | bytes 32800 | tf_op jit(solution)/shard_map/ppermute | solution.py:51
  43.3 1.5 collective-permute-start.6
  44.9 4.0 %collective-permute-done.6 = bf16[16,1024]{1,0:T(8,128)(2,1)S(1)} collective-permute-done((bf16[16,1024]{1,0:T(8,128)(2,1)S(1)}, bf16[16,1024]{1,0:T(8,128)(2,1)S(1)}, u32[]{:S(2)}, u32[]{:S(2)}) %collective-permute-start.6) | collective-permute-done | bytes 32800 | tf_op jit(solution)/shard_map/ppermute | solution.py:51
  49.0 2.6 %collective-permute-done.7 = bf16[16,1024]{1,0:T(8,128)(2,1)S(1)} collective-permute-done((bf16[16,1024]{1,0:T(8,128)(2,1)S(1)}, bf16[16,1024]{1,0:T(8,128)(2,1)S(1)}, u32[]{:S(2)}, u32[]{:S(2)}) %collective-permute-start.7) | collective-permute-done | bytes 32800 | tf_op jit(solution)/shard_map/ppermute | solution.py:51
  51.6 4.1 %collective-permute-start.8 = (bf16[16,1024]{1,0:T(8,128)(2,1)S(1)}, bf16[16,1024]{1,0:T(8,128)(2,1)S(1)}, u32[]{:S(2)}, u32[]{:S(2)}) collective-permute-start(bf16[16,1024]{1,0:T(8,128)(2,1)S(1)} %get-tuple-element.24), channel_id=1, source_target_pairs={{0,56},{8,64},{16,72},{24,80},{32,88},{40,96},{48,104},{56,112},{6... | collective-permute-start | bytes 98312 | tf_op jit(solution)/shard_map/ppermute | solution.py:51
  55.7 1.0 collective-permute-done.8
  56.7 2.3 collective-permute-start.9
  59.0 1.3 collective-permute-done.9
  60.4 4.8 %collective-permute-start.10 = (bf16[16,1024]{1,0:T(8,128)(2,1)S(1)}, bf16[16,1024]{1,0:T(8,128)(2,1)S(1)}, u32[]{:S(2)}, u32[]{:S(2)}) collective-permute-start(bf16[16,1024]{1,0:T(8,128)(2,1)S(1)} %get-tuple-element.22), channel_id=1, source_target_pairs={{0,40},{8,48},{16,56},{24,64},{32,72},{40,80},{48,88},{56,96},{64,... | collective-permute-start | bytes 98312 | tf_op jit(solution)/shard_map/ppermute | solution.py:51
  65.2 1.1 collective-permute-done.10
  66.2 2.8 %collective-permute-start.11 = (bf16[16,1024]{1,0:T(8,128)(2,1)S(1)}, bf16[16,1024]{1,0:T(8,128)(2,1)S(1)}, u32[]{:S(2)}, u32[]{:S(2)}) collective-permute-start(bf16[16,1024]{1,0:T(8,128)(2,1)S(1)} %get-tuple-element.21), channel_id=1, source_target_pairs={{0,32},{8,40},{16,48},{24,56},{32,64},{40,72},{48,80},{56,88},{64,... | collective-permute-start | bytes 98312 | tf_op jit(solution)/shard_map/ppermute | solution.py:51
  69.1 2.4 collective-permute-done.11
  71.4 2.8 %collective-permute-start.12 = (bf16[16,1024]{1,0:T(8,128)(2,1)S(1)}, bf16[16,1024]{1,0:T(8,128)(2,1)S(1)}, u32[]{:S(2)}, u32[]{:S(2)}) collective-permute-start(bf16[16,1024]{1,0:T(8,128)(2,1)S(1)} %get-tuple-element.20), channel_id=1, source_target_pairs={{0,24},{8,32},{16,40},{24,48},{32,56},{40,64},{48,72},{56,80},{64,... | collective-permute-start | bytes 98312 | tf_op jit(solution)/shard_map/ppermute | solution.py:51
  74.3 3.5 %collective-permute-done.12 = bf16[16,1024]{1,0:T(8,128)(2,1)S(1)} collective-permute-done((bf16[16,1024]{1,0:T(8,128)(2,1)S(1)}, bf16[16,1024]{1,0:T(8,128)(2,1)S(1)}, u32[]{:S(2)}, u32[]{:S(2)}) %collective-permute-start.12) | collective-permute-done | bytes 32800 | tf_op jit(solution)/shard_map/ppermute | solution.py:51
  77.8 4.9 %collective-permute-done.13 = bf16[16,1024]{1,0:T(8,128)(2,1)S(1)} collective-permute-done((bf16[16,1024]{1,0:T(8,128)(2,1)S(1)}, bf16[16,1024]{1,0:T(8,128)(2,1)S(1)}, u32[]{:S(2)}, u32[]{:S(2)}) %collective-permute-start.13) | collective-permute-done | bytes 32800 | tf_op jit(solution)/shard_map/ppermute | solution.py:51
  83.2 2.8 %collective-permute-done.14 = bf16[16,1024]{1,0:T(8,128)(2,1)S(1)} collective-permute-done((bf16[16,1024]{1,0:T(8,128)(2,1)S(1)}, bf16[16,1024]{1,0:T(8,128)(2,1)S(1)}, u32[]{:S(2)}, u32[]{:S(2)}) %collective-permute-start.14) | collective-permute-done | bytes 32800 | tf_op jit(solution)/shard_map/ppermute | solution.py:51
  86.0 1.5 collective-permute-start.19
  89.2 1.6 collective-permute-start.20
  91.8 2.2 collective-permute-done.19
  94.0 1.6 collective-permute-done.20
  95.6 4.3 %collective-permute-done.21 = bf16[128,512]{1,0:T(8,128)(2,1)S(1)} collective-permute-done((bf16[128,512]{1,0:T(8,128)(2,1)S(1)}, bf16[128,512]{1,0:T(8,128)(2,1)S(1)}, u32[]{:S(2)}, u32[]{:S(2)}) %collective-permute-start.21) | collective-permute-done | bytes 131104 | tf_op jit(solution)/shard_map/ppermute | solution.py:61
  100.2 1.2 fusion.4
  101.4 8.2 %all-to-all-start.2 = ((f32[16,16,512]{2,1,0:T(8,128)}), f32[16,16,512]{2,1,0:T(8,128)S(1)}, u32[]{:S(2)}, u32[]{:S(2)}) async-start(f32[16,16,512]{2,1,0:T(8,128)} %fusion.4), calls=%async_computation.2 | async-start | bytes 1048576 | tf_op jit(solution)/shard_map/all_to_all | solution.py:30
  109.7 2.7 %bitcast_bitcast_fusion = (f32[8,128,512]{2,1,0:T(8,128)S(1)}, f32[8,128,512]{2,1,0:T(8,128)S(1)}) fusion(f32[16,8,8,512]{3,2,1,0:T(8,128)} %bitcast.108, f32[16,8,8,512]{3,2,1,0:T(8,128)} %bitcast.109), kind=kLoop, calls=%fused_computation.3 | loop fusion | bytes 8388608 | tf_op jit(solution)/shard_map/transpose | solution.py:70
  112.3 3.5 %pad_maximum_fusion = f32[8,384,512]{2,1,0:T(8,128)} fusion(f32[8,128,512]{2,1,0:T(8,128)S(1)} %get-tuple-element.33, f32[8,128,512]{2,1,0:T(8,128)S(1)} %get-tuple-element.34, f32[8,128,512]{2,1,0:T(8,128)S(1)} %bitcast.105), kind=kLoop, calls=%fused_computation | loop fusion | flops 3145728 | bytes 12582912 | tf_op jit(solution)/shard_map/concatenate | solution.py:71
  115.8 3.4 %all-to-all-done.2 = f32[16,16,512]{2,1,0:T(8,128)S(1)} async-done(((f32[16,16,512]{2,1,0:T(8,128)}), f32[16,16,512]{2,1,0:T(8,128)S(1)}, u32[]{:S(2)}, u32[]{:S(2)}) %all-to-all-start.2) | async-done | bytes 524320 | tf_op jit(solution)/shard_map/all_to_all | solution.py:30
  119.3 4.8 %all-to-all-start = ((f32[8,384,512]{2,1,0:T(8,128)}), f32[8,384,512]{2,1,0:T(8,128)}, u32[]{:S(2)}, u32[]{:S(2)}) async-start(f32[8,384,512]{2,1,0:T(8,128)} %pad_maximum_fusion), calls=%async_computation | async-start | bytes 12582912 | tf_op jit(solution)/shard_map/all_to_all | solution.py:71
  124.1 86.7 %all-to-all-done = f32[8,384,512]{2,1,0:T(8,128)} async-done(((f32[8,384,512]{2,1,0:T(8,128)}), f32[8,384,512]{2,1,0:T(8,128)}, u32[]{:S(2)}, u32[]{:S(2)}) %all-to-all-start) | async-done | bytes 6291488 | tf_op jit(solution)/shard_map/all_to_all | solution.py:71
  211.5 5.3 %all-to-all-start.3 = ((bf16[16,16,512]{2,1,0:T(8,128)(2,1)}), bf16[16,16,512]{2,1,0:T(8,128)(2,1)S(1)}, u32[]{:S(2)}, u32[]{:S(2)}) async-start(bf16[16,16,512]{2,1,0:T(8,128)(2,1)} %broadcast_in_dim.2), calls=%async_computation.3 | async-start | bytes 524288 | tf_op jit(solution)/shard_map/all_to_all | solution.py:26
  216.8 4.3 %slice_multiply_fusion.1 = (f32[8,128,512]{2,1,0:T(8,128)S(1)}, f32[8,128,512]{2,1,0:T(8,128)S(1)}, f32[8,128,512]{2,1,0:T(8,128)S(1)}) fusion(f32[8,384,512]{2,1,0:T(8,128)} %all-to-all-done), kind=kLoop, calls=%fused_computation.7 | loop fusion | flops 1048576 | bytes 12582912 | tf_op jit(solution)/shard_map/mul | solution.py:18
  221.1 3.3 %bitcast_subtract_fusion = (f32[1024,512]{1,0:T(8,128)S(1)}, f32[1024,512]{1,0:T(8,128)}, f32[1024,512]{1,0:T(8,128)}) fusion(f32[8,128,512]{2,1,0:T(8,128)S(1)} %get-tuple-element.17, f32[1024,512]{1,0:T(8,128)S(1)} %copy-done.1, f32[8,128,512]{2,1,0:T(8,128)S(1)} %get-tuple-element.16, f32[8,128,512]{2,1,0:T(8,128)S(1)} %get-tuple-element.15), kind=kLoop, calls=%fused_computation.9 | loop fusion | flops 4718592 | bytes 14680064 | tf_op jit(solution)/shard_map/sub | solution.py:21
  224.4 1.5 fusion.1
  225.9 5.7 %all-to-all-start.1 = ((f32[16,16,512]{2,1,0:T(8,128)}), f32[16,16,512]{2,1,0:T(8,128)S(1)}, u32[]{:S(2)}, u32[]{:S(2)}) async-start(f32[16,16,512]{2,1,0:T(8,128)} %fusion.1), calls=%async_computation.1 | async-start | bytes 1048576 | tf_op jit(solution)/shard_map/all_to_all | solution.py:30
  231.6 9.5 %all-to-all-done.1 = f32[16,16,512]{2,1,0:T(8,128)S(1)} async-done(((f32[16,16,512]{2,1,0:T(8,128)}), f32[16,16,512]{2,1,0:T(8,128)S(1)}, u32[]{:S(2)}, u32[]{:S(2)}) %all-to-all-start.1) | async-done | bytes 524320 | tf_op jit(solution)/shard_map/all_to_all | solution.py:30
  (74 shorter events, 7.1 us)
Async XLA Ops:
  1.9 14.3 %collective-permute-start = (bf16[16,1024]{1,0:T(8,128)(2,1)S(1)}, bf16[16,1024]{1,0:T(8,128)(2,1)S(1)}, u32[]{:S(2)}, u32[]{:S(2)}) collective-permute-start(bf16[16,1024]{1,0:T(8,128)(2,1)S(1)} %get-tuple-element.32), channel_id=1, source_target_pairs={{0,120},{8,0},{16,8},{24,16},{32,24},{40,32},{48,40},{56,48},{64,5... | collective-permute-start | bytes 98312 | tf_op jit(solution)/shard_map/ppermute | solution.py:51
  5.5 83.6 %collective-permute-start.15 = (bf16[128,512]{1,0:T(8,128)(2,1)S(1)}, bf16[128,512]{1,0:T(8,128)(2,1)S(1)}, u32[]{:S(2)}, u32[]{:S(2)}) collective-permute-start(bf16[128,512]{1,0:T(8,128)(2,1)S(1)} %get-tuple-element.8), channel_id=1, source_target_pairs={{0,7},{1,0},{2,1},{3,2},{4,3},{5,4},{6,5},{7,6},{8,15},{9,8},{10,9... | collective-permute-start | bytes 393224 | tf_op jit(solution)/shard_map/ppermute | solution.py:61
  11.4 79.4 %collective-permute-start.16 = (bf16[128,512]{1,0:T(8,128)(2,1)S(1)}, bf16[128,512]{1,0:T(8,128)(2,1)S(1)}, u32[]{:S(2)}, u32[]{:S(2)}) collective-permute-start(bf16[128,512]{1,0:T(8,128)(2,1)S(1)} %get-tuple-element.8), channel_id=1, source_target_pairs={{0,6},{1,7},{2,0},{3,1},{4,2},{5,3},{6,4},{7,5},{8,14},{9,15},{10,... | collective-permute-start | bytes 393224 | tf_op jit(solution)/shard_map/ppermute | solution.py:61
  12.0 79.8 %collective-permute-start.17 = (bf16[128,512]{1,0:T(8,128)(2,1)S(1)}, bf16[128,512]{1,0:T(8,128)(2,1)S(1)}, u32[]{:S(2)}, u32[]{:S(2)}) collective-permute-start(bf16[128,512]{1,0:T(8,128)(2,1)S(1)} %get-tuple-element.8), channel_id=1, source_target_pairs={{0,5},{1,6},{2,7},{3,0},{4,1},{5,2},{6,3},{7,4},{8,13},{9,14},{10,... | collective-permute-start | bytes 393224 | tf_op jit(solution)/shard_map/ppermute | solution.py:61
  12.0 79.8 %collective-permute-start.18 = (bf16[128,512]{1,0:T(8,128)(2,1)S(1)}, bf16[128,512]{1,0:T(8,128)(2,1)S(1)}, u32[]{:S(2)}, u32[]{:S(2)}) collective-permute-start(bf16[128,512]{1,0:T(8,128)(2,1)S(1)} %get-tuple-element.8), channel_id=1, source_target_pairs={{0,4},{1,5},{2,6},{3,7},{4,0},{5,1},{6,2},{7,3},{8,12},{9,13},{10,... | collective-permute-start | bytes 393224 | tf_op jit(solution)/shard_map/ppermute | solution.py:61
  16.3 4.6 %collective-permute-start.1 = (bf16[16,1024]{1,0:T(8,128)(2,1)S(1)}, bf16[16,1024]{1,0:T(8,128)(2,1)S(1)}, u32[]{:S(2)}, u32[]{:S(2)}) collective-permute-start(bf16[16,1024]{1,0:T(8,128)(2,1)S(1)} %get-tuple-element.31), channel_id=1, source_target_pairs={{0,112},{8,120},{16,0},{24,8},{32,16},{40,24},{48,32},{56,40},{64,... | collective-permute-start | bytes 98312 | tf_op jit(solution)/shard_map/ppermute | solution.py:51
  20.8 7.2 %collective-permute-start.2 = (bf16[16,1024]{1,0:T(8,128)(2,1)S(1)}, bf16[16,1024]{1,0:T(8,128)(2,1)S(1)}, u32[]{:S(2)}, u32[]{:S(2)}) collective-permute-start(bf16[16,1024]{1,0:T(8,128)(2,1)S(1)} %get-tuple-element.30), channel_id=1, source_target_pairs={{0,104},{8,112},{16,120},{24,0},{32,8},{40,16},{48,24},{56,32},{64... | collective-permute-start | bytes 98312 | tf_op jit(solution)/shard_map/ppermute | solution.py:51
  28.0 4.3 %collective-permute-start.3 = (bf16[16,1024]{1,0:T(8,128)(2,1)S(1)}, bf16[16,1024]{1,0:T(8,128)(2,1)S(1)}, u32[]{:S(2)}, u32[]{:S(2)}) collective-permute-start(bf16[16,1024]{1,0:T(8,128)(2,1)S(1)} %get-tuple-element.29), channel_id=1, source_target_pairs={{0,96},{8,104},{16,112},{24,120},{32,0},{40,8},{48,16},{56,24},{64... | collective-permute-start | bytes 98312 | tf_op jit(solution)/shard_map/ppermute | solution.py:51
  32.3 7.1 %collective-permute-start.4 = (bf16[16,1024]{1,0:T(8,128)(2,1)S(1)}, bf16[16,1024]{1,0:T(8,128)(2,1)S(1)}, u32[]{:S(2)}, u32[]{:S(2)}) collective-permute-start(bf16[16,1024]{1,0:T(8,128)(2,1)S(1)} %get-tuple-element.28), channel_id=1, source_target_pairs={{0,88},{8,96},{16,104},{24,112},{32,120},{40,0},{48,8},{56,16},{64... | collective-permute-start | bytes 98312 | tf_op jit(solution)/shard_map/ppermute | solution.py:51
  39.4 4.0 %collective-permute-start.5 = (bf16[16,1024]{1,0:T(8,128)(2,1)S(1)}, bf16[16,1024]{1,0:T(8,128)(2,1)S(1)}, u32[]{:S(2)}, u32[]{:S(2)}) collective-permute-start(bf16[16,1024]{1,0:T(8,128)(2,1)S(1)} %get-tuple-element.27), channel_id=1, source_target_pairs={{0,80},{8,88},{16,96},{24,104},{32,112},{40,120},{48,0},{56,8},{64... | collective-permute-start | bytes 98312 | tf_op jit(solution)/shard_map/ppermute | solution.py:51
  43.3 5.5 %collective-permute-start.6 = (bf16[16,1024]{1,0:T(8,128)(2,1)S(1)}, bf16[16,1024]{1,0:T(8,128)(2,1)S(1)}, u32[]{:S(2)}, u32[]{:S(2)}) collective-permute-start(bf16[16,1024]{1,0:T(8,128)(2,1)S(1)} %get-tuple-element.26), channel_id=1, source_target_pairs={{0,72},{8,80},{16,88},{24,96},{32,104},{40,112},{48,120},{56,0},{6... | collective-permute-start | bytes 98312 | tf_op jit(solution)/shard_map/ppermute | solution.py:51
  48.8 2.8 %collective-permute-start.7 = (bf16[16,1024]{1,0:T(8,128)(2,1)S(1)}, bf16[16,1024]{1,0:T(8,128)(2,1)S(1)}, u32[]{:S(2)}, u32[]{:S(2)}) collective-permute-start(bf16[16,1024]{1,0:T(8,128)(2,1)S(1)} %get-tuple-element.25), channel_id=1, source_target_pairs={{0,64},{8,72},{16,80},{24,88},{32,96},{40,104},{48,112},{56,120},{... | collective-permute-start | bytes 98312 | tf_op jit(solution)/shard_map/ppermute | solution.py:51
  51.6 5.1 %collective-permute-start.8 = (bf16[16,1024]{1,0:T(8,128)(2,1)S(1)}, bf16[16,1024]{1,0:T(8,128)(2,1)S(1)}, u32[]{:S(2)}, u32[]{:S(2)}) collective-permute-start(bf16[16,1024]{1,0:T(8,128)(2,1)S(1)} %get-tuple-element.24), channel_id=1, source_target_pairs={{0,56},{8,64},{16,72},{24,80},{32,88},{40,96},{48,104},{56,112},{6... | collective-permute-start | bytes 98312 | tf_op jit(solution)/shard_map/ppermute | solution.py:51
  56.7 3.7 %collective-permute-start.9 = (bf16[16,1024]{1,0:T(8,128)(2,1)S(1)}, bf16[16,1024]{1,0:T(8,128)(2,1)S(1)}, u32[]{:S(2)}, u32[]{:S(2)}) collective-permute-start(bf16[16,1024]{1,0:T(8,128)(2,1)S(1)} %get-tuple-element.23), channel_id=1, source_target_pairs={{0,48},{8,56},{16,64},{24,72},{32,80},{40,88},{48,96},{56,104},{64... | collective-permute-start | bytes 98312 | tf_op jit(solution)/shard_map/ppermute | solution.py:51
  60.4 5.9 %collective-permute-start.10 = (bf16[16,1024]{1,0:T(8,128)(2,1)S(1)}, bf16[16,1024]{1,0:T(8,128)(2,1)S(1)}, u32[]{:S(2)}, u32[]{:S(2)}) collective-permute-start(bf16[16,1024]{1,0:T(8,128)(2,1)S(1)} %get-tuple-element.22), channel_id=1, source_target_pairs={{0,40},{8,48},{16,56},{24,64},{32,72},{40,80},{48,88},{56,96},{64,... | collective-permute-start | bytes 98312 | tf_op jit(solution)/shard_map/ppermute | solution.py:51
  66.2 5.2 %collective-permute-start.11 = (bf16[16,1024]{1,0:T(8,128)(2,1)S(1)}, bf16[16,1024]{1,0:T(8,128)(2,1)S(1)}, u32[]{:S(2)}, u32[]{:S(2)}) collective-permute-start(bf16[16,1024]{1,0:T(8,128)(2,1)S(1)} %get-tuple-element.21), channel_id=1, source_target_pairs={{0,32},{8,40},{16,48},{24,56},{32,64},{40,72},{48,80},{56,88},{64,... | collective-permute-start | bytes 98312 | tf_op jit(solution)/shard_map/ppermute | solution.py:51
  71.4 6.4 %collective-permute-start.12 = (bf16[16,1024]{1,0:T(8,128)(2,1)S(1)}, bf16[16,1024]{1,0:T(8,128)(2,1)S(1)}, u32[]{:S(2)}, u32[]{:S(2)}) collective-permute-start(bf16[16,1024]{1,0:T(8,128)(2,1)S(1)} %get-tuple-element.20), channel_id=1, source_target_pairs={{0,24},{8,32},{16,40},{24,48},{32,56},{40,64},{48,72},{56,80},{64,... | collective-permute-start | bytes 98312 | tf_op jit(solution)/shard_map/ppermute | solution.py:51
  77.8 4.9 %collective-permute-start.13 = (bf16[16,1024]{1,0:T(8,128)(2,1)S(1)}, bf16[16,1024]{1,0:T(8,128)(2,1)S(1)}, u32[]{:S(2)}, u32[]{:S(2)}) collective-permute-start(bf16[16,1024]{1,0:T(8,128)(2,1)S(1)} %get-tuple-element.19), channel_id=1, source_target_pairs={{0,16},{8,24},{16,32},{24,40},{32,48},{40,56},{48,64},{56,72},{64,... | collective-permute-start | bytes 98312 | tf_op jit(solution)/shard_map/ppermute | solution.py:51
  82.6 3.3 %collective-permute-start.14 = (bf16[16,1024]{1,0:T(8,128)(2,1)S(1)}, bf16[16,1024]{1,0:T(8,128)(2,1)S(1)}, u32[]{:S(2)}, u32[]{:S(2)}) collective-permute-start(bf16[16,1024]{1,0:T(8,128)(2,1)S(1)} %get-tuple-element.18), channel_id=1, source_target_pairs={{0,8},{8,16},{16,24},{24,32},{32,40},{40,48},{48,56},{56,64},{64,7... | collective-permute-start | bytes 98312 | tf_op jit(solution)/shard_map/ppermute | solution.py:51
  86.0 8.1 %collective-permute-start.19 = (bf16[128,512]{1,0:T(8,128)(2,1)S(1)}, bf16[128,512]{1,0:T(8,128)(2,1)S(1)}, u32[]{:S(2)}, u32[]{:S(2)}) collective-permute-start(bf16[128,512]{1,0:T(8,128)(2,1)S(1)} %get-tuple-element.8), channel_id=1, source_target_pairs={{0,3},{1,4},{2,5},{3,6},{4,7},{5,0},{6,1},{7,2},{8,11},{9,12},{10,... | collective-permute-start | bytes 393224 | tf_op jit(solution)/shard_map/ppermute | solution.py:61
  89.1 11.1 %copy-start.2 = (bf16[32,16,1024]{2,1,0:T(8,128)(2,1)}, bf16[32,16,1024]{2,1,0:T(8,128)(2,1)S(1)}, u32[]{:S(2)}) copy-start(bf16[32,16,1024]{2,1,0:T(8,128)(2,1)S(1)} %constant_dynamic-update-slice_fusion) | copy-start | bytes 3145732
  89.2 6.5 %collective-permute-start.20 = (bf16[128,512]{1,0:T(8,128)(2,1)S(1)}, bf16[128,512]{1,0:T(8,128)(2,1)S(1)}, u32[]{:S(2)}, u32[]{:S(2)}) collective-permute-start(bf16[128,512]{1,0:T(8,128)(2,1)S(1)} %get-tuple-element.8), channel_id=1, source_target_pairs={{0,2},{1,3},{2,4},{3,5},{4,6},{5,7},{6,0},{7,1},{8,10},{9,11},{10,... | collective-permute-start | bytes 393224 | tf_op jit(solution)/shard_map/ppermute | solution.py:61
  90.8 9.1 %collective-permute-start.21 = (bf16[128,512]{1,0:T(8,128)(2,1)S(1)}, bf16[128,512]{1,0:T(8,128)(2,1)S(1)}, u32[]{:S(2)}, u32[]{:S(2)}) collective-permute-start(bf16[128,512]{1,0:T(8,128)(2,1)S(1)} %get-tuple-element.8), channel_id=1, source_target_pairs={{0,1},{1,2},{2,3},{3,4},{4,5},{5,6},{6,7},{7,0},{8,9},{9,10},{10,1... | collective-permute-start | bytes 393224 | tf_op jit(solution)/shard_map/ppermute | solution.py:61
  101.4 17.8 %all-to-all-start.2 = ((f32[16,16,512]{2,1,0:T(8,128)}), f32[16,16,512]{2,1,0:T(8,128)S(1)}, u32[]{:S(2)}, u32[]{:S(2)}) async-start(f32[16,16,512]{2,1,0:T(8,128)} %fusion.4), calls=%async_computation.2 | async-start | bytes 1048576 | tf_op jit(solution)/shard_map/all_to_all | solution.py:30
  119.3 91.6 %all-to-all-start = ((f32[8,384,512]{2,1,0:T(8,128)}), f32[8,384,512]{2,1,0:T(8,128)}, u32[]{:S(2)}, u32[]{:S(2)}) async-start(f32[8,384,512]{2,1,0:T(8,128)} %pad_maximum_fusion), calls=%async_computation | async-start | bytes 12582912 | tf_op jit(solution)/shard_map/all_to_all | solution.py:71
  211.5 14.3 %all-to-all-start.3 = ((bf16[16,16,512]{2,1,0:T(8,128)(2,1)}), bf16[16,16,512]{2,1,0:T(8,128)(2,1)S(1)}, u32[]{:S(2)}, u32[]{:S(2)}) async-start(bf16[16,16,512]{2,1,0:T(8,128)(2,1)} %broadcast_in_dim.2), calls=%async_computation.3 | async-start | bytes 524288 | tf_op jit(solution)/shard_map/all_to_all | solution.py:26
  216.8 4.3 %copy-start.1 = (f32[1024,512]{1,0:T(8,128)S(1)}, f32[1024,512]{1,0:T(8,128)}, u32[]{:S(2)}) copy-start(f32[1024,512]{1,0:T(8,128)} %param.13) | copy-start | bytes 6291460
  221.1 3.3 %copy-start.3 = (bf16[32,16,1024]{2,1,0:T(8,128)(2,1)S(1)}, bf16[32,16,1024]{2,1,0:T(8,128)(2,1)}, u32[]{:S(2)}) copy-start(bf16[32,16,1024]{2,1,0:T(8,128)(2,1)} %copy-done.2) | copy-start | bytes 3145732
  224.4 1.5 copy-start
  225.9 15.2 %all-to-all-start.1 = ((f32[16,16,512]{2,1,0:T(8,128)}), f32[16,16,512]{2,1,0:T(8,128)S(1)}, u32[]{:S(2)}, u32[]{:S(2)}) async-start(f32[16,16,512]{2,1,0:T(8,128)} %fusion.1), calls=%async_computation.1 | async-start | bytes 1048576 | tf_op jit(solution)/shard_map/all_to_all | solution.py:30

commit v7 on v5

--- a/solution.py
+++ b/solution.py
@@ -56,12 +56,14 @@
     tp = lax.axis_size("tp")
     me_tp = lax.axis_index("tp")
     wkv_low = wkv_new.astype(jnp.bfloat16)
-    rows_kv = [wkv_low]
+    slice_kv = wkv_low.shape[1] // tp
+    rows_kv = [lax.dynamic_slice_in_dim(wkv_low, me_tp * slice_kv, slice_kv, 1)]
     for k in range(1, tp):
-        rows_kv.append(lax.ppermute(wkv_low, "tp", [(i, (i + k) % tp) for i in range(tp)]))
+        block = lax.dynamic_slice_in_dim(wkv_low, ((me_tp + k) % tp) * slice_kv, slice_kv, 1)
+        rows_kv.append(lax.ppermute(block, "tp", [(i, (i + k) % tp) for i in range(tp)]))
     rows_kv = jnp.stack(rows_kv[::-1])
     wkv_rows = lax.dynamic_slice_in_dim(jnp.concatenate([rows_kv, rows_kv]), tp - 1 - me_tp, tp, 0)
-    wkv_rows = wkv_rows.reshape(tp * wkv_low.shape[0], wkv_low.shape[1])
+    wkv_rows = wkv_rows.reshape(tp * wkv_low.shape[0], slice_kv)
     kv_term = jnp.dot(columns, wkv_rows, preferred_element_type=jnp.float32)
 
     rows, cols = wq_master.shape
@@ -74,7 +76,11 @@
     sums = scatter_sum_rows(jnp.concatenate([q_term, kv_term], axis=1), "fsdp", fsdp)
     q_cols = q_term.shape[1]
     probe_query = sums[:, :q_cols].astype(jnp.bfloat16)
-    probe_keyvalue = gather_rows(sums[:, q_cols:].astype(jnp.bfloat16), "fsdp", fsdp)
+    kv_block = sums[:, q_cols:].astype(jnp.bfloat16)
+    kv_all = gather_rows(kv_block, ("fsdp", "tp"), fsdp * tp)
+    tokens = kv_block.shape[0]
+    kv_all = kv_all.reshape(fsdp, tp, tokens, slice_kv).transpose(0, 2, 1, 3)
+    probe_keyvalue = kv_all.reshape(fsdp * tokens, tp * slice_kv)
     return (wq_new, wq_mom, wq_var, wkv_new, wkv_mom, wkv_var, probe_query, probe_keyvalue)
 
 

time: 197 us -> 204 us (1.036)
  starting transfers between devices: 52.5 us -> 112 us
  waiting for transfers between devices: 88.3 us -> 54.8 us
  blocking collectives: 34.3 us -> 15.2 us
    ppermute x15, waiting for transfers between devices: 80 us -> 3.19 us  [step(): lax.ppermute(block, 'fsdp', [(i, (i + k) % fsdp) for i in range(fsdp)])]
    ppermute x7, starting transfers between devices: 16.7 us -> 65.1 us  [step(): lax.ppermute(block, 'tp', [(i, (i + k) % tp) for i in range(tp)])]
    ppermute x7, waiting for transfers between devices: 8.28 us -> 41.7 us  [step(): lax.ppermute(block, 'tp', [(i, (i + k) % tp) for i in range(tp)])]
    all_to_all x1 -> x0, blocking collectives: 11.1 us -> none  [gather_rows(): lax.all_to_all(copies, axis_name, split_axis=0, concat_axis=0, tiled=True)]
    all_to_all x0 -> x1, waiting for transfers between devices: none -> 9.97 us  [gather_rows(): lax.all_to_all(copies, axis_name, split_axis=0, concat_axis=0, tiled=True)]
    all_to_all x1, blocking collectives: 23.1 us -> 15.2 us  [scatter_sum_rows(): lax.all_to_all(x, axis_name, split_axis=0, concat_axis=0, tiled=True)]
    all_to_all x0 -> x1, starting transfers between devices: none -> 6.07 us  [gather_rows(): lax.all_to_all(copies, axis_name, split_axis=0, concat_axis=0, tiled=True)]
    all_to_all x1, starting transfers between devices: 5.54 us -> 8.29 us  [step(): lax.all_to_all(jnp.concatenate(pieces, axis=1), 'tp', split_axis=0, conca...]
  transfers between devices with their start and end apart: 23 -> 24, of which waited for: 17 -> 10; matrix products, arithmetic and copies ran while one was open for 3% -> 1% of each run, Pallas kernels for 0% -> 0%
where the time goes in v7:
time: 204 us
  starting transfers between devices  112 us (55%)
  waiting for transfers between devices  54.8 us (27%)
  blocking collectives  15.2 us (7%)
  other arithmetic  11.9 us (6%)
  local copies, waits for them, and re-layouts  8.01 us (4%)
    ppermute x7, starting transfers between devices, step(): lax.ppermute(block, 'tp', [(i, (i + k) % tp) for i in range(tp)])  65.1 us
    ppermute x7, waiting for transfers between devices, step(): lax.ppermute(block, 'tp', [(i, (i + k) % tp) for i in range(tp)])  41.7 us
    ppermute x15, starting transfers between devices, step(): lax.ppermute(block, 'fsdp', [(i, (i + k) % fsdp) for i in range(fsdp)])  32.1 us
    all_to_all x1, blocking collectives, scatter_sum_rows(): lax.all_to_all(x, axis_name, split_axis=0, concat_axis=0, tiled=True)  15.2 us
    all_to_all x1, waiting for transfers between devices, gather_rows(): lax.all_to_all(copies, axis_name, split_axis=0, concat_axis=0, tiled=True)  9.97 us
    all_to_all x1, starting transfers between devices, step(): lax.all_to_all(jnp.concatenate(pieces, axis=1), 'tp', split_axis=0, conca...  8.29 us
    all_to_all x1, starting transfers between devices, gather_rows(): lax.all_to_all(copies, axis_name, split_axis=0, concat_axis=0, tiled=True)  6.07 us
    mul x1, other arithmetic, adam_step(): first_new = BETA_ONE * first + (1.0 - BETA_ONE) * grad  4.27 us
  transfers between devices with their start and end apart: 24, of which 10 were waited for; matrix products, arithmetic and copies ran while one was open for 1% of the time, Pallas kernels for 0%

profile of v7, /device:TPU:1, one launch (start us, length us, event | category | flops | bytes accessed | tf_op | source)
XLA Modules:
  0.0 203.5 jit_solution(14239562907033108524)
XLA Ops:
  0.7 1.9 copy.37
  2.6 0.3 copy-done.2
  2.9 0.6 copy-done.3
  3.5 0.4 bitcast_bitcast_fusion
  3.9 3.3 %pad_maximum_fusion = f32[8,384,512]{2,1,0:T(8,128)} fusion(f32[8,128,512]{2,1,0:T(8,128)S(1)} %get-tuple-element.40, f32[8,128,512]{2,1,0:T(8,128)S(1)} %get-tuple-element.41, f32[8,128,512]{2,1,0:T(8,128)S(1)} %bitcast.108), kind=kLoop, calls=%fused_computation | loop fusion | flops 3145728 | bytes 12582912 | tf_op jit(solution)/shard_map/concatenate | solution.py:71
  7.3 8.3 %all-to-all-start = ((f32[8,384,512]{2,1,0:T(8,128)}), f32[8,384,512]{2,1,0:T(8,128)}, u32[]{:S(2)}, u32[]{:S(2)}) async-start(f32[8,384,512]{2,1,0:T(8,128)} %pad_maximum_fusion), calls=%async_computation | async-start | bytes 12582912 | tf_op jit(solution)/shard_map/all_to_all | solution.py:71
  15.7 1.0 fusion.4
  16.8 5.0 %collective-permute-start.15 = (bf16[128,64]{1,0:T(8,128)(2,1)S(1)}, bf16[128,64]{1,0:T(8,128)(2,1)S(1)}, u32[]{:S(2)}, u32[]{:S(2)}) collective-permute-start(bf16[128,64]{1,0:T(8,128)(2,1)S(1)} %get-tuple-element.39), channel_id=1, source_target_pairs={{0,7},{1,0},{2,1},{3,2},{4,3},{5,4},{6,5},{7,6},{8,15},{9,8},{10,9... | collective-permute-start | bytes 49160 | tf_op jit(solution)/shard_map/ppermute | solution.py:63
  21.9 1.6 collective-permute-start
  23.5 3.2 %collective-permute-start.1 = (bf16[16,1024]{1,0:T(8,128)(2,1)S(1)}, bf16[16,1024]{1,0:T(8,128)(2,1)S(1)}, u32[]{:S(2)}, u32[]{:S(2)}) collective-permute-start(bf16[16,1024]{1,0:T(8,128)(2,1)S(1)} %get-tuple-element.31), channel_id=1, source_target_pairs={{0,112},{8,120},{16,0},{24,8},{32,16},{40,24},{48,32},{56,40},{64,... | collective-permute-start | bytes 98312 | tf_op jit(solution)/shard_map/ppermute | solution.py:51
  26.7 0.7 collective-permute-start.2
  27.4 2.0 collective-permute-start.3
  29.4 29.0 %collective-permute-done.15 = bf16[128,64]{1,0:T(8,128)(2,1)S(1)} collective-permute-done((bf16[128,64]{1,0:T(8,128)(2,1)S(1)}, bf16[128,64]{1,0:T(8,128)(2,1)S(1)}, u32[]{:S(2)}, u32[]{:S(2)}) %collective-permute-start.15) | collective-permute-done | bytes 16416 | tf_op jit(solution)/shard_map/ppermute | solution.py:63
  58.4 42.3 %collective-permute-start.16 = (bf16[128,64]{1,0:T(8,128)(2,1)S(1)}, bf16[128,64]{1,0:T(8,128)(2,1)S(1)}, u32[]{:S(2)}, u32[]{:S(2)}) collective-permute-start(bf16[128,64]{1,0:T(8,128)(2,1)S(1)} %get-tuple-element.38), channel_id=1, source_target_pairs={{0,6},{1,7},{2,0},{3,1},{4,2},{5,3},{6,4},{7,5},{8,14},{9,15},{10,... | collective-permute-start | bytes 49160 | tf_op jit(solution)/shard_map/ppermute | solution.py:63
  100.7 2.7 %collective-permute-done.16 = bf16[128,64]{1,0:T(8,128)(2,1)S(1)} collective-permute-done((bf16[128,64]{1,0:T(8,128)(2,1)S(1)}, bf16[128,64]{1,0:T(8,128)(2,1)S(1)}, u32[]{:S(2)}, u32[]{:S(2)}) %collective-permute-start.16) | collective-permute-done | bytes 16416 | tf_op jit(solution)/shard_map/ppermute | solution.py:63
  103.4 4.1 %collective-permute-start.17 = (bf16[128,64]{1,0:T(8,128)(2,1)S(1)}, bf16[128,64]{1,0:T(8,128)(2,1)S(1)}, u32[]{:S(2)}, u32[]{:S(2)}) collective-permute-start(bf16[128,64]{1,0:T(8,128)(2,1)S(1)} %get-tuple-element.37), channel_id=1, source_target_pairs={{0,5},{1,6},{2,7},{3,0},{4,1},{5,2},{6,3},{7,4},{8,13},{9,14},{10,... | collective-permute-start | bytes 49160 | tf_op jit(solution)/shard_map/ppermute | solution.py:63
  107.5 1.1 collective-permute-done.17
  108.6 2.8 %collective-permute-start.18 = (bf16[128,64]{1,0:T(8,128)(2,1)S(1)}, bf16[128,64]{1,0:T(8,128)(2,1)S(1)}, u32[]{:S(2)}, u32[]{:S(2)}) collective-permute-start(bf16[128,64]{1,0:T(8,128)(2,1)S(1)} %get-tuple-element.36), channel_id=1, source_target_pairs={{0,4},{1,5},{2,6},{3,7},{4,0},{5,1},{6,2},{7,3},{8,12},{9,13},{10,... | collective-permute-start | bytes 49160 | tf_op jit(solution)/shard_map/ppermute | solution.py:63
  111.4 1.5 collective-permute-done.18
  112.9 5.2 %collective-permute-start.19 = (bf16[128,64]{1,0:T(8,128)(2,1)S(1)}, bf16[128,64]{1,0:T(8,128)(2,1)S(1)}, u32[]{:S(2)}, u32[]{:S(2)}) collective-permute-start(bf16[128,64]{1,0:T(8,128)(2,1)S(1)} %get-tuple-element.35), channel_id=1, source_target_pairs={{0,3},{1,4},{2,5},{3,6},{4,7},{5,0},{6,1},{7,2},{8,11},{9,12},{10,... | collective-permute-start | bytes 49160 | tf_op jit(solution)/shard_map/ppermute | solution.py:63
  118.1 1.8 collective-permute-done.19
  119.9 1.5 collective-permute-start.20
  121.4 3.4 %collective-permute-done.20 = bf16[128,64]{1,0:T(8,128)(2,1)S(1)} collective-permute-done((bf16[128,64]{1,0:T(8,128)(2,1)S(1)}, bf16[128,64]{1,0:T(8,128)(2,1)S(1)}, u32[]{:S(2)}, u32[]{:S(2)}) %collective-permute-start.20) | collective-permute-done | bytes 16416 | tf_op jit(solution)/shard_map/ppermute | solution.py:63
  124.8 4.1 %collective-permute-start.21 = (bf16[128,64]{1,0:T(8,128)(2,1)S(1)}, bf16[128,64]{1,0:T(8,128)(2,1)S(1)}, u32[]{:S(2)}, u32[]{:S(2)}) collective-permute-start(bf16[128,64]{1,0:T(8,128)(2,1)S(1)} %get-tuple-element.33), channel_id=1, source_target_pairs={{0,1},{1,2},{2,3},{3,4},{4,5},{5,6},{6,7},{7,0},{8,9},{9,10},{10,1... | collective-permute-start | bytes 49160 | tf_op jit(solution)/shard_map/ppermute | solution.py:63
  129.0 2.2 %collective-permute-done.21 = bf16[128,64]{1,0:T(8,128)(2,1)S(1)} collective-permute-done((bf16[128,64]{1,0:T(8,128)(2,1)S(1)}, bf16[128,64]{1,0:T(8,128)(2,1)S(1)}, u32[]{:S(2)}, u32[]{:S(2)}) %collective-permute-start.21) | collective-permute-done | bytes 16416 | tf_op jit(solution)/shard_map/ppermute | solution.py:63
  131.2 12.0 %collective-permute-start.4 = (bf16[16,1024]{1,0:T(8,128)(2,1)S(1)}, bf16[16,1024]{1,0:T(8,128)(2,1)S(1)}, u32[]{:S(2)}, u32[]{:S(2)}) collective-permute-start(bf16[16,1024]{1,0:T(8,128)(2,1)S(1)} %get-tuple-element.28), channel_id=1, source_target_pairs={{0,88},{8,96},{16,104},{24,112},{32,120},{40,0},{48,8},{56,16},{64... | collective-permute-start | bytes 98312 | tf_op jit(solution)/shard_map/ppermute | solution.py:51
  143.6 2.3 %collective-permute-start.5 = (bf16[16,1024]{1,0:T(8,128)(2,1)S(1)}, bf16[16,1024]{1,0:T(8,128)(2,1)S(1)}, u32[]{:S(2)}, u32[]{:S(2)}) collective-permute-start(bf16[16,1024]{1,0:T(8,128)(2,1)S(1)} %get-tuple-element.27), channel_id=1, source_target_pairs={{0,80},{8,88},{16,96},{24,104},{32,112},{40,120},{48,0},{56,8},{64... | collective-permute-start | bytes 98312 | tf_op jit(solution)/shard_map/ppermute | solution.py:51
  146.0 0.8 collective-permute-start.7
  146.8 1.9 collective-permute-start.8
  148.7 0.7 collective-permute-start.9
  149.4 1.4 collective-permute-start.10
  150.8 1.7 collective-permute-start.11
  152.5 2.1 %collective-permute-start.12 = (bf16[16,1024]{1,0:T(8,128)(2,1)S(1)}, bf16[16,1024]{1,0:T(8,128)(2,1)S(1)}, u32[]{:S(2)}, u32[]{:S(2)}) collective-permute-start(bf16[16,1024]{1,0:T(8,128)(2,1)S(1)} %get-tuple-element.20), channel_id=1, source_target_pairs={{0,24},{8,32},{16,40},{24,48},{32,56},{40,64},{48,72},{56,80},{64,... | collective-permute-start | bytes 98312 | tf_op jit(solution)/shard_map/ppermute | solution.py:51
  154.7 1.7 collective-permute-start.14
  156.3 2.0 collective-permute-done.12
  158.3 1.2 collective-permute-done.13
  159.8 0.3 fusion.7
  160.1 4.3 %slice_multiply_fusion.1 = (f32[8,128,512]{2,1,0:T(8,128)S(1)}, f32[8,128,512]{2,1,0:T(8,128)S(1)}, f32[8,128,512]{2,1,0:T(8,128)S(1)}) fusion(f32[8,384,512]{2,1,0:T(8,128)} %all-to-all-done), kind=kLoop, calls=%fused_computation.7 | loop fusion | flops 1048576 | bytes 12582912 | tf_op jit(solution)/shard_map/mul | solution.py:18
  164.4 3.3 %bitcast_subtract_fusion = (f32[1024,512]{1,0:T(8,128)S(1)}, f32[1024,512]{1,0:T(8,128)}, f32[1024,512]{1,0:T(8,128)}) fusion(f32[8,128,512]{2,1,0:T(8,128)S(1)} %get-tuple-element.17, f32[1024,512]{1,0:T(8,128)S(1)} %copy-done.1, f32[8,128,512]{2,1,0:T(8,128)S(1)} %get-tuple-element.16, f32[8,128,512]{2,1,0:T(8,128)S(1)} %get-tuple-element.15), kind=kLoop, calls=%fused_computation.9 | loop fusion | flops 4718592 | bytes 14680064 | tf_op jit(solution)/shard_map/sub | solution.py:21
  167.7 0.4 fusion.1
  168.2 0.8 copy-done
  169.0 15.2 %all_to_all.20 = f32[16,16,576]{2,1,0:T(8,128)S(1)} all-to-all(f32[16,16,576]{2,1,0:T(8,128)S(1)} %bitcast.111), channel_id=1, replica_groups=mesh['fsdp'=16,'tp'=8] {'fsdp'}, dimensions={0} | all-to-all | bytes 1179648 | tf_op jit(solution)/shard_map/all_to_all | solution.py:30
  184.4 1.0 reshape.64
  185.4 6.1 %all-to-all-start.2 = ((bf16[128,2,512]{2,1,0:T(2,128)(2,1)}), bf16[128,2,512]{2,1,0:T(2,128)(2,1)S(1)}, u32[]{:S(2)}, u32[]{:S(2)}) async-start(bf16[128,2,512]{2,1,0:T(2,128)(2,1)} %reshape.64), calls=%async_computation.2 | async-start | bytes 524288 | tf_op jit(solution)/shard_map/all_to_all | solution.py:26
  191.4 0.6 slice.25
  192.0 10.0 %all-to-all-done.2 = bf16[128,2,512]{2,1,0:T(2,128)(2,1)S(1)} async-done(((bf16[128,2,512]{2,1,0:T(2,128)(2,1)}), bf16[128,2,512]{2,1,0:T(2,128)(2,1)S(1)}, u32[]{:S(2)}, u32[]{:S(2)}) %all-to-all-start.2) | async-done | bytes 262176 | tf_op jit(solution)/shard_map/all_to_all | solution.py:26
  202.0 0.3 reshape.65
  202.5 1.0 reshape.63
  (88 shorter events, 1.1 us)
Async XLA Ops:
  0.6 2.2 %copy-start.2 = (f32[128,4096]{1,0:T(8,128)S(1)}, f32[128,4096]{1,0:T(8,128)}, u32[]{:S(2)}) copy-start(f32[128,4096]{1,0:T(8,128)} %param.12) | copy-start | bytes 6291460
  0.6 2.8 %copy-start.3 = (f32[128,4096]{1,0:T(8,128)S(1)}, f32[128,4096]{1,0:T(8,128)}, u32[]{:S(2)}) copy-start(f32[128,4096]{1,0:T(8,128)} %param.11) | copy-start | bytes 6291460
  7.3 8.4 %copy-start.5 = (f32[128,512]{1,0:T(8,128)S(1)}, f32[128,512]{1,0:T(8,128)}, u32[]{:S(2)}) copy-start(f32[128,512]{1,0:T(8,128)} %param.14) | copy-start | bytes 786436
  7.3 8.4 %copy-start.6 = (f32[128,512]{1,0:T(8,128)S(1)}, f32[128,512]{1,0:T(8,128)}, u32[]{:S(2)}) copy-start(f32[128,512]{1,0:T(8,128)} %param.17) | copy-start | bytes 786436
  7.3 8.4 %copy-start.7 = (f32[128,512]{1,0:T(8,128)S(1)}, f32[128,512]{1,0:T(8,128)}, u32[]{:S(2)}) copy-start(f32[128,512]{1,0:T(8,128)} %param.16) | copy-start | bytes 786436
  7.3 8.4 %copy-start.8 = (f32[128,512]{1,0:T(8,128)S(1)}, f32[128,512]{1,0:T(8,128)}, u32[]{:S(2)}) copy-start(f32[128,512]{1,0:T(8,128)} %param.15) | copy-start | bytes 786436
  7.3 152.8 %all-to-all-start = ((f32[8,384,512]{2,1,0:T(8,128)}), f32[8,384,512]{2,1,0:T(8,128)}, u32[]{:S(2)}, u32[]{:S(2)}) async-start(f32[8,384,512]{2,1,0:T(8,128)} %pad_maximum_fusion), calls=%async_computation | async-start | bytes 12582912 | tf_op jit(solution)/shard_map/all_to_all | solution.py:71
  15.6 6.3 %copy-start.4 = (bf16[16,16384]{1,0:T(8,128)(2,1)S(1)}, bf16[16,16384]{1,0:T(8,128)(2,1)}, u32[]{:S(2)}) copy-start(bf16[16,16384]{1,0:T(8,128)(2,1)} %param.9) | copy-start | bytes 1572868
  16.8 41.6 %collective-permute-start.15 = (bf16[128,64]{1,0:T(8,128)(2,1)S(1)}, bf16[128,64]{1,0:T(8,128)(2,1)S(1)}, u32[]{:S(2)}, u32[]{:S(2)}) collective-permute-start(bf16[128,64]{1,0:T(8,128)(2,1)S(1)} %get-tuple-element.39), channel_id=1, source_target_pairs={{0,7},{1,0},{2,1},{3,2},{4,3},{5,4},{6,5},{7,6},{8,15},{9,8},{10,9... | collective-permute-start | bytes 49160 | tf_op jit(solution)/shard_map/ppermute | solution.py:63
  21.9 121.7 %collective-permute-start = (bf16[16,1024]{1,0:T(8,128)(2,1)S(1)}, bf16[16,1024]{1,0:T(8,128)(2,1)S(1)}, u32[]{:S(2)}, u32[]{:S(2)}) collective-permute-start(bf16[16,1024]{1,0:T(8,128)(2,1)S(1)} %get-tuple-element.32), channel_id=1, source_target_pairs={{0,120},{8,0},{16,8},{24,16},{32,24},{40,32},{48,40},{56,48},{64,5... | collective-permute-start | bytes 98312 | tf_op jit(solution)/shard_map/ppermute | solution.py:51
  23.5 122.4 %collective-permute-start.1 = (bf16[16,1024]{1,0:T(8,128)(2,1)S(1)}, bf16[16,1024]{1,0:T(8,128)(2,1)S(1)}, u32[]{:S(2)}, u32[]{:S(2)}) collective-permute-start(bf16[16,1024]{1,0:T(8,128)(2,1)S(1)} %get-tuple-element.31), channel_id=1, source_target_pairs={{0,112},{8,120},{16,0},{24,8},{32,16},{40,24},{48,32},{56,40},{64,... | collective-permute-start | bytes 98312 | tf_op jit(solution)/shard_map/ppermute | solution.py:51
  26.7 119.3 %collective-permute-start.2 = (bf16[16,1024]{1,0:T(8,128)(2,1)S(1)}, bf16[16,1024]{1,0:T(8,128)(2,1)S(1)}, u32[]{:S(2)}, u32[]{:S(2)}) collective-permute-start(bf16[16,1024]{1,0:T(8,128)(2,1)S(1)} %get-tuple-element.30), channel_id=1, source_target_pairs={{0,104},{8,112},{16,120},{24,0},{32,8},{40,16},{48,24},{56,32},{64... | collective-permute-start | bytes 98312 | tf_op jit(solution)/shard_map/ppermute | solution.py:51
  27.4 119.4 %collective-permute-start.3 = (bf16[16,1024]{1,0:T(8,128)(2,1)S(1)}, bf16[16,1024]{1,0:T(8,128)(2,1)S(1)}, u32[]{:S(2)}, u32[]{:S(2)}) collective-permute-start(bf16[16,1024]{1,0:T(8,128)(2,1)S(1)} %get-tuple-element.29), channel_id=1, source_target_pairs={{0,96},{8,104},{16,112},{24,120},{32,0},{40,8},{48,16},{56,24},{64... | collective-permute-start | bytes 98312 | tf_op jit(solution)/shard_map/ppermute | solution.py:51
  58.4 45.0 %collective-permute-start.16 = (bf16[128,64]{1,0:T(8,128)(2,1)S(1)}, bf16[128,64]{1,0:T(8,128)(2,1)S(1)}, u32[]{:S(2)}, u32[]{:S(2)}) collective-permute-start(bf16[128,64]{1,0:T(8,128)(2,1)S(1)} %get-tuple-element.38), channel_id=1, source_target_pairs={{0,6},{1,7},{2,0},{3,1},{4,2},{5,3},{6,4},{7,5},{8,14},{9,15},{10,... | collective-permute-start | bytes 49160 | tf_op jit(solution)/shard_map/ppermute | solution.py:63
  103.4 5.2 %collective-permute-start.17 = (bf16[128,64]{1,0:T(8,128)(2,1)S(1)}, bf16[128,64]{1,0:T(8,128)(2,1)S(1)}, u32[]{:S(2)}, u32[]{:S(2)}) collective-permute-start(bf16[128,64]{1,0:T(8,128)(2,1)S(1)} %get-tuple-element.37), channel_id=1, source_target_pairs={{0,5},{1,6},{2,7},{3,0},{4,1},{5,2},{6,3},{7,4},{8,13},{9,14},{10,... | collective-permute-start | bytes 49160 | tf_op jit(solution)/shard_map/ppermute | solution.py:63
  108.6 4.3 %collective-permute-start.18 = (bf16[128,64]{1,0:T(8,128)(2,1)S(1)}, bf16[128,64]{1,0:T(8,128)(2,1)S(1)}, u32[]{:S(2)}, u32[]{:S(2)}) collective-permute-start(bf16[128,64]{1,0:T(8,128)(2,1)S(1)} %get-tuple-element.36), channel_id=1, source_target_pairs={{0,4},{1,5},{2,6},{3,7},{4,0},{5,1},{6,2},{7,3},{8,12},{9,13},{10,... | collective-permute-start | bytes 49160 | tf_op jit(solution)/shard_map/ppermute | solution.py:63
  112.9 7.0 %collective-permute-start.19 = (bf16[128,64]{1,0:T(8,128)(2,1)S(1)}, bf16[128,64]{1,0:T(8,128)(2,1)S(1)}, u32[]{:S(2)}, u32[]{:S(2)}) collective-permute-start(bf16[128,64]{1,0:T(8,128)(2,1)S(1)} %get-tuple-element.35), channel_id=1, source_target_pairs={{0,3},{1,4},{2,5},{3,6},{4,7},{5,0},{6,1},{7,2},{8,11},{9,12},{10,... | collective-permute-start | bytes 49160 | tf_op jit(solution)/shard_map/ppermute | solution.py:63
  119.9 4.9 %collective-permute-start.20 = (bf16[128,64]{1,0:T(8,128)(2,1)S(1)}, bf16[128,64]{1,0:T(8,128)(2,1)S(1)}, u32[]{:S(2)}, u32[]{:S(2)}) collective-permute-start(bf16[128,64]{1,0:T(8,128)(2,1)S(1)} %get-tuple-element.34), channel_id=1, source_target_pairs={{0,2},{1,3},{2,4},{3,5},{4,6},{5,7},{6,0},{7,1},{8,10},{9,11},{10,... | collective-permute-start | bytes 49160 | tf_op jit(solution)/shard_map/ppermute | solution.py:63
  124.8 6.4 %collective-permute-start.21 = (bf16[128,64]{1,0:T(8,128)(2,1)S(1)}, bf16[128,64]{1,0:T(8,128)(2,1)S(1)}, u32[]{:S(2)}, u32[]{:S(2)}) collective-permute-start(bf16[128,64]{1,0:T(8,128)(2,1)S(1)} %get-tuple-element.33), channel_id=1, source_target_pairs={{0,1},{1,2},{2,3},{3,4},{4,5},{5,6},{6,7},{7,0},{8,9},{9,10},{10,1... | collective-permute-start | bytes 49160 | tf_op jit(solution)/shard_map/ppermute | solution.py:63
  131.2 17.5 %collective-permute-start.4 = (bf16[16,1024]{1,0:T(8,128)(2,1)S(1)}, bf16[16,1024]{1,0:T(8,128)(2,1)S(1)}, u32[]{:S(2)}, u32[]{:S(2)}) collective-permute-start(bf16[16,1024]{1,0:T(8,128)(2,1)S(1)} %get-tuple-element.28), channel_id=1, source_target_pairs={{0,88},{8,96},{16,104},{24,112},{32,120},{40,0},{48,8},{56,16},{64... | collective-permute-start | bytes 98312 | tf_op jit(solution)/shard_map/ppermute | solution.py:51
  143.6 5.8 %collective-permute-start.5 = (bf16[16,1024]{1,0:T(8,128)(2,1)S(1)}, bf16[16,1024]{1,0:T(8,128)(2,1)S(1)}, u32[]{:S(2)}, u32[]{:S(2)}) collective-permute-start(bf16[16,1024]{1,0:T(8,128)(2,1)S(1)} %get-tuple-element.27), channel_id=1, source_target_pairs={{0,80},{8,88},{16,96},{24,104},{32,112},{40,120},{48,0},{56,8},{64... | collective-permute-start | bytes 98312 | tf_op jit(solution)/shard_map/ppermute | solution.py:51
  145.9 4.9 %collective-permute-start.6 = (bf16[16,1024]{1,0:T(8,128)(2,1)S(1)}, bf16[16,1024]{1,0:T(8,128)(2,1)S(1)}, u32[]{:S(2)}, u32[]{:S(2)}) collective-permute-start(bf16[16,1024]{1,0:T(8,128)(2,1)S(1)} %get-tuple-element.26), channel_id=1, source_target_pairs={{0,72},{8,80},{16,88},{24,96},{32,104},{40,112},{48,120},{56,0},{6... | collective-permute-start | bytes 98312 | tf_op jit(solution)/shard_map/ppermute | solution.py:51
  146.0 6.6 %collective-permute-start.7 = (bf16[16,1024]{1,0:T(8,128)(2,1)S(1)}, bf16[16,1024]{1,0:T(8,128)(2,1)S(1)}, u32[]{:S(2)}, u32[]{:S(2)}) collective-permute-start(bf16[16,1024]{1,0:T(8,128)(2,1)S(1)} %get-tuple-element.25), channel_id=1, source_target_pairs={{0,64},{8,72},{16,80},{24,88},{32,96},{40,104},{48,112},{56,120},{... | collective-permute-start | bytes 98312 | tf_op jit(solution)/shard_map/ppermute | solution.py:51
  146.8 7.8 %collective-permute-start.8 = (bf16[16,1024]{1,0:T(8,128)(2,1)S(1)}, bf16[16,1024]{1,0:T(8,128)(2,1)S(1)}, u32[]{:S(2)}, u32[]{:S(2)}) collective-permute-start(bf16[16,1024]{1,0:T(8,128)(2,1)S(1)} %get-tuple-element.24), channel_id=1, source_target_pairs={{0,56},{8,64},{16,72},{24,80},{32,88},{40,96},{48,104},{56,112},{6... | collective-permute-start | bytes 98312 | tf_op jit(solution)/shard_map/ppermute | solution.py:51
  148.7 5.9 %collective-permute-start.9 = (bf16[16,1024]{1,0:T(8,128)(2,1)S(1)}, bf16[16,1024]{1,0:T(8,128)(2,1)S(1)}, u32[]{:S(2)}, u32[]{:S(2)}) collective-permute-start(bf16[16,1024]{1,0:T(8,128)(2,1)S(1)} %get-tuple-element.23), channel_id=1, source_target_pairs={{0,48},{8,56},{16,64},{24,72},{32,80},{40,88},{48,96},{56,104},{64... | collective-permute-start | bytes 98312 | tf_op jit(solution)/shard_map/ppermute | solution.py:51
  149.4 6.9 %collective-permute-start.10 = (bf16[16,1024]{1,0:T(8,128)(2,1)S(1)}, bf16[16,1024]{1,0:T(8,128)(2,1)S(1)}, u32[]{:S(2)}, u32[]{:S(2)}) collective-permute-start(bf16[16,1024]{1,0:T(8,128)(2,1)S(1)} %get-tuple-element.22), channel_id=1, source_target_pairs={{0,40},{8,48},{16,56},{24,64},{32,72},{40,80},{48,88},{56,96},{64,... | collective-permute-start | bytes 98312 | tf_op jit(solution)/shard_map/ppermute | solution.py:51
  150.8 5.5 %collective-permute-start.11 = (bf16[16,1024]{1,0:T(8,128)(2,1)S(1)}, bf16[16,1024]{1,0:T(8,128)(2,1)S(1)}, u32[]{:S(2)}, u32[]{:S(2)}) collective-permute-start(bf16[16,1024]{1,0:T(8,128)(2,1)S(1)} %get-tuple-element.21), channel_id=1, source_target_pairs={{0,32},{8,40},{16,48},{24,56},{32,64},{40,72},{48,80},{56,88},{64,... | collective-permute-start | bytes 98312 | tf_op jit(solution)/shard_map/ppermute | solution.py:51
  152.5 5.8 %collective-permute-start.12 = (bf16[16,1024]{1,0:T(8,128)(2,1)S(1)}, bf16[16,1024]{1,0:T(8,128)(2,1)S(1)}, u32[]{:S(2)}, u32[]{:S(2)}) collective-permute-start(bf16[16,1024]{1,0:T(8,128)(2,1)S(1)} %get-tuple-element.20), channel_id=1, source_target_pairs={{0,24},{8,32},{16,40},{24,48},{32,56},{40,64},{48,72},{56,80},{64,... | collective-permute-start | bytes 98312 | tf_op jit(solution)/shard_map/ppermute | solution.py:51
  154.6 4.9 %collective-permute-start.13 = (bf16[16,1024]{1,0:T(8,128)(2,1)S(1)}, bf16[16,1024]{1,0:T(8,128)(2,1)S(1)}, u32[]{:S(2)}, u32[]{:S(2)}) collective-permute-start(bf16[16,1024]{1,0:T(8,128)(2,1)S(1)} %get-tuple-element.19), channel_id=1, source_target_pairs={{0,16},{8,24},{16,32},{24,40},{32,48},{40,56},{48,64},{56,72},{64,... | collective-permute-start | bytes 98312 | tf_op jit(solution)/shard_map/ppermute | solution.py:51
  154.7 4.8 %collective-permute-start.14 = (bf16[16,1024]{1,0:T(8,128)(2,1)S(1)}, bf16[16,1024]{1,0:T(8,128)(2,1)S(1)}, u32[]{:S(2)}, u32[]{:S(2)}) collective-permute-start(bf16[16,1024]{1,0:T(8,128)(2,1)S(1)} %get-tuple-element.18), channel_id=1, source_target_pairs={{0,8},{8,16},{16,24},{24,32},{32,40},{40,48},{48,56},{56,64},{64,7... | collective-permute-start | bytes 98312 | tf_op jit(solution)/shard_map/ppermute | solution.py:51
  160.1 4.3 %copy-start.1 = (f32[1024,512]{1,0:T(8,128)S(1)}, f32[1024,512]{1,0:T(8,128)}, u32[]{:S(2)}) copy-start(f32[1024,512]{1,0:T(8,128)} %param.13) | copy-start | bytes 6291460
  167.7 1.3 copy-start
  185.4 16.7 %all-to-all-start.2 = ((bf16[128,2,512]{2,1,0:T(2,128)(2,1)}), bf16[128,2,512]{2,1,0:T(2,128)(2,1)S(1)}, u32[]{:S(2)}, u32[]{:S(2)}) async-start(bf16[128,2,512]{2,1,0:T(2,128)(2,1)} %reshape.64), calls=%async_computation.2 | async-start | bytes 524288 | tf_op jit(solution)/shard_map/all_to_all | solution.py:26

commit v8 on v7

--- a/solution.py
+++ b/solution.py
@@ -3,6 +3,7 @@
 import jax
 import jax.numpy as jnp
 from jax import lax
+from jax.experimental import pallas as pl
 from jax.sharding import PartitionSpec as P
 
 
@@ -19,6 +20,57 @@
     second_new = BETA_TWO * second + (1.0 - BETA_TWO) * grad * grad
     update = first_new / CORRECT_ONE / (jnp.sqrt(second_new / CORRECT_TWO) + EPSILON)
     return (master - LEARN_RATE * update, first_new, second_new)
+
+
+def adam_kernel(state_ref, grad_ref, master_out, first_out, second_out, low_out):
+    per, rows = state_ref.shape[0], grad_ref.shape[0] // state_ref.shape[0]
+    for j in range(per):
+        out = pl.ds(j * rows, rows)
+        new, first_new, second_new = adam_step(
+            state_ref[j, pl.ds(0, rows), :],
+            state_ref[j, pl.ds(rows, rows), :],
+            state_ref[j, pl.ds(2 * rows, rows), :],
+            grad_ref[out, :],
+        )
+        master_out[out, :] = new
+        first_out[out, :] = first_new
+        second_out[out, :] = second_new
+        low_out[out, :] = new.astype(low_out.dtype)
+
+
+def adam_from_blocks(state, grad, per=2):
+    sources, stacked, cols = state.shape
+    rows = stacked // 3
+    block = pl.BlockSpec((per * rows, cols), lambda i: (i, 0))
+    f32 = jax.ShapeDtypeStruct(grad.shape, jnp.float32)
+    return pl.pallas_call(
+        adam_kernel,
+        grid=(sources // per,),
+        in_specs=[pl.BlockSpec((per, stacked, cols), lambda i: (i, 0, 0)), block],
+        out_specs=[block] * 4,
+        out_shape=[f32, f32, f32, jax.ShapeDtypeStruct(grad.shape, jnp.bfloat16)],
+    )(state, grad)
+
+
+def pack_kernel(master_ref, first_ref, second_ref, out_ref):
+    rows, width = master_ref.shape[0], out_ref.shape[2]
+    for j in range(out_ref.shape[0]):
+        cols = pl.ds(j * width, width)
+        for k, ref in enumerate((master_ref, first_ref, second_ref)):
+            out_ref[j, pl.ds(k * rows, rows), :] = ref[:, cols]
+
+
+def pack_by_destination(master, first, second, dests, per=2):
+    rows, cols = master.shape
+    width = cols // dests
+    block = pl.BlockSpec((rows, per * width), lambda i: (0, i))
+    return pl.pallas_call(
+        pack_kernel,
+        grid=(dests // per,),
+        in_specs=[block] * 3,
+        out_specs=pl.BlockSpec((per, 3 * rows, width), lambda i: (i, 0, 0)),
+        out_shape=jax.ShapeDtypeStruct((dests, 3 * rows, width), master.dtype),
+    )(master, first, second)
 
 
 def gather_rows(x, axis_name, size):
@@ -66,12 +118,10 @@
     wkv_rows = wkv_rows.reshape(tp * wkv_low.shape[0], slice_kv)
     kv_term = jnp.dot(columns, wkv_rows, preferred_element_type=jnp.float32)
 
-    rows, cols = wq_master.shape
-    pieces = [x.reshape(rows, tp, cols // tp).transpose(1, 0, 2) for x in (wq_master, wq_first, wq_second)]
-    state = lax.all_to_all(jnp.concatenate(pieces, axis=1), "tp", split_axis=0, concat_axis=0, tiled=True)
-    master, first, second = (state[:, k * rows:(k + 1) * rows].reshape(tp * rows, cols // tp) for k in range(3))
-    wq_new, wq_mom, wq_var = adam_step(master, first, second, wq_grad)
-    q_term = jnp.dot(columns, wq_new.astype(jnp.bfloat16), preferred_element_type=jnp.float32)
+    send = pack_by_destination(wq_master, wq_first, wq_second, tp)
+    state = lax.all_to_all(send, "tp", split_axis=0, concat_axis=0, tiled=True)
+    wq_new, wq_mom, wq_var, wq_low = adam_from_blocks(state, wq_grad)
+    q_term = jnp.dot(columns, wq_low, preferred_element_type=jnp.float32)
 
     sums = scatter_sum_rows(jnp.concatenate([q_term, kv_term], axis=1), "fsdp", fsdp)
     q_cols = q_term.shape[1]

time: 204 us -> 203 us (level)
  Pallas kernels: 0 us -> 12.8 us
  other arithmetic: 11.9 us -> 1.07 us
  local copies, waits for them, and re-layouts: 8.01 us -> 3.92 us
    pallas_call x0 -> x2, Pallas kernels: none -> 12.8 us  [the longest x1 6.88 us: adam_from_blocks(): pl.pallas_call(adam_kernel, grid=(sources // per,), in_specs=[pl.BlockSpe...]
    mul x1 -> x0, other arithmetic: 4.27 us -> none  [adam_step(): first_new = BETA_ONE * first + (1.0 - BETA_ONE) * grad]
    concatenate x1 -> x0, other arithmetic: 3.33 us -> none  [step(): jnp.concatenate(pieces, axis=1)]
    sub x1 -> x0, other arithmetic: 3.26 us -> none  [adam_step(): return (master - LEARN_RATE * update, first_new, second_new)]
where the time goes in v8:
time: 203 us
  starting transfers between devices  112 us (55%)
  waiting for transfers between devices  54.8 us (27%)
  blocking collectives  15.3 us (8%)
  Pallas kernels  12.8 us (6%)
  local copies, waits for them, and re-layouts  3.92 us (2%)
    ppermute x7, starting transfers between devices, step(): lax.ppermute(block, 'tp', [(i, (i + k) % tp) for i in range(tp)])  65.1 us
    ppermute x7, waiting for transfers between devices, step(): lax.ppermute(block, 'tp', [(i, (i + k) % tp) for i in range(tp)])  41.7 us
    ppermute x15, starting transfers between devices, step(): lax.ppermute(block, 'fsdp', [(i, (i + k) % fsdp) for i in range(fsdp)])  32.1 us
    all_to_all x1, blocking collectives, scatter_sum_rows(): lax.all_to_all(x, axis_name, split_axis=0, concat_axis=0, tiled=True)  15.3 us
    all_to_all x1, waiting for transfers between devices, gather_rows(): lax.all_to_all(copies, axis_name, split_axis=0, concat_axis=0, tiled=True)  9.97 us
    all_to_all x1, starting transfers between devices, step(): state = lax.all_to_all(send, 'tp', split_axis=0, concat_axis=0, tiled=True)  8.29 us
    pallas_call x1, Pallas kernels, adam_from_blocks(): pl.pallas_call(adam_kernel, grid=(sources // per,), in_specs=[pl.BlockSpe...  6.88 us
    all_to_all x1, starting transfers between devices, gather_rows(): lax.all_to_all(copies, axis_name, split_axis=0, concat_axis=0, tiled=True)  6.07 us
  transfers between devices with their start and end apart: 24, of which 10 were waited for; matrix products, arithmetic and copies ran while one was open for 1% of the time, Pallas kernels for 0%

profile of v8, /device:TPU:1, one launch (start us, length us, event | category | flops | bytes accessed | tf_op | source)
XLA Modules:
  0.0 202.5 jit_solution(16588315446108516811)
XLA Ops:
  0.6 5.9 %shard_map.152 = f32[8,384,512]{2,1,0:T(8,128)} custom-call(f32[128,4096]{1,0:T(8,128)} %master_ref.1, f32[128,4096]{1,0:T(8,128)} %first_ref.1, f32[128,4096]{1,0:T(8,128)} %second_ref.1), custom_call_target="tpu_custom_call" | custom-call | tf_op jit(solution)/shard_map/pallas_call | solution.py:67
  6.5 8.3 %all-to-all-start = ((f32[8,384,512]{2,1,0:T(8,128)}), f32[8,384,512]{2,1,0:T(8,128)}, u32[]{:S(2)}, u32[]{:S(2)}) async-start(f32[8,384,512]{2,1,0:T(8,128)} %shard_map.152), calls=%async_computation | async-start | bytes 12582912 | tf_op jit(solution)/shard_map/all_to_all | solution.py:122
  15.0 1.0 fusion.1
  15.9 0.1 constant_dynamic-slice_fusion.1
  16.1 5.0 %collective-permute-start.15 = (bf16[128,64]{1,0:T(8,128)(2,1)S(1)}, bf16[128,64]{1,0:T(8,128)(2,1)S(1)}, u32[]{:S(2)}, u32[]{:S(2)}) collective-permute-start(bf16[128,64]{1,0:T(8,128)(2,1)S(1)} %get-tuple-element.41), channel_id=1, source_target_pairs={{0,7},{1,0},{2,1},{3,2},{4,3},{5,4},{6,5},{7,6},{8,15},{9,8},{10,9... | collective-permute-start | bytes 49160 | tf_op jit(solution)/shard_map/ppermute | solution.py:115
  21.2 1.6 collective-permute-start
  22.7 3.2 %collective-permute-start.1 = (bf16[16,1024]{1,0:T(8,128)(2,1)S(1)}, bf16[16,1024]{1,0:T(8,128)(2,1)S(1)}, u32[]{:S(2)}, u32[]{:S(2)}) collective-permute-start(bf16[16,1024]{1,0:T(8,128)(2,1)S(1)} %get-tuple-element.33), channel_id=1, source_target_pairs={{0,112},{8,120},{16,0},{24,8},{32,16},{40,24},{48,32},{56,40},{64,... | collective-permute-start | bytes 98312 | tf_op jit(solution)/shard_map/ppermute | solution.py:103
  25.9 0.7 collective-permute-start.2
  26.6 2.0 %collective-permute-start.3 = (bf16[16,1024]{1,0:T(8,128)(2,1)S(1)}, bf16[16,1024]{1,0:T(8,128)(2,1)S(1)}, u32[]{:S(2)}, u32[]{:S(2)}) collective-permute-start(bf16[16,1024]{1,0:T(8,128)(2,1)S(1)} %get-tuple-element.31), channel_id=1, source_target_pairs={{0,96},{8,104},{16,112},{24,120},{32,0},{40,8},{48,16},{56,24},{64... | collective-permute-start | bytes 98312 | tf_op jit(solution)/shard_map/ppermute | solution.py:103
  28.7 29.0 %collective-permute-done.15 = bf16[128,64]{1,0:T(8,128)(2,1)S(1)} collective-permute-done((bf16[128,64]{1,0:T(8,128)(2,1)S(1)}, bf16[128,64]{1,0:T(8,128)(2,1)S(1)}, u32[]{:S(2)}, u32[]{:S(2)}) %collective-permute-start.15) | collective-permute-done | bytes 16416 | tf_op jit(solution)/shard_map/ppermute | solution.py:115
  57.6 42.3 %collective-permute-start.16 = (bf16[128,64]{1,0:T(8,128)(2,1)S(1)}, bf16[128,64]{1,0:T(8,128)(2,1)S(1)}, u32[]{:S(2)}, u32[]{:S(2)}) collective-permute-start(bf16[128,64]{1,0:T(8,128)(2,1)S(1)} %get-tuple-element.40), channel_id=1, source_target_pairs={{0,6},{1,7},{2,0},{3,1},{4,2},{5,3},{6,4},{7,5},{8,14},{9,15},{10,... | collective-permute-start | bytes 49160 | tf_op jit(solution)/shard_map/ppermute | solution.py:115
  100.0 2.7 %collective-permute-done.16 = bf16[128,64]{1,0:T(8,128)(2,1)S(1)} collective-permute-done((bf16[128,64]{1,0:T(8,128)(2,1)S(1)}, bf16[128,64]{1,0:T(8,128)(2,1)S(1)}, u32[]{:S(2)}, u32[]{:S(2)}) %collective-permute-start.16) | collective-permute-done | bytes 16416 | tf_op jit(solution)/shard_map/ppermute | solution.py:115
  102.7 4.1 %collective-permute-start.17 = (bf16[128,64]{1,0:T(8,128)(2,1)S(1)}, bf16[128,64]{1,0:T(8,128)(2,1)S(1)}, u32[]{:S(2)}, u32[]{:S(2)}) collective-permute-start(bf16[128,64]{1,0:T(8,128)(2,1)S(1)} %get-tuple-element.39), channel_id=1, source_target_pairs={{0,5},{1,6},{2,7},{3,0},{4,1},{5,2},{6,3},{7,4},{8,13},{9,14},{10,... | collective-permute-start | bytes 49160 | tf_op jit(solution)/shard_map/ppermute | solution.py:115
  106.8 1.1 collective-permute-done.17
  107.9 2.8 %collective-permute-start.18 = (bf16[128,64]{1,0:T(8,128)(2,1)S(1)}, bf16[128,64]{1,0:T(8,128)(2,1)S(1)}, u32[]{:S(2)}, u32[]{:S(2)}) collective-permute-start(bf16[128,64]{1,0:T(8,128)(2,1)S(1)} %get-tuple-element.38), channel_id=1, source_target_pairs={{0,4},{1,5},{2,6},{3,7},{4,0},{5,1},{6,2},{7,3},{8,12},{9,13},{10,... | collective-permute-start | bytes 49160 | tf_op jit(solution)/shard_map/ppermute | solution.py:115
  110.7 1.5 collective-permute-done.18
  112.1 5.2 %collective-permute-start.19 = (bf16[128,64]{1,0:T(8,128)(2,1)S(1)}, bf16[128,64]{1,0:T(8,128)(2,1)S(1)}, u32[]{:S(2)}, u32[]{:S(2)}) collective-permute-start(bf16[128,64]{1,0:T(8,128)(2,1)S(1)} %get-tuple-element.37), channel_id=1, source_target_pairs={{0,3},{1,4},{2,5},{3,6},{4,7},{5,0},{6,1},{7,2},{8,11},{9,12},{10,... | collective-permute-start | bytes 49160 | tf_op jit(solution)/shard_map/ppermute | solution.py:115
  117.3 1.8 collective-permute-done.19
  119.1 1.5 collective-permute-start.20
  120.7 3.4 %collective-permute-done.20 = bf16[128,64]{1,0:T(8,128)(2,1)S(1)} collective-permute-done((bf16[128,64]{1,0:T(8,128)(2,1)S(1)}, bf16[128,64]{1,0:T(8,128)(2,1)S(1)}, u32[]{:S(2)}, u32[]{:S(2)}) %collective-permute-start.20) | collective-permute-done | bytes 16416 | tf_op jit(solution)/shard_map/ppermute | solution.py:115
  124.1 4.1 %collective-permute-start.21 = (bf16[128,64]{1,0:T(8,128)(2,1)S(1)}, bf16[128,64]{1,0:T(8,128)(2,1)S(1)}, u32[]{:S(2)}, u32[]{:S(2)}) collective-permute-start(bf16[128,64]{1,0:T(8,128)(2,1)S(1)} %get-tuple-element.35), channel_id=1, source_target_pairs={{0,1},{1,2},{2,3},{3,4},{4,5},{5,6},{6,7},{7,0},{8,9},{9,10},{10,1... | collective-permute-start | bytes 49160 | tf_op jit(solution)/shard_map/ppermute | solution.py:115
  128.2 2.2 %collective-permute-done.21 = bf16[128,64]{1,0:T(8,128)(2,1)S(1)} collective-permute-done((bf16[128,64]{1,0:T(8,128)(2,1)S(1)}, bf16[128,64]{1,0:T(8,128)(2,1)S(1)}, u32[]{:S(2)}, u32[]{:S(2)}) %collective-permute-start.21) | collective-permute-done | bytes 16416 | tf_op jit(solution)/shard_map/ppermute | solution.py:115
  130.5 12.0 %collective-permute-start.4 = (bf16[16,1024]{1,0:T(8,128)(2,1)S(1)}, bf16[16,1024]{1,0:T(8,128)(2,1)S(1)}, u32[]{:S(2)}, u32[]{:S(2)}) collective-permute-start(bf16[16,1024]{1,0:T(8,128)(2,1)S(1)} %get-tuple-element.30), channel_id=1, source_target_pairs={{0,88},{8,96},{16,104},{24,112},{32,120},{40,0},{48,8},{56,16},{64... | collective-permute-start | bytes 98312 | tf_op jit(solution)/shard_map/ppermute | solution.py:103
  142.5 0.1 constant_dynamic-update-slice_fusion.40
  142.7 0.1 constant_dynamic-update-slice_fusion.32
  142.9 2.3 %collective-permute-start.5 = (bf16[16,1024]{1,0:T(8,128)(2,1)S(1)}, bf16[16,1024]{1,0:T(8,128)(2,1)S(1)}, u32[]{:S(2)}, u32[]{:S(2)}) collective-permute-start(bf16[16,1024]{1,0:T(8,128)(2,1)S(1)} %get-tuple-element.29), channel_id=1, source_target_pairs={{0,80},{8,88},{16,96},{24,104},{32,112},{40,120},{48,0},{56,8},{64... | collective-permute-start | bytes 98312 | tf_op jit(solution)/shard_map/ppermute | solution.py:103
  145.2 0.8 collective-permute-start.7
  146.0 1.9 collective-permute-start.8
  148.0 0.7 collective-permute-start.9
  148.7 1.4 collective-permute-start.10
  150.1 1.7 collective-permute-start.11
  151.8 2.1 %collective-permute-start.12 = (bf16[16,1024]{1,0:T(8,128)(2,1)S(1)}, bf16[16,1024]{1,0:T(8,128)(2,1)S(1)}, u32[]{:S(2)}, u32[]{:S(2)}) collective-permute-start(bf16[16,1024]{1,0:T(8,128)(2,1)S(1)} %get-tuple-element.22), channel_id=1, source_target_pairs={{0,24},{8,32},{16,40},{24,48},{32,56},{40,64},{48,72},{56,80},{64,... | collective-permute-start | bytes 98312 | tf_op jit(solution)/shard_map/ppermute | solution.py:103
  153.9 1.7 collective-permute-start.14
  155.6 2.0 collective-permute-done.12
  157.5 1.2 collective-permute-done.13
  159.0 0.3 fusion.4
  159.4 6.9 %shard_map.153 = (f32[1024,512]{1,0:T(8,128)}, f32[1024,512]{1,0:T(8,128)}, f32[1024,512]{1,0:T(8,128)}, bf16[1024,512]{1,0:T(8,128)(2,1)}) custom-call(f32[8,384,512]{2,1,0:T(8,128)} %all-to-all-done.state_ref, f32[1024,512]{1,0:T(8,128)} %grad_ref.1), custom_call_target="tpu_custom_call" | custom-call | tf_op jit(solution)/shard_map/pallas_call | solution.py:46
  166.2 1.7 fusion.3
  167.9 0.1 pad_maximum_fusion
  167.9 15.3 %all_to_all.20 = f32[16,16,576]{2,1,0:T(8,128)S(1)} all-to-all(f32[16,16,576]{2,1,0:T(8,128)S(1)} %bitcast.86), channel_id=1, replica_groups=mesh['fsdp'=16,'tp'=8] {'fsdp'}, dimensions={0} | all-to-all | bytes 1179648 | tf_op jit(solution)/shard_map/all_to_all | solution.py:82
  183.3 0.1 broadcast_in_dim.2
  183.3 1.0 reshape.42
  184.3 6.1 %all-to-all-start.2 = ((bf16[128,2,512]{2,1,0:T(2,128)(2,1)}), bf16[128,2,512]{2,1,0:T(2,128)(2,1)S(1)}, u32[]{:S(2)}, u32[]{:S(2)}) async-start(bf16[128,2,512]{2,1,0:T(2,128)(2,1)} %reshape.42), calls=%async_computation.2 | async-start | bytes 524288 | tf_op jit(solution)/shard_map/all_to_all | solution.py:78
  190.4 0.6 slice.10
  191.0 10.0 %all-to-all-done.2 = bf16[128,2,512]{2,1,0:T(2,128)(2,1)S(1)} async-done(((bf16[128,2,512]{2,1,0:T(2,128)(2,1)}), bf16[128,2,512]{2,1,0:T(2,128)(2,1)S(1)}, u32[]{:S(2)}, u32[]{:S(2)}) %all-to-all-start.2) | async-done | bytes 262176 | tf_op jit(solution)/shard_map/all_to_all | solution.py:78
  201.0 0.3 reshape.43
  201.3 0.1 copy.20
  201.5 1.0 reshape.41
  (77 shorter events, 0.5 us)
Async XLA Ops:
  6.5 8.4 %copy-start.1 = (f32[128,512]{1,0:T(8,128)S(1)}, f32[128,512]{1,0:T(8,128)}, u32[]{:S(2)}) copy-start(f32[128,512]{1,0:T(8,128)} %param.14) | copy-start | bytes 786436
  6.5 8.4 %copy-start.2 = (f32[128,512]{1,0:T(8,128)S(1)}, f32[128,512]{1,0:T(8,128)}, u32[]{:S(2)}) copy-start(f32[128,512]{1,0:T(8,128)} %param.17) | copy-start | bytes 786436
  6.5 8.4 %copy-start.3 = (f32[128,512]{1,0:T(8,128)S(1)}, f32[128,512]{1,0:T(8,128)}, u32[]{:S(2)}) copy-start(f32[128,512]{1,0:T(8,128)} %param.16) | copy-start | bytes 786436
  6.5 8.4 %copy-start.4 = (f32[128,512]{1,0:T(8,128)S(1)}, f32[128,512]{1,0:T(8,128)}, u32[]{:S(2)}) copy-start(f32[128,512]{1,0:T(8,128)} %param.15) | copy-start | bytes 786436
  6.5 152.8 %all-to-all-start = ((f32[8,384,512]{2,1,0:T(8,128)}), f32[8,384,512]{2,1,0:T(8,128)}, u32[]{:S(2)}, u32[]{:S(2)}) async-start(f32[8,384,512]{2,1,0:T(8,128)} %shard_map.152), calls=%async_computation | async-start | bytes 12582912 | tf_op jit(solution)/shard_map/all_to_all | solution.py:122
  14.8 6.3 %copy-start = (bf16[16,16384]{1,0:T(8,128)(2,1)S(1)}, bf16[16,16384]{1,0:T(8,128)(2,1)}, u32[]{:S(2)}) copy-start(bf16[16,16384]{1,0:T(8,128)(2,1)} %param.9) | copy-start | bytes 1572868
  16.1 41.6 %collective-permute-start.15 = (bf16[128,64]{1,0:T(8,128)(2,1)S(1)}, bf16[128,64]{1,0:T(8,128)(2,1)S(1)}, u32[]{:S(2)}, u32[]{:S(2)}) collective-permute-start(bf16[128,64]{1,0:T(8,128)(2,1)S(1)} %get-tuple-element.41), channel_id=1, source_target_pairs={{0,7},{1,0},{2,1},{3,2},{4,3},{5,4},{6,5},{7,6},{8,15},{9,8},{10,9... | collective-permute-start | bytes 49160 | tf_op jit(solution)/shard_map/ppermute | solution.py:115
  21.2 121.7 %collective-permute-start = (bf16[16,1024]{1,0:T(8,128)(2,1)S(1)}, bf16[16,1024]{1,0:T(8,128)(2,1)S(1)}, u32[]{:S(2)}, u32[]{:S(2)}) collective-permute-start(bf16[16,1024]{1,0:T(8,128)(2,1)S(1)} %get-tuple-element.34), channel_id=1, source_target_pairs={{0,120},{8,0},{16,8},{24,16},{32,24},{40,32},{48,40},{56,48},{64,5... | collective-permute-start | bytes 98312 | tf_op jit(solution)/shard_map/ppermute | solution.py:103
  22.7 122.4 %collective-permute-start.1 = (bf16[16,1024]{1,0:T(8,128)(2,1)S(1)}, bf16[16,1024]{1,0:T(8,128)(2,1)S(1)}, u32[]{:S(2)}, u32[]{:S(2)}) collective-permute-start(bf16[16,1024]{1,0:T(8,128)(2,1)S(1)} %get-tuple-element.33), channel_id=1, source_target_pairs={{0,112},{8,120},{16,0},{24,8},{32,16},{40,24},{48,32},{56,40},{64,... | collective-permute-start | bytes 98312 | tf_op jit(solution)/shard_map/ppermute | solution.py:103
  25.9 119.3 %collective-permute-start.2 = (bf16[16,1024]{1,0:T(8,128)(2,1)S(1)}, bf16[16,1024]{1,0:T(8,128)(2,1)S(1)}, u32[]{:S(2)}, u32[]{:S(2)}) collective-permute-start(bf16[16,1024]{1,0:T(8,128)(2,1)S(1)} %get-tuple-element.32), channel_id=1, source_target_pairs={{0,104},{8,112},{16,120},{24,0},{32,8},{40,16},{48,24},{56,32},{64... | collective-permute-start | bytes 98312 | tf_op jit(solution)/shard_map/ppermute | solution.py:103
  26.6 119.4 %collective-permute-start.3 = (bf16[16,1024]{1,0:T(8,128)(2,1)S(1)}, bf16[16,1024]{1,0:T(8,128)(2,1)S(1)}, u32[]{:S(2)}, u32[]{:S(2)}) collective-permute-start(bf16[16,1024]{1,0:T(8,128)(2,1)S(1)} %get-tuple-element.31), channel_id=1, source_target_pairs={{0,96},{8,104},{16,112},{24,120},{32,0},{40,8},{48,16},{56,24},{64... | collective-permute-start | bytes 98312 | tf_op jit(solution)/shard_map/ppermute | solution.py:103
  57.6 45.0 %collective-permute-start.16 = (bf16[128,64]{1,0:T(8,128)(2,1)S(1)}, bf16[128,64]{1,0:T(8,128)(2,1)S(1)}, u32[]{:S(2)}, u32[]{:S(2)}) collective-permute-start(bf16[128,64]{1,0:T(8,128)(2,1)S(1)} %get-tuple-element.40), channel_id=1, source_target_pairs={{0,6},{1,7},{2,0},{3,1},{4,2},{5,3},{6,4},{7,5},{8,14},{9,15},{10,... | collective-permute-start | bytes 49160 | tf_op jit(solution)/shard_map/ppermute | solution.py:115
  102.7 5.2 %collective-permute-start.17 = (bf16[128,64]{1,0:T(8,128)(2,1)S(1)}, bf16[128,64]{1,0:T(8,128)(2,1)S(1)}, u32[]{:S(2)}, u32[]{:S(2)}) collective-permute-start(bf16[128,64]{1,0:T(8,128)(2,1)S(1)} %get-tuple-element.39), channel_id=1, source_target_pairs={{0,5},{1,6},{2,7},{3,0},{4,1},{5,2},{6,3},{7,4},{8,13},{9,14},{10,... | collective-permute-start | bytes 49160 | tf_op jit(solution)/shard_map/ppermute | solution.py:115
  107.9 4.3 %collective-permute-start.18 = (bf16[128,64]{1,0:T(8,128)(2,1)S(1)}, bf16[128,64]{1,0:T(8,128)(2,1)S(1)}, u32[]{:S(2)}, u32[]{:S(2)}) collective-permute-start(bf16[128,64]{1,0:T(8,128)(2,1)S(1)} %get-tuple-element.38), channel_id=1, source_target_pairs={{0,4},{1,5},{2,6},{3,7},{4,0},{5,1},{6,2},{7,3},{8,12},{9,13},{10,... | collective-permute-start | bytes 49160 | tf_op jit(solution)/shard_map/ppermute | solution.py:115
  112.1 7.0 %collective-permute-start.19 = (bf16[128,64]{1,0:T(8,128)(2,1)S(1)}, bf16[128,64]{1,0:T(8,128)(2,1)S(1)}, u32[]{:S(2)}, u32[]{:S(2)}) collective-permute-start(bf16[128,64]{1,0:T(8,128)(2,1)S(1)} %get-tuple-element.37), channel_id=1, source_target_pairs={{0,3},{1,4},{2,5},{3,6},{4,7},{5,0},{6,1},{7,2},{8,11},{9,12},{10,... | collective-permute-start | bytes 49160 | tf_op jit(solution)/shard_map/ppermute | solution.py:115
  119.1 4.9 %collective-permute-start.20 = (bf16[128,64]{1,0:T(8,128)(2,1)S(1)}, bf16[128,64]{1,0:T(8,128)(2,1)S(1)}, u32[]{:S(2)}, u32[]{:S(2)}) collective-permute-start(bf16[128,64]{1,0:T(8,128)(2,1)S(1)} %get-tuple-element.36), channel_id=1, source_target_pairs={{0,2},{1,3},{2,4},{3,5},{4,6},{5,7},{6,0},{7,1},{8,10},{9,11},{10,... | collective-permute-start | bytes 49160 | tf_op jit(solution)/shard_map/ppermute | solution.py:115
  124.1 6.4 %collective-permute-start.21 = (bf16[128,64]{1,0:T(8,128)(2,1)S(1)}, bf16[128,64]{1,0:T(8,128)(2,1)S(1)}, u32[]{:S(2)}, u32[]{:S(2)}) collective-permute-start(bf16[128,64]{1,0:T(8,128)(2,1)S(1)} %get-tuple-element.35), channel_id=1, source_target_pairs={{0,1},{1,2},{2,3},{3,4},{4,5},{5,6},{6,7},{7,0},{8,9},{9,10},{10,1... | collective-permute-start | bytes 49160 | tf_op jit(solution)/shard_map/ppermute | solution.py:115
  130.5 17.5 %collective-permute-start.4 = (bf16[16,1024]{1,0:T(8,128)(2,1)S(1)}, bf16[16,1024]{1,0:T(8,128)(2,1)S(1)}, u32[]{:S(2)}, u32[]{:S(2)}) collective-permute-start(bf16[16,1024]{1,0:T(8,128)(2,1)S(1)} %get-tuple-element.30), channel_id=1, source_target_pairs={{0,88},{8,96},{16,104},{24,112},{32,120},{40,0},{48,8},{56,16},{64... | collective-permute-start | bytes 98312 | tf_op jit(solution)/shard_map/ppermute | solution.py:103
  142.9 5.8 %collective-permute-start.5 = (bf16[16,1024]{1,0:T(8,128)(2,1)S(1)}, bf16[16,1024]{1,0:T(8,128)(2,1)S(1)}, u32[]{:S(2)}, u32[]{:S(2)}) collective-permute-start(bf16[16,1024]{1,0:T(8,128)(2,1)S(1)} %get-tuple-element.29), channel_id=1, source_target_pairs={{0,80},{8,88},{16,96},{24,104},{32,112},{40,120},{48,0},{56,8},{64... | collective-permute-start | bytes 98312 | tf_op jit(solution)/shard_map/ppermute | solution.py:103
  145.2 4.9 %collective-permute-start.6 = (bf16[16,1024]{1,0:T(8,128)(2,1)S(1)}, bf16[16,1024]{1,0:T(8,128)(2,1)S(1)}, u32[]{:S(2)}, u32[]{:S(2)}) collective-permute-start(bf16[16,1024]{1,0:T(8,128)(2,1)S(1)} %get-tuple-element.28), channel_id=1, source_target_pairs={{0,72},{8,80},{16,88},{24,96},{32,104},{40,112},{48,120},{56,0},{6... | collective-permute-start | bytes 98312 | tf_op jit(solution)/shard_map/ppermute | solution.py:103
  145.2 6.6 %collective-permute-start.7 = (bf16[16,1024]{1,0:T(8,128)(2,1)S(1)}, bf16[16,1024]{1,0:T(8,128)(2,1)S(1)}, u32[]{:S(2)}, u32[]{:S(2)}) collective-permute-start(bf16[16,1024]{1,0:T(8,128)(2,1)S(1)} %get-tuple-element.27), channel_id=1, source_target_pairs={{0,64},{8,72},{16,80},{24,88},{32,96},{40,104},{48,112},{56,120},{... | collective-permute-start | bytes 98312 | tf_op jit(solution)/shard_map/ppermute | solution.py:103
  146.0 7.8 %collective-permute-start.8 = (bf16[16,1024]{1,0:T(8,128)(2,1)S(1)}, bf16[16,1024]{1,0:T(8,128)(2,1)S(1)}, u32[]{:S(2)}, u32[]{:S(2)}) collective-permute-start(bf16[16,1024]{1,0:T(8,128)(2,1)S(1)} %get-tuple-element.26), channel_id=1, source_target_pairs={{0,56},{8,64},{16,72},{24,80},{32,88},{40,96},{48,104},{56,112},{6... | collective-permute-start | bytes 98312 | tf_op jit(solution)/shard_map/ppermute | solution.py:103
  148.0 5.9 %collective-permute-start.9 = (bf16[16,1024]{1,0:T(8,128)(2,1)S(1)}, bf16[16,1024]{1,0:T(8,128)(2,1)S(1)}, u32[]{:S(2)}, u32[]{:S(2)}) collective-permute-start(bf16[16,1024]{1,0:T(8,128)(2,1)S(1)} %get-tuple-element.25), channel_id=1, source_target_pairs={{0,48},{8,56},{16,64},{24,72},{32,80},{40,88},{48,96},{56,104},{64... | collective-permute-start | bytes 98312 | tf_op jit(solution)/shard_map/ppermute | solution.py:103
  148.7 6.9 %collective-permute-start.10 = (bf16[16,1024]{1,0:T(8,128)(2,1)S(1)}, bf16[16,1024]{1,0:T(8,128)(2,1)S(1)}, u32[]{:S(2)}, u32[]{:S(2)}) collective-permute-start(bf16[16,1024]{1,0:T(8,128)(2,1)S(1)} %get-tuple-element.24), channel_id=1, source_target_pairs={{0,40},{8,48},{16,56},{24,64},{32,72},{40,80},{48,88},{56,96},{64,... | collective-permute-start | bytes 98312 | tf_op jit(solution)/shard_map/ppermute | solution.py:103
  150.1 5.5 %collective-permute-start.11 = (bf16[16,1024]{1,0:T(8,128)(2,1)S(1)}, bf16[16,1024]{1,0:T(8,128)(2,1)S(1)}, u32[]{:S(2)}, u32[]{:S(2)}) collective-permute-start(bf16[16,1024]{1,0:T(8,128)(2,1)S(1)} %get-tuple-element.23), channel_id=1, source_target_pairs={{0,32},{8,40},{16,48},{24,56},{32,64},{40,72},{48,80},{56,88},{64,... | collective-permute-start | bytes 98312 | tf_op jit(solution)/shard_map/ppermute | solution.py:103
  151.8 5.8 %collective-permute-start.12 = (bf16[16,1024]{1,0:T(8,128)(2,1)S(1)}, bf16[16,1024]{1,0:T(8,128)(2,1)S(1)}, u32[]{:S(2)}, u32[]{:S(2)}) collective-permute-start(bf16[16,1024]{1,0:T(8,128)(2,1)S(1)} %get-tuple-element.22), channel_id=1, source_target_pairs={{0,24},{8,32},{16,40},{24,48},{32,56},{40,64},{48,72},{56,80},{64,... | collective-permute-start | bytes 98312 | tf_op jit(solution)/shard_map/ppermute | solution.py:103
  153.9 4.9 %collective-permute-start.13 = (bf16[16,1024]{1,0:T(8,128)(2,1)S(1)}, bf16[16,1024]{1,0:T(8,128)(2,1)S(1)}, u32[]{:S(2)}, u32[]{:S(2)}) collective-permute-start(bf16[16,1024]{1,0:T(8,128)(2,1)S(1)} %get-tuple-element.21), channel_id=1, source_target_pairs={{0,16},{8,24},{16,32},{24,40},{32,48},{40,56},{48,64},{56,72},{64,... | collective-permute-start | bytes 98312 | tf_op jit(solution)/shard_map/ppermute | solution.py:103
  153.9 4.8 %collective-permute-start.14 = (bf16[16,1024]{1,0:T(8,128)(2,1)S(1)}, bf16[16,1024]{1,0:T(8,128)(2,1)S(1)}, u32[]{:S(2)}, u32[]{:S(2)}) collective-permute-start(bf16[16,1024]{1,0:T(8,128)(2,1)S(1)} %get-tuple-element.20), channel_id=1, source_target_pairs={{0,8},{8,16},{16,24},{24,32},{32,40},{40,48},{48,56},{56,64},{64,7... | collective-permute-start | bytes 98312 | tf_op jit(solution)/shard_map/ppermute | solution.py:103
  184.3 16.7 %all-to-all-start.2 = ((bf16[128,2,512]{2,1,0:T(2,128)(2,1)}), bf16[128,2,512]{2,1,0:T(2,128)(2,1)S(1)}, u32[]{:S(2)}, u32[]{:S(2)}) async-start(bf16[128,2,512]{2,1,0:T(2,128)(2,1)} %reshape.42), calls=%async_computation.2 | async-start | bytes 524288 | tf_op jit(solution)/shard_map/all_to_all | solution.py:78

commit v9 on v8

--- a/solution.py
+++ b/solution.py
@@ -22,14 +22,14 @@
     return (master - LEARN_RATE * update, first_new, second_new)
 
 
-def adam_kernel(state_ref, grad_ref, master_out, first_out, second_out, low_out):
+def adam_kernel(state_ref, second_ref, grad_ref, master_out, first_out, second_out, low_out):
     per, rows = state_ref.shape[0], grad_ref.shape[0] // state_ref.shape[0]
     for j in range(per):
         out = pl.ds(j * rows, rows)
         new, first_new, second_new = adam_step(
             state_ref[j, pl.ds(0, rows), :],
             state_ref[j, pl.ds(rows, rows), :],
-            state_ref[j, pl.ds(2 * rows, rows), :],
+            second_ref[out, :],
             grad_ref[out, :],
         )
         master_out[out, :] = new
@@ -38,39 +38,40 @@
         low_out[out, :] = new.astype(low_out.dtype)
 
 
-def adam_from_blocks(state, grad, per=2):
+def adam_from_blocks(state, second, grad, per=2):
     sources, stacked, cols = state.shape
-    rows = stacked // 3
+    rows = stacked // 2
     block = pl.BlockSpec((per * rows, cols), lambda i: (i, 0))
     f32 = jax.ShapeDtypeStruct(grad.shape, jnp.float32)
     return pl.pallas_call(
         adam_kernel,
         grid=(sources // per,),
-        in_specs=[pl.BlockSpec((per, stacked, cols), lambda i: (i, 0, 0)), block],
+        in_specs=[pl.BlockSpec((per, stacked, cols), lambda i: (i, 0, 0)), block, block],
         out_specs=[block] * 4,
         out_shape=[f32, f32, f32, jax.ShapeDtypeStruct(grad.shape, jnp.bfloat16)],
-    )(state, grad)
+    )(state, second, grad)
 
 
-def pack_kernel(master_ref, first_ref, second_ref, out_ref):
-    rows, width = master_ref.shape[0], out_ref.shape[2]
+def pack_kernel(*refs):
+    *in_refs, out_ref = refs
+    rows, width = in_refs[0].shape[0], out_ref.shape[2]
     for j in range(out_ref.shape[0]):
         cols = pl.ds(j * width, width)
-        for k, ref in enumerate((master_ref, first_ref, second_ref)):
+        for k, ref in enumerate(in_refs):
             out_ref[j, pl.ds(k * rows, rows), :] = ref[:, cols]
 
 
-def pack_by_destination(master, first, second, dests, per=2):
-    rows, cols = master.shape
+def pack_by_destination(arrays, dests, per=2):
+    rows, cols = arrays[0].shape
     width = cols // dests
     block = pl.BlockSpec((rows, per * width), lambda i: (0, i))
     return pl.pallas_call(
         pack_kernel,
         grid=(dests // per,),
-        in_specs=[block] * 3,
-        out_specs=pl.BlockSpec((per, 3 * rows, width), lambda i: (i, 0, 0)),
-        out_shape=jax.ShapeDtypeStruct((dests, 3 * rows, width), master.dtype),
-    )(master, first, second)
+        in_specs=[block] * len(arrays),
+        out_specs=pl.BlockSpec((per, len(arrays) * rows, width), lambda i: (i, 0, 0)),
+        out_shape=jax.ShapeDtypeStruct((dests, len(arrays) * rows, width), arrays[0].dtype),
+    )(*arrays)
 
 
 def gather_rows(x, axis_name, size):
@@ -118,17 +119,27 @@
     wkv_rows = wkv_rows.reshape(tp * wkv_low.shape[0], slice_kv)
     kv_term = jnp.dot(columns, wkv_rows, preferred_element_type=jnp.float32)
 
-    send = pack_by_destination(wq_master, wq_first, wq_second, tp)
+    rows, cols = wq_master.shape
+    send = pack_by_destination((wq_master, wq_first), tp)
+    width = cols // tp
+    got2 = [lax.dynamic_slice_in_dim(wq_second, me_tp * width, width, 1)]
     state = lax.all_to_all(send, "tp", split_axis=0, concat_axis=0, tiled=True)
-    wq_new, wq_mom, wq_var, wq_low = adam_from_blocks(state, wq_grad)
+    for k in range(1, tp):
+        block = lax.dynamic_slice_in_dim(wq_second, ((me_tp + k) % tp) * width, width, 1)
+        got2.append(lax.ppermute(block, "tp", [(i, (i + k) % tp) for i in range(tp)]))
+    got2 = jnp.stack(got2[::-1])
+    second = lax.dynamic_slice_in_dim(jnp.concatenate([got2, got2]), tp - 1 - me_tp, tp, 0)
+    second = second.reshape(tp * rows, width)
+    wq_new, wq_mom, wq_var, wq_low = adam_from_blocks(state, second, wq_grad)
     q_term = jnp.dot(columns, wq_low, preferred_element_type=jnp.float32)
 
     sums = scatter_sum_rows(jnp.concatenate([q_term, kv_term], axis=1), "fsdp", fsdp)
     q_cols = q_term.shape[1]
     probe_query = sums[:, :q_cols].astype(jnp.bfloat16)
     kv_block = sums[:, q_cols:].astype(jnp.bfloat16)
-    kv_all = gather_rows(kv_block, ("fsdp", "tp"), fsdp * tp)
     tokens = kv_block.shape[0]
+    lanes = 128
+    kv_all = gather_rows(kv_block.reshape(tokens * slice_kv // lanes, lanes), ("fsdp", "tp"), fsdp * tp)
     kv_all = kv_all.reshape(fsdp, tp, tokens, slice_kv).transpose(0, 2, 1, 3)
     probe_keyvalue = kv_all.reshape(fsdp * tokens, tp * slice_kv)
     return (wq_new, wq_mom, wq_var, wkv_new, wkv_mom, wkv_var, probe_query, probe_keyvalue)

time: 203 us -> 215 us (1.059)
  waiting for transfers between devices: 54.8 us -> 64.8 us
  local copies, waits for them, and re-layouts: 3.92 us -> 10.5 us
  starting transfers between devices: 112 us -> 107 us
    ppermute x7 -> x14, waiting for transfers between devices: 41.7 us -> 54.8 us  [step(): lax.ppermute(block, 'tp', [(i, (i + k) % tp) for i in range(tp)])]
    ppermute x7 -> x14, starting transfers between devices: 65.1 us -> 61.4 us  [step(): lax.ppermute(block, 'tp', [(i, (i + k) % tp) for i in range(tp)])]
    ppermute x15, waiting for transfers between devices: 3.19 us -> 0.04 us  [step(): lax.ppermute(block, 'fsdp', [(i, (i + k) % fsdp) for i in range(fsdp)])]
    dynamic_slice x0 -> x2, local copies, waits for them, and re-layouts: none -> 2.68 us  [the longest x1 1.62 us: step(): lax.dynamic_slice_in_dim(jnp.concatenate([got2, got2]), tp - 1 - me_tp, t...]
    ppermute x15, starting transfers between devices: 32.1 us -> 29.5 us  [step(): lax.ppermute(block, 'fsdp', [(i, (i + k) % fsdp) for i in range(fsdp)])]
    all_to_all x1, starting transfers between devices: 6.07 us -> 8.5 us  [gather_rows(): lax.all_to_all(copies, axis_name, split_axis=0, concat_axis=0, tiled=True)]
  transfers between devices with their start and end apart: 24 -> 31, of which waited for: 10 -> 13; matrix products, arithmetic and copies ran while one was open for 1% -> 4% of each run, Pallas kernels for 0% -> 2%
where the time goes in v9:
time: 215 us; the launch traced here: 214 us
  starting transfers between devices  107 us (50%)
  waiting for transfers between devices  64.8 us (30%)
  blocking collectives  15.9 us (7%)
  Pallas kernels  11.7 us (5%)
  local copies, waits for them, and re-layouts  10.5 us (5%)
    ppermute x14, starting transfers between devices, step(): lax.ppermute(block, 'tp', [(i, (i + k) % tp) for i in range(tp)])  61.4 us
    ppermute x14, waiting for transfers between devices, step(): lax.ppermute(block, 'tp', [(i, (i + k) % tp) for i in range(tp)])  54.8 us
    ppermute x15, starting transfers between devices, step(): lax.ppermute(block, 'fsdp', [(i, (i + k) % fsdp) for i in range(fsdp)])  29.5 us
    all_to_all x1, blocking collectives, scatter_sum_rows(): lax.all_to_all(x, axis_name, split_axis=0, concat_axis=0, tiled=True)  15.9 us
    all_to_all x1, waiting for transfers between devices, gather_rows(): lax.all_to_all(copies, axis_name, split_axis=0, concat_axis=0, tiled=True)  9.97 us
    all_to_all x1, starting transfers between devices, gather_rows(): lax.all_to_all(copies, axis_name, split_axis=0, concat_axis=0, tiled=True)  8.5 us
    all_to_all x1, starting transfers between devices, step(): state = lax.all_to_all(send, 'tp', split_axis=0, concat_axis=0, tiled=True)  7.61 us
    pallas_call x1, Pallas kernels, adam_from_blocks(): pl.pallas_call(adam_kernel, grid=(sources // per,), in_specs=[pl.BlockSpe...  6.89 us
  transfers between devices with their start and end apart: 31, of which 13 were waited for; matrix products, arithmetic and copies ran while one was open for 4% of the time, Pallas kernels for 2%

profile of v9, /device:TPU:1, one launch (start us, length us, event | category | flops | bytes accessed | tf_op | source)
XLA Modules:
  0.0 214.3 jit_solution(14424455969771075353)
XLA Ops:
  0.8 1.8 constant_dynamic-slice_fusion.9
  2.7 1.4 collective-permute-start.7
  4.1 4.2 %collective-permute-start.8 = (bf16[16,1024]{1,0:T(8,128)(2,1)}, bf16[16,1024]{1,0:T(8,128)(2,1)S(1)}, u32[]{:S(2)}, u32[]{:S(2)}) collective-permute-start(bf16[16,1024]{1,0:T(8,128)(2,1)} %get-tuple-element.40), channel_id=1, source_target_pairs={{0,112},{8,120},{16,0},{24,8},{32,16},{40,24},{48,32},{56,40},{64,... | collective-permute-start | bytes 98312 | tf_op jit(solution)/shard_map/ppermute | solution.py:104
  9.0 2.0 collective-permute-start.10
  11.0 4.8 %shard_map.152 = f32[8,256,512]{2,1,0:T(8,128)} custom-call(f32[128,4096]{1,0:T(8,128)} %refs_0_.1, f32[128,4096]{1,0:T(8,128)} %refs_1_.1), custom_call_target="tpu_custom_call" | custom-call | tf_op jit(solution)/shard_map/pallas_call | solution.py:68
  15.8 7.6 %all-to-all-start = ((f32[8,256,512]{2,1,0:T(8,128)}), f32[8,256,512]{2,1,0:T(8,128)}, u32[]{:S(2)}, u32[]{:S(2)}) async-start(f32[8,256,512]{2,1,0:T(8,128)} %shard_map.152), calls=%async_computation | async-start | bytes 8388608 | tf_op jit(solution)/shard_map/all_to_all | solution.py:126
  23.5 1.0 fusion.1
  25.2 5.1 %collective-permute-start.22 = (bf16[128,64]{1,0:T(8,128)(2,1)S(1)}, bf16[128,64]{1,0:T(8,128)(2,1)S(1)}, u32[]{:S(2)}, u32[]{:S(2)}) collective-permute-start(bf16[128,64]{1,0:T(8,128)(2,1)S(1)} %get-tuple-element.48), channel_id=1, source_target_pairs={{0,7},{1,0},{2,1},{3,2},{4,3},{5,4},{6,5},{7,6},{8,15},{9,8},{10,9... | collective-permute-start | bytes 49160 | tf_op jit(solution)/shard_map/ppermute | solution.py:116
  30.2 1.1 constant_dynamic-slice_fusion.25
  31.3 20.3 %collective-permute-done.22 = bf16[128,64]{1,0:T(8,128)(2,1)S(1)} collective-permute-done((bf16[128,64]{1,0:T(8,128)(2,1)S(1)}, bf16[128,64]{1,0:T(8,128)(2,1)S(1)}, u32[]{:S(2)}, u32[]{:S(2)}) %collective-permute-start.22) | collective-permute-done | bytes 16416 | tf_op jit(solution)/shard_map/ppermute | solution.py:116
  51.6 29.1 %collective-permute-start.23 = (bf16[128,64]{1,0:T(8,128)(2,1)S(1)}, bf16[128,64]{1,0:T(8,128)(2,1)S(1)}, u32[]{:S(2)}, u32[]{:S(2)}) collective-permute-start(bf16[128,64]{1,0:T(8,128)(2,1)S(1)} %get-tuple-element.47), channel_id=1, source_target_pairs={{0,6},{1,7},{2,0},{3,1},{4,2},{5,3},{6,4},{7,5},{8,14},{9,15},{10,... | collective-permute-start | bytes 49160 | tf_op jit(solution)/shard_map/ppermute | solution.py:116
  80.7 2.7 %collective-permute-done.23 = bf16[128,64]{1,0:T(8,128)(2,1)S(1)} collective-permute-done((bf16[128,64]{1,0:T(8,128)(2,1)S(1)}, bf16[128,64]{1,0:T(8,128)(2,1)S(1)}, u32[]{:S(2)}, u32[]{:S(2)}) %collective-permute-start.23) | collective-permute-done | bytes 16416 | tf_op jit(solution)/shard_map/ppermute | solution.py:116
  83.4 4.1 %collective-permute-start.24 = (bf16[128,64]{1,0:T(8,128)(2,1)S(1)}, bf16[128,64]{1,0:T(8,128)(2,1)S(1)}, u32[]{:S(2)}, u32[]{:S(2)}) collective-permute-start(bf16[128,64]{1,0:T(8,128)(2,1)S(1)} %get-tuple-element.46), channel_id=1, source_target_pairs={{0,5},{1,6},{2,7},{3,0},{4,1},{5,2},{6,3},{7,4},{8,13},{9,14},{10,... | collective-permute-start | bytes 49160 | tf_op jit(solution)/shard_map/ppermute | solution.py:116
  87.5 1.1 collective-permute-done.24
  88.5 2.8 %collective-permute-start.25 = (bf16[128,64]{1,0:T(8,128)(2,1)S(1)}, bf16[128,64]{1,0:T(8,128)(2,1)S(1)}, u32[]{:S(2)}, u32[]{:S(2)}) collective-permute-start(bf16[128,64]{1,0:T(8,128)(2,1)S(1)} %get-tuple-element.45), channel_id=1, source_target_pairs={{0,4},{1,5},{2,6},{3,7},{4,0},{5,1},{6,2},{7,3},{8,12},{9,13},{10,... | collective-permute-start | bytes 49160 | tf_op jit(solution)/shard_map/ppermute | solution.py:116
  91.3 1.5 collective-permute-done.25
  92.8 5.2 %collective-permute-start.26 = (bf16[128,64]{1,0:T(8,128)(2,1)S(1)}, bf16[128,64]{1,0:T(8,128)(2,1)S(1)}, u32[]{:S(2)}, u32[]{:S(2)}) collective-permute-start(bf16[128,64]{1,0:T(8,128)(2,1)S(1)} %get-tuple-element.44), channel_id=1, source_target_pairs={{0,3},{1,4},{2,5},{3,6},{4,7},{5,0},{6,1},{7,2},{8,11},{9,12},{10,... | collective-permute-start | bytes 49160 | tf_op jit(solution)/shard_map/ppermute | solution.py:116
  98.0 1.7 collective-permute-done.26
  99.7 1.7 collective-permute-start.27
  101.4 3.5 %collective-permute-done.27 = bf16[128,64]{1,0:T(8,128)(2,1)S(1)} collective-permute-done((bf16[128,64]{1,0:T(8,128)(2,1)}, bf16[128,64]{1,0:T(8,128)(2,1)S(1)}, u32[]{:S(2)}, u32[]{:S(2)}) %collective-permute-start.27) | collective-permute-done | bytes 16416 | tf_op jit(solution)/shard_map/ppermute | solution.py:116
  104.9 4.3 %collective-permute-start.28 = (bf16[128,64]{1,0:T(8,128)(2,1)S(1)}, bf16[128,64]{1,0:T(8,128)(2,1)S(1)}, u32[]{:S(2)}, u32[]{:S(2)}) collective-permute-start(bf16[128,64]{1,0:T(8,128)(2,1)S(1)} %get-tuple-element.42), channel_id=1, source_target_pairs={{0,1},{1,2},{2,3},{3,4},{4,5},{5,6},{6,7},{7,0},{8,9},{9,10},{10,1... | collective-permute-start | bytes 49160 | tf_op jit(solution)/shard_map/ppermute | solution.py:116
  109.1 2.1 collective-permute-done.28
  111.3 7.9 %collective-permute-start.11 = (bf16[16,1024]{1,0:T(8,128)(2,1)}, bf16[16,1024]{1,0:T(8,128)(2,1)S(1)}, u32[]{:S(2)}, u32[]{:S(2)}) collective-permute-start(bf16[16,1024]{1,0:T(8,128)(2,1)} %get-tuple-element.37), channel_id=1, source_target_pairs={{0,88},{8,96},{16,104},{24,112},{32,120},{40,0},{48,8},{56,16},{64... | collective-permute-start | bytes 98312 | tf_op jit(solution)/shard_map/ppermute | solution.py:104
  119.5 2.8 %collective-permute-start.12 = (bf16[16,1024]{1,0:T(8,128)(2,1)}, bf16[16,1024]{1,0:T(8,128)(2,1)S(1)}, u32[]{:S(2)}, u32[]{:S(2)}) collective-permute-start(bf16[16,1024]{1,0:T(8,128)(2,1)} %get-tuple-element.36), channel_id=1, source_target_pairs={{0,80},{8,88},{16,96},{24,104},{32,112},{40,120},{48,0},{56,8},{64... | collective-permute-start | bytes 98312 | tf_op jit(solution)/shard_map/ppermute | solution.py:104
  122.4 1.7 collective-permute-start.15
  124.1 2.0 collective-permute-start.16
  126.1 0.9 collective-permute-start.17
  127.0 2.0 collective-permute-start.18
  129.0 2.6 %collective-permute-start.19 = (bf16[16,1024]{1,0:T(8,128)(2,1)S(1)}, bf16[16,1024]{1,0:T(8,128)(2,1)S(1)}, u32[]{:S(2)}, u32[]{:S(2)}) collective-permute-start(bf16[16,1024]{1,0:T(8,128)(2,1)S(1)} %get-tuple-element.29), channel_id=1, source_target_pairs={{0,24},{8,32},{16,40},{24,48},{32,56},{40,64},{48,72},{56,80},{64,... | collective-permute-start | bytes 98312 | tf_op jit(solution)/shard_map/ppermute | solution.py:104
  131.7 1.3 collective-permute-start.21
  133.0 2.3 %collective-permute-start = (f32[128,512]{1,0:T(8,128)}, f32[128,512]{1,0:T(8,128)S(1)}, u32[]{:S(2)}, u32[]{:S(2)}) collective-permute-start(f32[128,512]{1,0:T(8,128)} %get-tuple-element.26), channel_id=1, source_target_pairs={{0,7},{1,0},{2,1},{3,2},{4,3},{5,4},{6,5},{7,6},{8,15},{9,8},{10,9... | collective-permute-start | bytes 786440 | tf_op jit(solution)/shard_map/ppermute | solution.py:129
  135.3 2.7 %collective-permute-start.2 = (f32[128,512]{1,0:T(8,128)}, f32[128,512]{1,0:T(8,128)S(1)}, u32[]{:S(2)}, u32[]{:S(2)}) collective-permute-start(f32[128,512]{1,0:T(8,128)} %get-tuple-element.24), channel_id=1, source_target_pairs={{0,5},{1,6},{2,7},{3,0},{4,1},{5,2},{6,3},{7,4},{8,13},{9,14},{10,... | collective-permute-start | bytes 786440 | tf_op jit(solution)/shard_map/ppermute | solution.py:129
  138.0 2.8 %collective-permute-start.3 = (f32[128,512]{1,0:T(8,128)}, f32[128,512]{1,0:T(8,128)S(1)}, u32[]{:S(2)}, u32[]{:S(2)}) collective-permute-start(f32[128,512]{1,0:T(8,128)} %get-tuple-element.23), channel_id=1, source_target_pairs={{0,4},{1,5},{2,6},{3,7},{4,0},{5,1},{6,2},{7,3},{8,12},{9,13},{10,... | collective-permute-start | bytes 786440 | tf_op jit(solution)/shard_map/ppermute | solution.py:129
  140.9 1.4 collective-permute-start.4
  142.3 0.8 constant_dynamic-update-slice_fusion.16
  143.2 0.8 constant_dynamic-update-slice_fusion
  144.3 2.4 %collective-permute-done = f32[128,512]{1,0:T(8,128)S(1)} collective-permute-done((f32[128,512]{1,0:T(8,128)}, f32[128,512]{1,0:T(8,128)S(1)}, u32[]{:S(2)}, u32[]{:S(2)}) %collective-permute-start) | collective-permute-done | bytes 262176 | tf_op jit(solution)/shard_map/ppermute | solution.py:129
  146.7 3.4 %collective-permute-done.1 = f32[128,512]{1,0:T(8,128)S(1)} collective-permute-done((f32[128,512]{1,0:T(8,128)}, f32[128,512]{1,0:T(8,128)S(1)}, u32[]{:S(2)}, u32[]{:S(2)}) %collective-permute-start.1) | collective-permute-done | bytes 262176 | tf_op jit(solution)/shard_map/ppermute | solution.py:129
  150.2 4.0 %collective-permute-done.3 = f32[128,512]{1,0:T(8,128)S(1)} collective-permute-done((f32[128,512]{1,0:T(8,128)}, f32[128,512]{1,0:T(8,128)S(1)}, u32[]{:S(2)}, u32[]{:S(2)}) %collective-permute-start.3) | collective-permute-done | bytes 262176 | tf_op jit(solution)/shard_map/ppermute | solution.py:129
  154.2 1.8 collective-permute-done.4
  156.1 10.3 %collective-permute-done.5 = f32[128,512]{1,0:T(8,128)S(1)} collective-permute-done((f32[128,512]{1,0:T(8,128)S(1)}, f32[128,512]{1,0:T(8,128)S(1)}, u32[]{:S(2)}, u32[]{:S(2)}) %collective-permute-start.5) | collective-permute-done | bytes 262176 | tf_op jit(solution)/shard_map/ppermute | solution.py:129
  166.7 1.6 constant_dynamic-slice_fusion.24
  168.3 6.9 %shard_map.153 = (f32[1024,512]{1,0:T(8,128)}, f32[1024,512]{1,0:T(8,128)}, f32[1024,512]{1,0:T(8,128)}, bf16[1024,512]{1,0:T(8,128)(2,1)}) custom-call(f32[8,256,512]{2,1,0:T(8,128)} %all-to-all-done.state_ref, f32[1024,512]{1,0:T(8,128)} %bitcast.107, f32[1024,512]{1,0:T(8,128)} %grad_ref.1), custom_call_target="tpu_custom_call" | custom-call | tf_op jit(solution)/shard_map/pallas_call | solution.py:46
  175.2 1.7 fusion.3
  176.9 15.9 %all_to_all.20 = f32[16,16,576]{2,1,0:T(8,128)S(1)} all-to-all(f32[16,16,576]{2,1,0:T(8,128)S(1)} %bitcast.110), channel_id=1, replica_groups=mesh['fsdp'=16,'tp'=8] {'fsdp'}, dimensions={0} | all-to-all | bytes 1179648 | tf_op jit(solution)/shard_map/all_to_all | solution.py:83
  193.7 8.5 %all-to-all-start.2 = ((bf16[128,8,128]{2,1,0:T(8,128)(2,1)}), bf16[128,8,128]{2,1,0:T(8,128)(2,1)S(1)}, u32[]{:S(2)}, u32[]{:S(2)}) async-start(bf16[128,8,128]{2,1,0:T(8,128)(2,1)} %broadcast_in_dim.8), calls=%async_computation.2 | async-start | bytes 524288 | tf_op jit(solution)/shard_map/all_to_all | solution.py:79
  202.9 10.0 %all-to-all-done.2 = bf16[128,8,128]{2,1,0:T(8,128)(2,1)S(1)} async-done(((bf16[128,8,128]{2,1,0:T(8,128)(2,1)}), bf16[128,8,128]{2,1,0:T(8,128)(2,1)S(1)}, u32[]{:S(2)}, u32[]{:S(2)}) %all-to-all-start.2) | async-done | bytes 262176 | tf_op jit(solution)/shard_map/all_to_all | solution.py:79
  213.2 1.0 reshape.45
  (111 shorter events, 4.6 us)
Async XLA Ops:
  2.7 116.8 %collective-permute-start.7 = (bf16[16,1024]{1,0:T(8,128)(2,1)}, bf16[16,1024]{1,0:T(8,128)(2,1)S(1)}, u32[]{:S(2)}, u32[]{:S(2)}) collective-permute-start(bf16[16,1024]{1,0:T(8,128)(2,1)} %get-tuple-element.41), channel_id=1, source_target_pairs={{0,120},{8,0},{16,8},{24,16},{32,24},{40,32},{48,40},{56,48},{64,5... | collective-permute-start | bytes 98312 | tf_op jit(solution)/shard_map/ppermute | solution.py:104
  4.1 118.1 %collective-permute-start.8 = (bf16[16,1024]{1,0:T(8,128)(2,1)}, bf16[16,1024]{1,0:T(8,128)(2,1)S(1)}, u32[]{:S(2)}, u32[]{:S(2)}) collective-permute-start(bf16[16,1024]{1,0:T(8,128)(2,1)} %get-tuple-element.40), channel_id=1, source_target_pairs={{0,112},{8,120},{16,0},{24,8},{32,16},{40,24},{48,32},{56,40},{64,... | collective-permute-start | bytes 98312 | tf_op jit(solution)/shard_map/ppermute | solution.py:104
  8.3 113.9 %collective-permute-start.9 = (bf16[16,1024]{1,0:T(8,128)(2,1)}, bf16[16,1024]{1,0:T(8,128)(2,1)S(1)}, u32[]{:S(2)}, u32[]{:S(2)}) collective-permute-start(bf16[16,1024]{1,0:T(8,128)(2,1)} %get-tuple-element.39), channel_id=1, source_target_pairs={{0,104},{8,112},{16,120},{24,0},{32,8},{40,16},{48,24},{56,32},{64... | collective-permute-start | bytes 98312 | tf_op jit(solution)/shard_map/ppermute | solution.py:104
  9.0 113.4 %collective-permute-start.10 = (bf16[16,1024]{1,0:T(8,128)(2,1)}, bf16[16,1024]{1,0:T(8,128)(2,1)S(1)}, u32[]{:S(2)}, u32[]{:S(2)}) collective-permute-start(bf16[16,1024]{1,0:T(8,128)(2,1)} %get-tuple-element.38), channel_id=1, source_target_pairs={{0,96},{8,104},{16,112},{24,120},{32,0},{40,8},{48,16},{56,24},{64... | collective-permute-start | bytes 98312 | tf_op jit(solution)/shard_map/ppermute | solution.py:104
  15.8 7.6 %copy-start.1 = (f32[128,512]{1,0:T(8,128)S(1)}, f32[128,512]{1,0:T(8,128)}, u32[]{:S(2)}) copy-start(f32[128,512]{1,0:T(8,128)} %param.14) | copy-start | bytes 786436
  15.8 7.6 %copy-start.2 = (f32[128,512]{1,0:T(8,128)S(1)}, f32[128,512]{1,0:T(8,128)}, u32[]{:S(2)}) copy-start(f32[128,512]{1,0:T(8,128)} %param.17) | copy-start | bytes 786436
  15.8 7.7 %copy-start.3 = (f32[128,512]{1,0:T(8,128)S(1)}, f32[128,512]{1,0:T(8,128)}, u32[]{:S(2)}) copy-start(f32[128,512]{1,0:T(8,128)} %param.16) | copy-start | bytes 786436
  15.8 7.7 %copy-start.4 = (f32[128,512]{1,0:T(8,128)S(1)}, f32[128,512]{1,0:T(8,128)}, u32[]{:S(2)}) copy-start(f32[128,512]{1,0:T(8,128)} %param.15) | copy-start | bytes 786436
  15.8 14.4 %copy-start = (f32[128,4096]{1,0:T(8,128)S(1)}, f32[128,4096]{1,0:T(8,128)}, u32[]{:S(2)}) copy-start(f32[128,4096]{1,0:T(8,128)} %param.12) | copy-start | bytes 6291460
  15.8 152.5 %all-to-all-start = ((f32[8,256,512]{2,1,0:T(8,128)}), f32[8,256,512]{2,1,0:T(8,128)}, u32[]{:S(2)}, u32[]{:S(2)}) async-start(f32[8,256,512]{2,1,0:T(8,128)} %shard_map.152), calls=%async_computation | async-start | bytes 8388608 | tf_op jit(solution)/shard_map/all_to_all | solution.py:126
  24.4 107.3 %copy-start.5 = (bf16[16,1024]{1,0:T(8,128)(2,1)S(1)}, bf16[16,1024]{1,0:T(8,128)(2,1)}, u32[]{:S(2)}) copy-start(bf16[16,1024]{1,0:T(8,128)(2,1)} %get-tuple-element.27) | copy-start | bytes 98308
  25.2 26.4 %collective-permute-start.22 = (bf16[128,64]{1,0:T(8,128)(2,1)S(1)}, bf16[128,64]{1,0:T(8,128)(2,1)S(1)}, u32[]{:S(2)}, u32[]{:S(2)}) collective-permute-start(bf16[128,64]{1,0:T(8,128)(2,1)S(1)} %get-tuple-element.48), channel_id=1, source_target_pairs={{0,7},{1,0},{2,1},{3,2},{4,3},{5,4},{6,5},{7,6},{8,15},{9,8},{10,9... | collective-permute-start | bytes 49160 | tf_op jit(solution)/shard_map/ppermute | solution.py:116
  51.6 31.8 %collective-permute-start.23 = (bf16[128,64]{1,0:T(8,128)(2,1)S(1)}, bf16[128,64]{1,0:T(8,128)(2,1)S(1)}, u32[]{:S(2)}, u32[]{:S(2)}) collective-permute-start(bf16[128,64]{1,0:T(8,128)(2,1)S(1)} %get-tuple-element.47), channel_id=1, source_target_pairs={{0,6},{1,7},{2,0},{3,1},{4,2},{5,3},{6,4},{7,5},{8,14},{9,15},{10,... | collective-permute-start | bytes 49160 | tf_op jit(solution)/shard_map/ppermute | solution.py:116
  83.4 5.2 %collective-permute-start.24 = (bf16[128,64]{1,0:T(8,128)(2,1)S(1)}, bf16[128,64]{1,0:T(8,128)(2,1)S(1)}, u32[]{:S(2)}, u32[]{:S(2)}) collective-permute-start(bf16[128,64]{1,0:T(8,128)(2,1)S(1)} %get-tuple-element.46), channel_id=1, source_target_pairs={{0,5},{1,6},{2,7},{3,0},{4,1},{5,2},{6,3},{7,4},{8,13},{9,14},{10,... | collective-permute-start | bytes 49160 | tf_op jit(solution)/shard_map/ppermute | solution.py:116
  88.5 4.3 %collective-permute-start.25 = (bf16[128,64]{1,0:T(8,128)(2,1)S(1)}, bf16[128,64]{1,0:T(8,128)(2,1)S(1)}, u32[]{:S(2)}, u32[]{:S(2)}) collective-permute-start(bf16[128,64]{1,0:T(8,128)(2,1)S(1)} %get-tuple-element.45), channel_id=1, source_target_pairs={{0,4},{1,5},{2,6},{3,7},{4,0},{5,1},{6,2},{7,3},{8,12},{9,13},{10,... | collective-permute-start | bytes 49160 | tf_op jit(solution)/shard_map/ppermute | solution.py:116
  92.8 6.9 %collective-permute-start.26 = (bf16[128,64]{1,0:T(8,128)(2,1)S(1)}, bf16[128,64]{1,0:T(8,128)(2,1)S(1)}, u32[]{:S(2)}, u32[]{:S(2)}) collective-permute-start(bf16[128,64]{1,0:T(8,128)(2,1)S(1)} %get-tuple-element.44), channel_id=1, source_target_pairs={{0,3},{1,4},{2,5},{3,6},{4,7},{5,0},{6,1},{7,2},{8,11},{9,12},{10,... | collective-permute-start | bytes 49160 | tf_op jit(solution)/shard_map/ppermute | solution.py:116
  99.7 5.2 %collective-permute-start.27 = (bf16[128,64]{1,0:T(8,128)(2,1)}, bf16[128,64]{1,0:T(8,128)(2,1)S(1)}, u32[]{:S(2)}, u32[]{:S(2)}) collective-permute-start(bf16[128,64]{1,0:T(8,128)(2,1)} %get-tuple-element.43), channel_id=1, source_target_pairs={{0,2},{1,3},{2,4},{3,5},{4,6},{5,7},{6,0},{7,1},{8,10},{9,11},{10,... | collective-permute-start | bytes 49160 | tf_op jit(solution)/shard_map/ppermute | solution.py:116
  104.9 6.4 %collective-permute-start.28 = (bf16[128,64]{1,0:T(8,128)(2,1)S(1)}, bf16[128,64]{1,0:T(8,128)(2,1)S(1)}, u32[]{:S(2)}, u32[]{:S(2)}) collective-permute-start(bf16[128,64]{1,0:T(8,128)(2,1)S(1)} %get-tuple-element.42), channel_id=1, source_target_pairs={{0,1},{1,2},{2,3},{3,4},{4,5},{5,6},{6,7},{7,0},{8,9},{9,10},{10,1... | collective-permute-start | bytes 49160 | tf_op jit(solution)/shard_map/ppermute | solution.py:116
  111.3 12.9 %collective-permute-start.11 = (bf16[16,1024]{1,0:T(8,128)(2,1)}, bf16[16,1024]{1,0:T(8,128)(2,1)S(1)}, u32[]{:S(2)}, u32[]{:S(2)}) collective-permute-start(bf16[16,1024]{1,0:T(8,128)(2,1)} %get-tuple-element.37), channel_id=1, source_target_pairs={{0,88},{8,96},{16,104},{24,112},{32,120},{40,0},{48,8},{56,16},{64... | collective-permute-start | bytes 98312 | tf_op jit(solution)/shard_map/ppermute | solution.py:104
  119.5 6.6 %collective-permute-start.12 = (bf16[16,1024]{1,0:T(8,128)(2,1)}, bf16[16,1024]{1,0:T(8,128)(2,1)S(1)}, u32[]{:S(2)}, u32[]{:S(2)}) collective-permute-start(bf16[16,1024]{1,0:T(8,128)(2,1)} %get-tuple-element.36), channel_id=1, source_target_pairs={{0,80},{8,88},{16,96},{24,104},{32,112},{40,120},{48,0},{56,8},{64... | collective-permute-start | bytes 98312 | tf_op jit(solution)/shard_map/ppermute | solution.py:104
  122.2 4.8 %collective-permute-start.13 = (bf16[16,1024]{1,0:T(8,128)(2,1)}, bf16[16,1024]{1,0:T(8,128)(2,1)S(1)}, u32[]{:S(2)}, u32[]{:S(2)}) collective-permute-start(bf16[16,1024]{1,0:T(8,128)(2,1)} %get-tuple-element.35), channel_id=1, source_target_pairs={{0,72},{8,80},{16,88},{24,96},{32,104},{40,112},{48,120},{56,0},{6... | collective-permute-start | bytes 98312 | tf_op jit(solution)/shard_map/ppermute | solution.py:104
  122.3 6.8 %collective-permute-start.14 = (bf16[16,1024]{1,0:T(8,128)(2,1)}, bf16[16,1024]{1,0:T(8,128)(2,1)S(1)}, u32[]{:S(2)}, u32[]{:S(2)}) collective-permute-start(bf16[16,1024]{1,0:T(8,128)(2,1)} %get-tuple-element.34), channel_id=1, source_target_pairs={{0,64},{8,72},{16,80},{24,88},{32,96},{40,104},{48,112},{56,120},{... | collective-permute-start | bytes 98312 | tf_op jit(solution)/shard_map/ppermute | solution.py:104
  122.4 9.3 %collective-permute-start.15 = (bf16[16,1024]{1,0:T(8,128)(2,1)}, bf16[16,1024]{1,0:T(8,128)(2,1)S(1)}, u32[]{:S(2)}, u32[]{:S(2)}) collective-permute-start(bf16[16,1024]{1,0:T(8,128)(2,1)} %get-tuple-element.33), channel_id=1, source_target_pairs={{0,56},{8,64},{16,72},{24,80},{32,88},{40,96},{48,104},{56,112},{6... | collective-permute-start | bytes 98312 | tf_op jit(solution)/shard_map/ppermute | solution.py:104
  124.1 7.5 %collective-permute-start.16 = (bf16[16,1024]{1,0:T(8,128)(2,1)}, bf16[16,1024]{1,0:T(8,128)(2,1)S(1)}, u32[]{:S(2)}, u32[]{:S(2)}) collective-permute-start(bf16[16,1024]{1,0:T(8,128)(2,1)} %get-tuple-element.32), channel_id=1, source_target_pairs={{0,48},{8,56},{16,64},{24,72},{32,80},{40,88},{48,96},{56,104},{64... | collective-permute-start | bytes 98312 | tf_op jit(solution)/shard_map/ppermute | solution.py:104
  126.1 6.8 %collective-permute-start.17 = (bf16[16,1024]{1,0:T(8,128)(2,1)S(1)}, bf16[16,1024]{1,0:T(8,128)(2,1)S(1)}, u32[]{:S(2)}, u32[]{:S(2)}) collective-permute-start(bf16[16,1024]{1,0:T(8,128)(2,1)S(1)} %get-tuple-element.31), channel_id=1, source_target_pairs={{0,40},{8,48},{16,56},{24,64},{32,72},{40,80},{48,88},{56,96},{64,... | collective-permute-start | bytes 98312 | tf_op jit(solution)/shard_map/ppermute | solution.py:104
  127.0 8.2 %collective-permute-start.18 = (bf16[16,1024]{1,0:T(8,128)(2,1)S(1)}, bf16[16,1024]{1,0:T(8,128)(2,1)S(1)}, u32[]{:S(2)}, u32[]{:S(2)}) collective-permute-start(bf16[16,1024]{1,0:T(8,128)(2,1)S(1)} %get-tuple-element.30), channel_id=1, source_target_pairs={{0,32},{8,40},{16,48},{24,56},{32,64},{40,72},{48,80},{56,88},{64,... | collective-permute-start | bytes 98312 | tf_op jit(solution)/shard_map/ppermute | solution.py:104
  129.0 6.3 %collective-permute-start.19 = (bf16[16,1024]{1,0:T(8,128)(2,1)S(1)}, bf16[16,1024]{1,0:T(8,128)(2,1)S(1)}, u32[]{:S(2)}, u32[]{:S(2)}) collective-permute-start(bf16[16,1024]{1,0:T(8,128)(2,1)S(1)} %get-tuple-element.29), channel_id=1, source_target_pairs={{0,24},{8,32},{16,40},{24,48},{32,56},{40,64},{48,72},{56,80},{64,... | collective-permute-start | bytes 98312 | tf_op jit(solution)/shard_map/ppermute | solution.py:104
  131.6 6.4 %collective-permute-start.20 = (bf16[16,1024]{1,0:T(8,128)(2,1)S(1)}, bf16[16,1024]{1,0:T(8,128)(2,1)S(1)}, u32[]{:S(2)}, u32[]{:S(2)}) collective-permute-start(bf16[16,1024]{1,0:T(8,128)(2,1)S(1)} %get-tuple-element.28), channel_id=1, source_target_pairs={{0,16},{8,24},{16,32},{24,40},{32,48},{40,56},{48,64},{56,72},{64,... | collective-permute-start | bytes 98312 | tf_op jit(solution)/shard_map/ppermute | solution.py:104
  131.7 9.2 %collective-permute-start.21 = (bf16[16,1024]{1,0:T(8,128)(2,1)S(1)}, bf16[16,1024]{1,0:T(8,128)(2,1)S(1)}, u32[]{:S(2)}, u32[]{:S(2)}) collective-permute-start(bf16[16,1024]{1,0:T(8,128)(2,1)S(1)} %copy-done.5), channel_id=1, source_target_pairs={{0,8},{8,16},{16,24},{24,32},{32,40},{40,48},{48,56},{56,64},{64,7... | collective-permute-start | bytes 98312 | tf_op jit(solution)/shard_map/ppermute | solution.py:104
  133.0 13.7 %collective-permute-start = (f32[128,512]{1,0:T(8,128)}, f32[128,512]{1,0:T(8,128)S(1)}, u32[]{:S(2)}, u32[]{:S(2)}) collective-permute-start(f32[128,512]{1,0:T(8,128)} %get-tuple-element.26), channel_id=1, source_target_pairs={{0,7},{1,0},{2,1},{3,2},{4,3},{5,4},{6,5},{7,6},{8,15},{9,8},{10,9... | collective-permute-start | bytes 786440 | tf_op jit(solution)/shard_map/ppermute | solution.py:129
  135.3 14.9 %collective-permute-start.1 = (f32[128,512]{1,0:T(8,128)}, f32[128,512]{1,0:T(8,128)S(1)}, u32[]{:S(2)}, u32[]{:S(2)}) collective-permute-start(f32[128,512]{1,0:T(8,128)} %get-tuple-element.25), channel_id=1, source_target_pairs={{0,6},{1,7},{2,0},{3,1},{4,2},{5,3},{6,4},{7,5},{8,14},{9,15},{10,... | collective-permute-start | bytes 786440 | tf_op jit(solution)/shard_map/ppermute | solution.py:129
  135.3 14.9 %collective-permute-start.2 = (f32[128,512]{1,0:T(8,128)}, f32[128,512]{1,0:T(8,128)S(1)}, u32[]{:S(2)}, u32[]{:S(2)}) collective-permute-start(f32[128,512]{1,0:T(8,128)} %get-tuple-element.24), channel_id=1, source_target_pairs={{0,5},{1,6},{2,7},{3,0},{4,1},{5,2},{6,3},{7,4},{8,13},{9,14},{10,... | collective-permute-start | bytes 786440 | tf_op jit(solution)/shard_map/ppermute | solution.py:129
  138.0 16.2 %collective-permute-start.3 = (f32[128,512]{1,0:T(8,128)}, f32[128,512]{1,0:T(8,128)S(1)}, u32[]{:S(2)}, u32[]{:S(2)}) collective-permute-start(f32[128,512]{1,0:T(8,128)} %get-tuple-element.23), channel_id=1, source_target_pairs={{0,4},{1,5},{2,6},{3,7},{4,0},{5,1},{6,2},{7,3},{8,12},{9,13},{10,... | collective-permute-start | bytes 786440 | tf_op jit(solution)/shard_map/ppermute | solution.py:129
  140.9 15.2 %collective-permute-start.4 = (f32[128,512]{1,0:T(8,128)S(1)}, f32[128,512]{1,0:T(8,128)S(1)}, u32[]{:S(2)}, u32[]{:S(2)}) collective-permute-start(f32[128,512]{1,0:T(8,128)S(1)} %get-tuple-element.22), channel_id=1, source_target_pairs={{0,3},{1,4},{2,5},{3,6},{4,7},{5,0},{6,1},{7,2},{8,11},{9,12},{10,... | collective-permute-start | bytes 786440 | tf_op jit(solution)/shard_map/ppermute | solution.py:129
  146.7 19.6 %collective-permute-start.5 = (f32[128,512]{1,0:T(8,128)S(1)}, f32[128,512]{1,0:T(8,128)S(1)}, u32[]{:S(2)}, u32[]{:S(2)}) collective-permute-start(f32[128,512]{1,0:T(8,128)S(1)} %get-tuple-element.21), channel_id=1, source_target_pairs={{0,2},{1,3},{2,4},{3,5},{4,6},{5,7},{6,0},{7,1},{8,10},{9,11},{10,... | collective-permute-start | bytes 786440 | tf_op jit(solution)/shard_map/ppermute | solution.py:129
  150.2 16.2 %collective-permute-start.6 = (f32[128,512]{1,0:T(8,128)S(1)}, f32[128,512]{1,0:T(8,128)S(1)}, u32[]{:S(2)}, u32[]{:S(2)}) collective-permute-start(f32[128,512]{1,0:T(8,128)S(1)} %get-tuple-element.20), channel_id=1, source_target_pairs={{0,1},{1,2},{2,3},{3,4},{4,5},{5,6},{6,7},{7,0},{8,9},{9,10},{10,1... | collective-permute-start | bytes 786440 | tf_op jit(solution)/shard_map/ppermute | solution.py:129
  193.7 19.1 %all-to-all-start.2 = ((bf16[128,8,128]{2,1,0:T(8,128)(2,1)}), bf16[128,8,128]{2,1,0:T(8,128)(2,1)S(1)}, u32[]{:S(2)}, u32[]{:S(2)}) async-start(bf16[128,8,128]{2,1,0:T(8,128)(2,1)} %broadcast_in_dim.8), calls=%async_computation.2 | async-start | bytes 524288 | tf_op jit(solution)/shard_map/all_to_all | solution.py:79

commit v10 on v8

--- a/solution.py
+++ b/solution.py
@@ -22,8 +22,13 @@
     return (master - LEARN_RATE * update, first_new, second_new)
 
 
-def adam_kernel(state_ref, grad_ref, master_out, first_out, second_out, low_out):
+def adam_kernel(state_ref, grad_ref, columns_ref, master_out, first_out, second_out, low_out, q_out):
     per, rows = state_ref.shape[0], grad_ref.shape[0] // state_ref.shape[0]
+
+    @pl.when(pl.program_id(0) == 0)
+    def _():
+        q_out[...] = jnp.zeros_like(q_out)
+
     for j in range(per):
         out = pl.ds(j * rows, rows)
         new, first_new, second_new = adam_step(
@@ -35,10 +40,12 @@
         master_out[out, :] = new
         first_out[out, :] = first_new
         second_out[out, :] = second_new
-        low_out[out, :] = new.astype(low_out.dtype)
+        low = new.astype(low_out.dtype)
+        low_out[out, :] = low
+        q_out[...] += jnp.dot(columns_ref[:, out], low, preferred_element_type=jnp.float32)
 
 
-def adam_from_blocks(state, grad, per=2):
+def adam_from_blocks(state, grad, columns, per=2):
     sources, stacked, cols = state.shape
     rows = stacked // 3
     block = pl.BlockSpec((per * rows, cols), lambda i: (i, 0))
@@ -46,10 +53,15 @@
     return pl.pallas_call(
         adam_kernel,
         grid=(sources // per,),
-        in_specs=[pl.BlockSpec((per, stacked, cols), lambda i: (i, 0, 0)), block],
-        out_specs=[block] * 4,
-        out_shape=[f32, f32, f32, jax.ShapeDtypeStruct(grad.shape, jnp.bfloat16)],
-    )(state, grad)
+        in_specs=[
+            pl.BlockSpec((per, stacked, cols), lambda i: (i, 0, 0)),
+            block,
+            pl.BlockSpec((columns.shape[0], per * rows), lambda i: (0, i)),
+        ],
+        out_specs=[block] * 4 + [pl.BlockSpec((columns.shape[0], cols), lambda i: (0, 0))],
+        out_shape=[f32, f32, f32, jax.ShapeDtypeStruct(grad.shape, jnp.bfloat16),
+                   jax.ShapeDtypeStruct((columns.shape[0], cols), jnp.float32)],
+    )(state, grad, columns)
 
 
 def pack_kernel(master_ref, first_ref, second_ref, out_ref):
@@ -120,15 +132,15 @@
 
     send = pack_by_destination(wq_master, wq_first, wq_second, tp)
     state = lax.all_to_all(send, "tp", split_axis=0, concat_axis=0, tiled=True)
-    wq_new, wq_mom, wq_var, wq_low = adam_from_blocks(state, wq_grad)
-    q_term = jnp.dot(columns, wq_low, preferred_element_type=jnp.float32)
+    wq_new, wq_mom, wq_var, _, q_term = adam_from_blocks(state, wq_grad, columns)
 
     sums = scatter_sum_rows(jnp.concatenate([q_term, kv_term], axis=1), "fsdp", fsdp)
     q_cols = q_term.shape[1]
     probe_query = sums[:, :q_cols].astype(jnp.bfloat16)
     kv_block = sums[:, q_cols:].astype(jnp.bfloat16)
-    kv_all = gather_rows(kv_block, ("fsdp", "tp"), fsdp * tp)
     tokens = kv_block.shape[0]
+    lanes = 128
+    kv_all = gather_rows(kv_block.reshape(tokens * slice_kv // lanes, lanes), ("fsdp", "tp"), fsdp * tp)
     kv_all = kv_all.reshape(fsdp, tp, tokens, slice_kv).transpose(0, 2, 1, 3)
     probe_keyvalue = kv_all.reshape(fsdp * tokens, tp * slice_kv)
     return (wq_new, wq_mom, wq_var, wkv_new, wkv_mom, wkv_var, probe_query, probe_keyvalue)

time: 203 us -> 203 us (level)
  no operation moved by 1% of the time
where the time goes in v10:
time: 203 us
  starting transfers between devices  112 us (55%)
  waiting for transfers between devices  54.8 us (27%)
  blocking collectives  15.3 us (8%)
  Pallas kernels  13.2 us (7%)
  local copies, waits for them, and re-layouts  4.1 us (2%)
  other arithmetic  2.1 us (1%)
    ppermute x7, starting transfers between devices, step(): lax.ppermute(block, 'tp', [(i, (i + k) % tp) for i in range(tp)])  65.1 us
    ppermute x7, waiting for transfers between devices, step(): lax.ppermute(block, 'tp', [(i, (i + k) % tp) for i in range(tp)])  41.7 us
    ppermute x15, starting transfers between devices, step(): lax.ppermute(block, 'fsdp', [(i, (i + k) % fsdp) for i in range(fsdp)])  32.1 us
    all_to_all x1, blocking collectives, scatter_sum_rows(): lax.all_to_all(x, axis_name, split_axis=0, concat_axis=0, tiled=True)  15.3 us
    all_to_all x1, waiting for transfers between devices, gather_rows(): lax.all_to_all(copies, axis_name, split_axis=0, concat_axis=0, tiled=True)  9.97 us
    all_to_all x1, starting transfers between devices, step(): state = lax.all_to_all(send, 'tp', split_axis=0, concat_axis=0, tiled=True)  8.29 us
    pallas_call x1, Pallas kernels, adam_from_blocks(): pl.pallas_call(adam_kernel, grid=(sources // per,), in_specs=[pl.BlockSpe...  7.37 us
    all_to_all x1, starting transfers between devices, gather_rows(): lax.all_to_all(copies, axis_name, split_axis=0, concat_axis=0, tiled=True)  6.07 us
  transfers between devices with their start and end apart: 24, of which 10 were waited for; matrix products, arithmetic and copies ran while one was open for 1% of the time, Pallas kernels for 0%

profile of v10, /device:TPU:1, one launch (start us, length us, event | category | flops | bytes accessed | tf_op | source)
XLA Modules:
  0.0 202.6 jit_solution(15346832306240343835)
XLA Ops:
  0.6 5.9 %shard_map.152 = f32[8,384,512]{2,1,0:T(8,128)} custom-call(f32[128,4096]{1,0:T(8,128)} %master_ref.1, f32[128,4096]{1,0:T(8,128)} %first_ref.1, f32[128,4096]{1,0:T(8,128)} %second_ref.1), custom_call_target="tpu_custom_call" | custom-call | tf_op jit(solution)/shard_map/pallas_call | solution.py:79
  6.5 8.3 %all-to-all-start = ((f32[8,384,512]{2,1,0:T(8,128)}), f32[8,384,512]{2,1,0:T(8,128)}, u32[]{:S(2)}, u32[]{:S(2)}) async-start(f32[8,384,512]{2,1,0:T(8,128)} %shard_map.152), calls=%async_computation | async-start | bytes 12582912 | tf_op jit(solution)/shard_map/all_to_all | solution.py:134
  15.0 1.0 fusion.1
  15.9 0.1 constant_dynamic-slice_fusion.1
  16.1 5.0 %collective-permute-start.15 = (bf16[128,64]{1,0:T(8,128)(2,1)S(1)}, bf16[128,64]{1,0:T(8,128)(2,1)S(1)}, u32[]{:S(2)}, u32[]{:S(2)}) collective-permute-start(bf16[128,64]{1,0:T(8,128)(2,1)S(1)} %get-tuple-element.41), channel_id=1, source_target_pairs={{0,7},{1,0},{2,1},{3,2},{4,3},{5,4},{6,5},{7,6},{8,15},{9,8},{10,9... | collective-permute-start | bytes 49160 | tf_op jit(solution)/shard_map/ppermute | solution.py:127
  21.1 1.6 collective-permute-start
  22.7 3.2 %collective-permute-start.1 = (bf16[16,1024]{1,0:T(8,128)(2,1)S(1)}, bf16[16,1024]{1,0:T(8,128)(2,1)S(1)}, u32[]{:S(2)}, u32[]{:S(2)}) collective-permute-start(bf16[16,1024]{1,0:T(8,128)(2,1)S(1)} %get-tuple-element.33), channel_id=1, source_target_pairs={{0,112},{8,120},{16,0},{24,8},{32,16},{40,24},{48,32},{56,40},{64,... | collective-permute-start | bytes 98312 | tf_op jit(solution)/shard_map/ppermute | solution.py:115
  25.9 0.7 collective-permute-start.2
  26.6 2.0 %collective-permute-start.3 = (bf16[16,1024]{1,0:T(8,128)(2,1)S(1)}, bf16[16,1024]{1,0:T(8,128)(2,1)S(1)}, u32[]{:S(2)}, u32[]{:S(2)}) collective-permute-start(bf16[16,1024]{1,0:T(8,128)(2,1)S(1)} %get-tuple-element.31), channel_id=1, source_target_pairs={{0,96},{8,104},{16,112},{24,120},{32,0},{40,8},{48,16},{56,24},{64... | collective-permute-start | bytes 98312 | tf_op jit(solution)/shard_map/ppermute | solution.py:115
  28.7 29.0 %collective-permute-done.15 = bf16[128,64]{1,0:T(8,128)(2,1)S(1)} collective-permute-done((bf16[128,64]{1,0:T(8,128)(2,1)S(1)}, bf16[128,64]{1,0:T(8,128)(2,1)S(1)}, u32[]{:S(2)}, u32[]{:S(2)}) %collective-permute-start.15) | collective-permute-done | bytes 16416 | tf_op jit(solution)/shard_map/ppermute | solution.py:127
  57.6 42.3 %collective-permute-start.16 = (bf16[128,64]{1,0:T(8,128)(2,1)S(1)}, bf16[128,64]{1,0:T(8,128)(2,1)S(1)}, u32[]{:S(2)}, u32[]{:S(2)}) collective-permute-start(bf16[128,64]{1,0:T(8,128)(2,1)S(1)} %get-tuple-element.40), channel_id=1, source_target_pairs={{0,6},{1,7},{2,0},{3,1},{4,2},{5,3},{6,4},{7,5},{8,14},{9,15},{10,... | collective-permute-start | bytes 49160 | tf_op jit(solution)/shard_map/ppermute | solution.py:127
  100.0 2.7 %collective-permute-done.16 = bf16[128,64]{1,0:T(8,128)(2,1)S(1)} collective-permute-done((bf16[128,64]{1,0:T(8,128)(2,1)S(1)}, bf16[128,64]{1,0:T(8,128)(2,1)S(1)}, u32[]{:S(2)}, u32[]{:S(2)}) %collective-permute-start.16) | collective-permute-done | bytes 16416 | tf_op jit(solution)/shard_map/ppermute | solution.py:127
  102.7 4.1 %collective-permute-start.17 = (bf16[128,64]{1,0:T(8,128)(2,1)S(1)}, bf16[128,64]{1,0:T(8,128)(2,1)S(1)}, u32[]{:S(2)}, u32[]{:S(2)}) collective-permute-start(bf16[128,64]{1,0:T(8,128)(2,1)S(1)} %get-tuple-element.39), channel_id=1, source_target_pairs={{0,5},{1,6},{2,7},{3,0},{4,1},{5,2},{6,3},{7,4},{8,13},{9,14},{10,... | collective-permute-start | bytes 49160 | tf_op jit(solution)/shard_map/ppermute | solution.py:127
  106.8 1.1 collective-permute-done.17
  107.9 2.8 %collective-permute-start.18 = (bf16[128,64]{1,0:T(8,128)(2,1)S(1)}, bf16[128,64]{1,0:T(8,128)(2,1)S(1)}, u32[]{:S(2)}, u32[]{:S(2)}) collective-permute-start(bf16[128,64]{1,0:T(8,128)(2,1)S(1)} %get-tuple-element.38), channel_id=1, source_target_pairs={{0,4},{1,5},{2,6},{3,7},{4,0},{5,1},{6,2},{7,3},{8,12},{9,13},{10,... | collective-permute-start | bytes 49160 | tf_op jit(solution)/shard_map/ppermute | solution.py:127
  110.6 1.5 collective-permute-done.18
  112.1 5.2 %collective-permute-start.19 = (bf16[128,64]{1,0:T(8,128)(2,1)S(1)}, bf16[128,64]{1,0:T(8,128)(2,1)S(1)}, u32[]{:S(2)}, u32[]{:S(2)}) collective-permute-start(bf16[128,64]{1,0:T(8,128)(2,1)S(1)} %get-tuple-element.37), channel_id=1, source_target_pairs={{0,3},{1,4},{2,5},{3,6},{4,7},{5,0},{6,1},{7,2},{8,11},{9,12},{10,... | collective-permute-start | bytes 49160 | tf_op jit(solution)/shard_map/ppermute | solution.py:127
  117.3 1.8 collective-permute-done.19
  119.1 1.5 collective-permute-start.20
  120.7 3.4 %collective-permute-done.20 = bf16[128,64]{1,0:T(8,128)(2,1)S(1)} collective-permute-done((bf16[128,64]{1,0:T(8,128)(2,1)S(1)}, bf16[128,64]{1,0:T(8,128)(2,1)S(1)}, u32[]{:S(2)}, u32[]{:S(2)}) %collective-permute-start.20) | collective-permute-done | bytes 16416 | tf_op jit(solution)/shard_map/ppermute | solution.py:127
  124.1 4.1 %collective-permute-start.21 = (bf16[128,64]{1,0:T(8,128)(2,1)S(1)}, bf16[128,64]{1,0:T(8,128)(2,1)S(1)}, u32[]{:S(2)}, u32[]{:S(2)}) collective-permute-start(bf16[128,64]{1,0:T(8,128)(2,1)S(1)} %get-tuple-element.35), channel_id=1, source_target_pairs={{0,1},{1,2},{2,3},{3,4},{4,5},{5,6},{6,7},{7,0},{8,9},{9,10},{10,1... | collective-permute-start | bytes 49160 | tf_op jit(solution)/shard_map/ppermute | solution.py:127
  128.2 2.2 %collective-permute-done.21 = bf16[128,64]{1,0:T(8,128)(2,1)S(1)} collective-permute-done((bf16[128,64]{1,0:T(8,128)(2,1)S(1)}, bf16[128,64]{1,0:T(8,128)(2,1)S(1)}, u32[]{:S(2)}, u32[]{:S(2)}) %collective-permute-start.21) | collective-permute-done | bytes 16416 | tf_op jit(solution)/shard_map/ppermute | solution.py:127
  130.5 12.0 %collective-permute-start.4 = (bf16[16,1024]{1,0:T(8,128)(2,1)S(1)}, bf16[16,1024]{1,0:T(8,128)(2,1)S(1)}, u32[]{:S(2)}, u32[]{:S(2)}) collective-permute-start(bf16[16,1024]{1,0:T(8,128)(2,1)S(1)} %get-tuple-element.30), channel_id=1, source_target_pairs={{0,88},{8,96},{16,104},{24,112},{32,120},{40,0},{48,8},{56,16},{64... | collective-permute-start | bytes 98312 | tf_op jit(solution)/shard_map/ppermute | solution.py:115
  142.5 0.1 constant_dynamic-update-slice_fusion.40
  142.7 0.1 constant_dynamic-update-slice_fusion.32
  142.9 2.3 %collective-permute-start.5 = (bf16[16,1024]{1,0:T(8,128)(2,1)S(1)}, bf16[16,1024]{1,0:T(8,128)(2,1)S(1)}, u32[]{:S(2)}, u32[]{:S(2)}) collective-permute-start(bf16[16,1024]{1,0:T(8,128)(2,1)S(1)} %get-tuple-element.29), channel_id=1, source_target_pairs={{0,80},{8,88},{16,96},{24,104},{32,112},{40,120},{48,0},{56,8},{64... | collective-permute-start | bytes 98312 | tf_op jit(solution)/shard_map/ppermute | solution.py:115
  145.2 0.8 collective-permute-start.7
  146.0 1.9 collective-permute-start.8
  148.0 0.7 collective-permute-start.9
  148.7 1.4 collective-permute-start.10
  150.1 1.7 collective-permute-start.11
  151.8 2.1 %collective-permute-start.12 = (bf16[16,1024]{1,0:T(8,128)(2,1)S(1)}, bf16[16,1024]{1,0:T(8,128)(2,1)S(1)}, u32[]{:S(2)}, u32[]{:S(2)}) collective-permute-start(bf16[16,1024]{1,0:T(8,128)(2,1)S(1)} %get-tuple-element.22), channel_id=1, source_target_pairs={{0,24},{8,32},{16,40},{24,48},{32,56},{40,64},{48,72},{56,80},{64,... | collective-permute-start | bytes 98312 | tf_op jit(solution)/shard_map/ppermute | solution.py:115
  153.9 1.7 collective-permute-start.14
  155.6 2.0 collective-permute-done.12
  157.5 1.2 collective-permute-done.13
  159.0 0.3 fusion.3
  159.4 0.5 copy-done
  159.9 7.4 %shard_map.153 = (f32[1024,512]{1,0:T(8,128)}, f32[1024,512]{1,0:T(8,128)}, f32[1024,512]{1,0:T(8,128)}, bf16[1024,512]{1,0:T(8,128)(2,1)}, f32[256,512]{1,0:T(8,128)}) custom-call(f32[8,384,512]{2,1,0:T(8,128)} %all-to-all-done.state_ref, f32[1024,512]{1,0:T(8,128)} %grad_ref.1, bf16[256,1024]{1,0:T(8,128)(2,1)} %bitcast.81), custom_call_target="tpu_custom_call" | custom-call | tf_op jit(solution)/shard_map/pallas_call | solution.py:53
  167.2 1.1 pad_maximum_fusion
  168.3 15.3 %all_to_all.20 = f32[16,16,576]{2,1,0:T(8,128)S(1)} all-to-all(f32[16,16,576]{2,1,0:T(8,128)S(1)} %bitcast.82), channel_id=1, replica_groups=mesh['fsdp'=16,'tp'=8] {'fsdp'}, dimensions={0} | all-to-all | bytes 1179648 | tf_op jit(solution)/shard_map/all_to_all | solution.py:94
  183.7 0.1 broadcast_in_dim.7
  183.7 0.7 broadcast_in_dim.8
  184.5 6.1 %all-to-all-start.2 = ((bf16[128,8,128]{2,1,0:T(8,128)(2,1)}), bf16[128,8,128]{2,1,0:T(8,128)(2,1)S(1)}, u32[]{:S(2)}, u32[]{:S(2)}) async-start(bf16[128,8,128]{2,1,0:T(8,128)(2,1)} %broadcast_in_dim.8), calls=%async_computation.2 | async-start | bytes 524288 | tf_op jit(solution)/shard_map/all_to_all | solution.py:90
  190.6 0.6 slice.10
  191.2 10.0 %all-to-all-done.2 = bf16[128,8,128]{2,1,0:T(8,128)(2,1)S(1)} async-done(((bf16[128,8,128]{2,1,0:T(8,128)(2,1)}), bf16[128,8,128]{2,1,0:T(8,128)(2,1)S(1)}, u32[]{:S(2)}, u32[]{:S(2)}) %all-to-all-start.2) | async-done | bytes 262176 | tf_op jit(solution)/shard_map/all_to_all | solution.py:90
  201.1 0.2 reshape.40
  201.4 0.1 copy.20
  201.5 1.0 reshape.41
  (78 shorter events, 0.5 us)
Async XLA Ops:
  6.5 8.4 %copy-start.2 = (f32[128,512]{1,0:T(8,128)S(1)}, f32[128,512]{1,0:T(8,128)}, u32[]{:S(2)}) copy-start(f32[128,512]{1,0:T(8,128)} %param.14) | copy-start | bytes 786436
  6.5 8.4 %copy-start.3 = (f32[128,512]{1,0:T(8,128)S(1)}, f32[128,512]{1,0:T(8,128)}, u32[]{:S(2)}) copy-start(f32[128,512]{1,0:T(8,128)} %param.17) | copy-start | bytes 786436
  6.5 8.4 %copy-start.4 = (f32[128,512]{1,0:T(8,128)S(1)}, f32[128,512]{1,0:T(8,128)}, u32[]{:S(2)}) copy-start(f32[128,512]{1,0:T(8,128)} %param.16) | copy-start | bytes 786436
  6.5 8.4 %copy-start.5 = (f32[128,512]{1,0:T(8,128)S(1)}, f32[128,512]{1,0:T(8,128)}, u32[]{:S(2)}) copy-start(f32[128,512]{1,0:T(8,128)} %param.15) | copy-start | bytes 786436
  6.5 152.8 %all-to-all-start = ((f32[8,384,512]{2,1,0:T(8,128)}), f32[8,384,512]{2,1,0:T(8,128)}, u32[]{:S(2)}, u32[]{:S(2)}) async-start(f32[8,384,512]{2,1,0:T(8,128)} %shard_map.152), calls=%async_computation | async-start | bytes 12582912 | tf_op jit(solution)/shard_map/all_to_all | solution.py:134
  14.8 6.3 %copy-start.1 = (bf16[16,16384]{1,0:T(8,128)(2,1)S(1)}, bf16[16,16384]{1,0:T(8,128)(2,1)}, u32[]{:S(2)}) copy-start(bf16[16,16384]{1,0:T(8,128)(2,1)} %param.9) | copy-start | bytes 1572868
  16.1 41.6 %collective-permute-start.15 = (bf16[128,64]{1,0:T(8,128)(2,1)S(1)}, bf16[128,64]{1,0:T(8,128)(2,1)S(1)}, u32[]{:S(2)}, u32[]{:S(2)}) collective-permute-start(bf16[128,64]{1,0:T(8,128)(2,1)S(1)} %get-tuple-element.41), channel_id=1, source_target_pairs={{0,7},{1,0},{2,1},{3,2},{4,3},{5,4},{6,5},{7,6},{8,15},{9,8},{10,9... | collective-permute-start | bytes 49160 | tf_op jit(solution)/shard_map/ppermute | solution.py:127
  21.1 121.7 %collective-permute-start = (bf16[16,1024]{1,0:T(8,128)(2,1)S(1)}, bf16[16,1024]{1,0:T(8,128)(2,1)S(1)}, u32[]{:S(2)}, u32[]{:S(2)}) collective-permute-start(bf16[16,1024]{1,0:T(8,128)(2,1)S(1)} %get-tuple-element.34), channel_id=1, source_target_pairs={{0,120},{8,0},{16,8},{24,16},{32,24},{40,32},{48,40},{56,48},{64,5... | collective-permute-start | bytes 98312 | tf_op jit(solution)/shard_map/ppermute | solution.py:115
  22.7 122.4 %collective-permute-start.1 = (bf16[16,1024]{1,0:T(8,128)(2,1)S(1)}, bf16[16,1024]{1,0:T(8,128)(2,1)S(1)}, u32[]{:S(2)}, u32[]{:S(2)}) collective-permute-start(bf16[16,1024]{1,0:T(8,128)(2,1)S(1)} %get-tuple-element.33), channel_id=1, source_target_pairs={{0,112},{8,120},{16,0},{24,8},{32,16},{40,24},{48,32},{56,40},{64,... | collective-permute-start | bytes 98312 | tf_op jit(solution)/shard_map/ppermute | solution.py:115
  25.9 119.3 %collective-permute-start.2 = (bf16[16,1024]{1,0:T(8,128)(2,1)S(1)}, bf16[16,1024]{1,0:T(8,128)(2,1)S(1)}, u32[]{:S(2)}, u32[]{:S(2)}) collective-permute-start(bf16[16,1024]{1,0:T(8,128)(2,1)S(1)} %get-tuple-element.32), channel_id=1, source_target_pairs={{0,104},{8,112},{16,120},{24,0},{32,8},{40,16},{48,24},{56,32},{64... | collective-permute-start | bytes 98312 | tf_op jit(solution)/shard_map/ppermute | solution.py:115
  26.6 119.4 %collective-permute-start.3 = (bf16[16,1024]{1,0:T(8,128)(2,1)S(1)}, bf16[16,1024]{1,0:T(8,128)(2,1)S(1)}, u32[]{:S(2)}, u32[]{:S(2)}) collective-permute-start(bf16[16,1024]{1,0:T(8,128)(2,1)S(1)} %get-tuple-element.31), channel_id=1, source_target_pairs={{0,96},{8,104},{16,112},{24,120},{32,0},{40,8},{48,16},{56,24},{64... | collective-permute-start | bytes 98312 | tf_op jit(solution)/shard_map/ppermute | solution.py:115
  57.6 45.0 %collective-permute-start.16 = (bf16[128,64]{1,0:T(8,128)(2,1)S(1)}, bf16[128,64]{1,0:T(8,128)(2,1)S(1)}, u32[]{:S(2)}, u32[]{:S(2)}) collective-permute-start(bf16[128,64]{1,0:T(8,128)(2,1)S(1)} %get-tuple-element.40), channel_id=1, source_target_pairs={{0,6},{1,7},{2,0},{3,1},{4,2},{5,3},{6,4},{7,5},{8,14},{9,15},{10,... | collective-permute-start | bytes 49160 | tf_op jit(solution)/shard_map/ppermute | solution.py:127
  102.7 5.2 %collective-permute-start.17 = (bf16[128,64]{1,0:T(8,128)(2,1)S(1)}, bf16[128,64]{1,0:T(8,128)(2,1)S(1)}, u32[]{:S(2)}, u32[]{:S(2)}) collective-permute-start(bf16[128,64]{1,0:T(8,128)(2,1)S(1)} %get-tuple-element.39), channel_id=1, source_target_pairs={{0,5},{1,6},{2,7},{3,0},{4,1},{5,2},{6,3},{7,4},{8,13},{9,14},{10,... | collective-permute-start | bytes 49160 | tf_op jit(solution)/shard_map/ppermute | solution.py:127
  107.9 4.3 %collective-permute-start.18 = (bf16[128,64]{1,0:T(8,128)(2,1)S(1)}, bf16[128,64]{1,0:T(8,128)(2,1)S(1)}, u32[]{:S(2)}, u32[]{:S(2)}) collective-permute-start(bf16[128,64]{1,0:T(8,128)(2,1)S(1)} %get-tuple-element.38), channel_id=1, source_target_pairs={{0,4},{1,5},{2,6},{3,7},{4,0},{5,1},{6,2},{7,3},{8,12},{9,13},{10,... | collective-permute-start | bytes 49160 | tf_op jit(solution)/shard_map/ppermute | solution.py:127
  112.1 7.0 %collective-permute-start.19 = (bf16[128,64]{1,0:T(8,128)(2,1)S(1)}, bf16[128,64]{1,0:T(8,128)(2,1)S(1)}, u32[]{:S(2)}, u32[]{:S(2)}) collective-permute-start(bf16[128,64]{1,0:T(8,128)(2,1)S(1)} %get-tuple-element.37), channel_id=1, source_target_pairs={{0,3},{1,4},{2,5},{3,6},{4,7},{5,0},{6,1},{7,2},{8,11},{9,12},{10,... | collective-permute-start | bytes 49160 | tf_op jit(solution)/shard_map/ppermute | solution.py:127
  119.1 4.9 %collective-permute-start.20 = (bf16[128,64]{1,0:T(8,128)(2,1)S(1)}, bf16[128,64]{1,0:T(8,128)(2,1)S(1)}, u32[]{:S(2)}, u32[]{:S(2)}) collective-permute-start(bf16[128,64]{1,0:T(8,128)(2,1)S(1)} %get-tuple-element.36), channel_id=1, source_target_pairs={{0,2},{1,3},{2,4},{3,5},{4,6},{5,7},{6,0},{7,1},{8,10},{9,11},{10,... | collective-permute-start | bytes 49160 | tf_op jit(solution)/shard_map/ppermute | solution.py:127
  124.1 6.4 %collective-permute-start.21 = (bf16[128,64]{1,0:T(8,128)(2,1)S(1)}, bf16[128,64]{1,0:T(8,128)(2,1)S(1)}, u32[]{:S(2)}, u32[]{:S(2)}) collective-permute-start(bf16[128,64]{1,0:T(8,128)(2,1)S(1)} %get-tuple-element.35), channel_id=1, source_target_pairs={{0,1},{1,2},{2,3},{3,4},{4,5},{5,6},{6,7},{7,0},{8,9},{9,10},{10,1... | collective-permute-start | bytes 49160 | tf_op jit(solution)/shard_map/ppermute | solution.py:127
  130.5 17.5 %collective-permute-start.4 = (bf16[16,1024]{1,0:T(8,128)(2,1)S(1)}, bf16[16,1024]{1,0:T(8,128)(2,1)S(1)}, u32[]{:S(2)}, u32[]{:S(2)}) collective-permute-start(bf16[16,1024]{1,0:T(8,128)(2,1)S(1)} %get-tuple-element.30), channel_id=1, source_target_pairs={{0,88},{8,96},{16,104},{24,112},{32,120},{40,0},{48,8},{56,16},{64... | collective-permute-start | bytes 98312 | tf_op jit(solution)/shard_map/ppermute | solution.py:115
  142.9 5.8 %collective-permute-start.5 = (bf16[16,1024]{1,0:T(8,128)(2,1)S(1)}, bf16[16,1024]{1,0:T(8,128)(2,1)S(1)}, u32[]{:S(2)}, u32[]{:S(2)}) collective-permute-start(bf16[16,1024]{1,0:T(8,128)(2,1)S(1)} %get-tuple-element.29), channel_id=1, source_target_pairs={{0,80},{8,88},{16,96},{24,104},{32,112},{40,120},{48,0},{56,8},{64... | collective-permute-start | bytes 98312 | tf_op jit(solution)/shard_map/ppermute | solution.py:115
  145.2 4.9 %collective-permute-start.6 = (bf16[16,1024]{1,0:T(8,128)(2,1)S(1)}, bf16[16,1024]{1,0:T(8,128)(2,1)S(1)}, u32[]{:S(2)}, u32[]{:S(2)}) collective-permute-start(bf16[16,1024]{1,0:T(8,128)(2,1)S(1)} %get-tuple-element.28), channel_id=1, source_target_pairs={{0,72},{8,80},{16,88},{24,96},{32,104},{40,112},{48,120},{56,0},{6... | collective-permute-start | bytes 98312 | tf_op jit(solution)/shard_map/ppermute | solution.py:115
  145.2 6.6 %collective-permute-start.7 = (bf16[16,1024]{1,0:T(8,128)(2,1)S(1)}, bf16[16,1024]{1,0:T(8,128)(2,1)S(1)}, u32[]{:S(2)}, u32[]{:S(2)}) collective-permute-start(bf16[16,1024]{1,0:T(8,128)(2,1)S(1)} %get-tuple-element.27), channel_id=1, source_target_pairs={{0,64},{8,72},{16,80},{24,88},{32,96},{40,104},{48,112},{56,120},{... | collective-permute-start | bytes 98312 | tf_op jit(solution)/shard_map/ppermute | solution.py:115
  146.0 7.8 %collective-permute-start.8 = (bf16[16,1024]{1,0:T(8,128)(2,1)S(1)}, bf16[16,1024]{1,0:T(8,128)(2,1)S(1)}, u32[]{:S(2)}, u32[]{:S(2)}) collective-permute-start(bf16[16,1024]{1,0:T(8,128)(2,1)S(1)} %get-tuple-element.26), channel_id=1, source_target_pairs={{0,56},{8,64},{16,72},{24,80},{32,88},{40,96},{48,104},{56,112},{6... | collective-permute-start | bytes 98312 | tf_op jit(solution)/shard_map/ppermute | solution.py:115
  148.0 5.9 %collective-permute-start.9 = (bf16[16,1024]{1,0:T(8,128)(2,1)S(1)}, bf16[16,1024]{1,0:T(8,128)(2,1)S(1)}, u32[]{:S(2)}, u32[]{:S(2)}) collective-permute-start(bf16[16,1024]{1,0:T(8,128)(2,1)S(1)} %get-tuple-element.25), channel_id=1, source_target_pairs={{0,48},{8,56},{16,64},{24,72},{32,80},{40,88},{48,96},{56,104},{64... | collective-permute-start | bytes 98312 | tf_op jit(solution)/shard_map/ppermute | solution.py:115
  148.7 6.9 %collective-permute-start.10 = (bf16[16,1024]{1,0:T(8,128)(2,1)S(1)}, bf16[16,1024]{1,0:T(8,128)(2,1)S(1)}, u32[]{:S(2)}, u32[]{:S(2)}) collective-permute-start(bf16[16,1024]{1,0:T(8,128)(2,1)S(1)} %get-tuple-element.24), channel_id=1, source_target_pairs={{0,40},{8,48},{16,56},{24,64},{32,72},{40,80},{48,88},{56,96},{64,... | collective-permute-start | bytes 98312 | tf_op jit(solution)/shard_map/ppermute | solution.py:115
  150.1 5.5 %collective-permute-start.11 = (bf16[16,1024]{1,0:T(8,128)(2,1)S(1)}, bf16[16,1024]{1,0:T(8,128)(2,1)S(1)}, u32[]{:S(2)}, u32[]{:S(2)}) collective-permute-start(bf16[16,1024]{1,0:T(8,128)(2,1)S(1)} %get-tuple-element.23), channel_id=1, source_target_pairs={{0,32},{8,40},{16,48},{24,56},{32,64},{40,72},{48,80},{56,88},{64,... | collective-permute-start | bytes 98312 | tf_op jit(solution)/shard_map/ppermute | solution.py:115
  151.8 5.8 %collective-permute-start.12 = (bf16[16,1024]{1,0:T(8,128)(2,1)S(1)}, bf16[16,1024]{1,0:T(8,128)(2,1)S(1)}, u32[]{:S(2)}, u32[]{:S(2)}) collective-permute-start(bf16[16,1024]{1,0:T(8,128)(2,1)S(1)} %get-tuple-element.22), channel_id=1, source_target_pairs={{0,24},{8,32},{16,40},{24,48},{32,56},{40,64},{48,72},{56,80},{64,... | collective-permute-start | bytes 98312 | tf_op jit(solution)/shard_map/ppermute | solution.py:115
  153.9 4.9 %collective-permute-start.13 = (bf16[16,1024]{1,0:T(8,128)(2,1)S(1)}, bf16[16,1024]{1,0:T(8,128)(2,1)S(1)}, u32[]{:S(2)}, u32[]{:S(2)}) collective-permute-start(bf16[16,1024]{1,0:T(8,128)(2,1)S(1)} %get-tuple-element.21), channel_id=1, source_target_pairs={{0,16},{8,24},{16,32},{24,40},{32,48},{40,56},{48,64},{56,72},{64,... | collective-permute-start | bytes 98312 | tf_op jit(solution)/shard_map/ppermute | solution.py:115
  153.9 4.8 %collective-permute-start.14 = (bf16[16,1024]{1,0:T(8,128)(2,1)S(1)}, bf16[16,1024]{1,0:T(8,128)(2,1)S(1)}, u32[]{:S(2)}, u32[]{:S(2)}) collective-permute-start(bf16[16,1024]{1,0:T(8,128)(2,1)S(1)} %get-tuple-element.20), channel_id=1, source_target_pairs={{0,8},{8,16},{16,24},{24,32},{32,40},{40,48},{48,56},{56,64},{64,7... | collective-permute-start | bytes 98312 | tf_op jit(solution)/shard_map/ppermute | solution.py:115
  159.0 0.8 copy-start
  184.5 16.7 %all-to-all-start.2 = ((bf16[128,8,128]{2,1,0:T(8,128)(2,1)}), bf16[128,8,128]{2,1,0:T(8,128)(2,1)S(1)}, u32[]{:S(2)}, u32[]{:S(2)}) async-start(bf16[128,8,128]{2,1,0:T(8,128)(2,1)} %broadcast_in_dim.8), calls=%async_computation.2 | async-start | bytes 524288 | tf_op jit(solution)/shard_map/all_to_all | solution.py:90

commit v11 on v8

--- a/solution.py
+++ b/solution.py
@@ -38,7 +38,7 @@
         low_out[out, :] = new.astype(low_out.dtype)
 
 
-def adam_from_blocks(state, grad, per=2):
+def adam_from_blocks(state, grad, per=4):
     sources, stacked, cols = state.shape
     rows = stacked // 3
     block = pl.BlockSpec((per * rows, cols), lambda i: (i, 0))
@@ -60,7 +60,7 @@
             out_ref[j, pl.ds(k * rows, rows), :] = ref[:, cols]
 
 
-def pack_by_destination(master, first, second, dests, per=2):
+def pack_by_destination(master, first, second, dests, per=4):
     rows, cols = master.shape
     width = cols // dests
     block = pl.BlockSpec((rows, per * width), lambda i: (0, i))
@@ -127,8 +127,9 @@
     q_cols = q_term.shape[1]
     probe_query = sums[:, :q_cols].astype(jnp.bfloat16)
     kv_block = sums[:, q_cols:].astype(jnp.bfloat16)
-    kv_all = gather_rows(kv_block, ("fsdp", "tp"), fsdp * tp)
     tokens = kv_block.shape[0]
+    lanes = 128
+    kv_all = gather_rows(kv_block.reshape(tokens * slice_kv // lanes, lanes), ("fsdp", "tp"), fsdp * tp)
     kv_all = kv_all.reshape(fsdp, tp, tokens, slice_kv).transpose(0, 2, 1, 3)
     probe_keyvalue = kv_all.reshape(fsdp * tokens, tp * slice_kv)
     return (wq_new, wq_mom, wq_var, wkv_new, wkv_mom, wkv_var, probe_query, probe_keyvalue)

time: 203 us -> 200 us (0.985)
  Pallas kernels: 12.8 us -> 10.6 us
where the time goes in v11:
time: 200 us
  starting transfers between devices  112 us (56%)
  waiting for transfers between devices  54.8 us (27%)
  blocking collectives  15.3 us (8%)
  Pallas kernels  10.6 us (5%)
  local copies, waits for them, and re-layouts  3.58 us (2%)
    ppermute x7, starting transfers between devices, step(): lax.ppermute(block, 'tp', [(i, (i + k) % tp) for i in range(tp)])  65.1 us
    ppermute x7, waiting for transfers between devices, step(): lax.ppermute(block, 'tp', [(i, (i + k) % tp) for i in range(tp)])  41.7 us
    ppermute x15, starting transfers between devices, step(): lax.ppermute(block, 'fsdp', [(i, (i + k) % fsdp) for i in range(fsdp)])  32.1 us
    all_to_all x1, blocking collectives, scatter_sum_rows(): lax.all_to_all(x, axis_name, split_axis=0, concat_axis=0, tiled=True)  15.3 us
    all_to_all x1, waiting for transfers between devices, gather_rows(): lax.all_to_all(copies, axis_name, split_axis=0, concat_axis=0, tiled=True)  9.97 us
    all_to_all x1, starting transfers between devices, step(): state = lax.all_to_all(send, 'tp', split_axis=0, concat_axis=0, tiled=True)  8.29 us
    all_to_all x1, starting transfers between devices, gather_rows(): lax.all_to_all(copies, axis_name, split_axis=0, concat_axis=0, tiled=True)  6.07 us
    pallas_call x1, Pallas kernels, adam_from_blocks(): pl.pallas_call(adam_kernel, grid=(sources // per,), in_specs=[pl.BlockSpe...  5.86 us
  transfers between devices with their start and end apart: 24, of which 10 were waited for; matrix products, arithmetic and copies ran while one was open for 1% of the time, Pallas kernels for 0%

profile of v11, /device:TPU:1, one launch (start us, length us, event | category | flops | bytes accessed | tf_op | source)
XLA Modules:
  0.0 200.0 jit_solution(2361685469053361939)
XLA Ops:
  0.6 4.7 %shard_map.152 = f32[8,384,512]{2,1,0:T(8,128)} custom-call(f32[128,4096]{1,0:T(8,128)} %master_ref.1, f32[128,4096]{1,0:T(8,128)} %first_ref.1, f32[128,4096]{1,0:T(8,128)} %second_ref.1), custom_call_target="tpu_custom_call" | custom-call | tf_op jit(solution)/shard_map/pallas_call | solution.py:67
  5.4 8.3 %all-to-all-start = ((f32[8,384,512]{2,1,0:T(8,128)}), f32[8,384,512]{2,1,0:T(8,128)}, u32[]{:S(2)}, u32[]{:S(2)}) async-start(f32[8,384,512]{2,1,0:T(8,128)} %shard_map.152), calls=%async_computation | async-start | bytes 12582912 | tf_op jit(solution)/shard_map/all_to_all | solution.py:122
  13.8 1.0 fusion.1
  14.8 0.1 constant_dynamic-slice_fusion.1
  14.9 5.0 %collective-permute-start.15 = (bf16[128,64]{1,0:T(8,128)(2,1)S(1)}, bf16[128,64]{1,0:T(8,128)(2,1)S(1)}, u32[]{:S(2)}, u32[]{:S(2)}) collective-permute-start(bf16[128,64]{1,0:T(8,128)(2,1)S(1)} %get-tuple-element.41), channel_id=1, source_target_pairs={{0,7},{1,0},{2,1},{3,2},{4,3},{5,4},{6,5},{7,6},{8,15},{9,8},{10,9... | collective-permute-start | bytes 49160 | tf_op jit(solution)/shard_map/ppermute | solution.py:115
  20.0 1.6 collective-permute-start
  21.6 3.2 %collective-permute-start.1 = (bf16[16,1024]{1,0:T(8,128)(2,1)S(1)}, bf16[16,1024]{1,0:T(8,128)(2,1)S(1)}, u32[]{:S(2)}, u32[]{:S(2)}) collective-permute-start(bf16[16,1024]{1,0:T(8,128)(2,1)S(1)} %get-tuple-element.33), channel_id=1, source_target_pairs={{0,112},{8,120},{16,0},{24,8},{32,16},{40,24},{48,32},{56,40},{64,... | collective-permute-start | bytes 98312 | tf_op jit(solution)/shard_map/ppermute | solution.py:103
  24.8 0.7 collective-permute-start.2
  25.5 2.0 %collective-permute-start.3 = (bf16[16,1024]{1,0:T(8,128)(2,1)S(1)}, bf16[16,1024]{1,0:T(8,128)(2,1)S(1)}, u32[]{:S(2)}, u32[]{:S(2)}) collective-permute-start(bf16[16,1024]{1,0:T(8,128)(2,1)S(1)} %get-tuple-element.31), channel_id=1, source_target_pairs={{0,96},{8,104},{16,112},{24,120},{32,0},{40,8},{48,16},{56,24},{64... | collective-permute-start | bytes 98312 | tf_op jit(solution)/shard_map/ppermute | solution.py:103
  27.5 29.0 %collective-permute-done.15 = bf16[128,64]{1,0:T(8,128)(2,1)S(1)} collective-permute-done((bf16[128,64]{1,0:T(8,128)(2,1)S(1)}, bf16[128,64]{1,0:T(8,128)(2,1)S(1)}, u32[]{:S(2)}, u32[]{:S(2)}) %collective-permute-start.15) | collective-permute-done | bytes 16416 | tf_op jit(solution)/shard_map/ppermute | solution.py:115
  56.5 42.3 %collective-permute-start.16 = (bf16[128,64]{1,0:T(8,128)(2,1)S(1)}, bf16[128,64]{1,0:T(8,128)(2,1)S(1)}, u32[]{:S(2)}, u32[]{:S(2)}) collective-permute-start(bf16[128,64]{1,0:T(8,128)(2,1)S(1)} %get-tuple-element.40), channel_id=1, source_target_pairs={{0,6},{1,7},{2,0},{3,1},{4,2},{5,3},{6,4},{7,5},{8,14},{9,15},{10,... | collective-permute-start | bytes 49160 | tf_op jit(solution)/shard_map/ppermute | solution.py:115
  98.8 2.7 %collective-permute-done.16 = bf16[128,64]{1,0:T(8,128)(2,1)S(1)} collective-permute-done((bf16[128,64]{1,0:T(8,128)(2,1)S(1)}, bf16[128,64]{1,0:T(8,128)(2,1)S(1)}, u32[]{:S(2)}, u32[]{:S(2)}) %collective-permute-start.16) | collective-permute-done | bytes 16416 | tf_op jit(solution)/shard_map/ppermute | solution.py:115
  101.5 4.1 %collective-permute-start.17 = (bf16[128,64]{1,0:T(8,128)(2,1)S(1)}, bf16[128,64]{1,0:T(8,128)(2,1)S(1)}, u32[]{:S(2)}, u32[]{:S(2)}) collective-permute-start(bf16[128,64]{1,0:T(8,128)(2,1)S(1)} %get-tuple-element.39), channel_id=1, source_target_pairs={{0,5},{1,6},{2,7},{3,0},{4,1},{5,2},{6,3},{7,4},{8,13},{9,14},{10,... | collective-permute-start | bytes 49160 | tf_op jit(solution)/shard_map/ppermute | solution.py:115
  105.6 1.1 collective-permute-done.17
  106.7 2.8 %collective-permute-start.18 = (bf16[128,64]{1,0:T(8,128)(2,1)S(1)}, bf16[128,64]{1,0:T(8,128)(2,1)S(1)}, u32[]{:S(2)}, u32[]{:S(2)}) collective-permute-start(bf16[128,64]{1,0:T(8,128)(2,1)S(1)} %get-tuple-element.38), channel_id=1, source_target_pairs={{0,4},{1,5},{2,6},{3,7},{4,0},{5,1},{6,2},{7,3},{8,12},{9,13},{10,... | collective-permute-start | bytes 49160 | tf_op jit(solution)/shard_map/ppermute | solution.py:115
  109.5 1.5 collective-permute-done.18
  111.0 5.2 %collective-permute-start.19 = (bf16[128,64]{1,0:T(8,128)(2,1)S(1)}, bf16[128,64]{1,0:T(8,128)(2,1)S(1)}, u32[]{:S(2)}, u32[]{:S(2)}) collective-permute-start(bf16[128,64]{1,0:T(8,128)(2,1)S(1)} %get-tuple-element.37), channel_id=1, source_target_pairs={{0,3},{1,4},{2,5},{3,6},{4,7},{5,0},{6,1},{7,2},{8,11},{9,12},{10,... | collective-permute-start | bytes 49160 | tf_op jit(solution)/shard_map/ppermute | solution.py:115
  116.2 1.8 collective-permute-done.19
  118.0 1.5 collective-permute-start.20
  119.5 3.4 %collective-permute-done.20 = bf16[128,64]{1,0:T(8,128)(2,1)S(1)} collective-permute-done((bf16[128,64]{1,0:T(8,128)(2,1)S(1)}, bf16[128,64]{1,0:T(8,128)(2,1)S(1)}, u32[]{:S(2)}, u32[]{:S(2)}) %collective-permute-start.20) | collective-permute-done | bytes 16416 | tf_op jit(solution)/shard_map/ppermute | solution.py:115
  122.9 4.1 %collective-permute-start.21 = (bf16[128,64]{1,0:T(8,128)(2,1)S(1)}, bf16[128,64]{1,0:T(8,128)(2,1)S(1)}, u32[]{:S(2)}, u32[]{:S(2)}) collective-permute-start(bf16[128,64]{1,0:T(8,128)(2,1)S(1)} %get-tuple-element.35), channel_id=1, source_target_pairs={{0,1},{1,2},{2,3},{3,4},{4,5},{5,6},{6,7},{7,0},{8,9},{9,10},{10,1... | collective-permute-start | bytes 49160 | tf_op jit(solution)/shard_map/ppermute | solution.py:115
  127.1 2.2 %collective-permute-done.21 = bf16[128,64]{1,0:T(8,128)(2,1)S(1)} collective-permute-done((bf16[128,64]{1,0:T(8,128)(2,1)S(1)}, bf16[128,64]{1,0:T(8,128)(2,1)S(1)}, u32[]{:S(2)}, u32[]{:S(2)}) %collective-permute-start.21) | collective-permute-done | bytes 16416 | tf_op jit(solution)/shard_map/ppermute | solution.py:115
  129.3 12.0 %collective-permute-start.4 = (bf16[16,1024]{1,0:T(8,128)(2,1)S(1)}, bf16[16,1024]{1,0:T(8,128)(2,1)S(1)}, u32[]{:S(2)}, u32[]{:S(2)}) collective-permute-start(bf16[16,1024]{1,0:T(8,128)(2,1)S(1)} %get-tuple-element.30), channel_id=1, source_target_pairs={{0,88},{8,96},{16,104},{24,112},{32,120},{40,0},{48,8},{56,16},{64... | collective-permute-start | bytes 98312 | tf_op jit(solution)/shard_map/ppermute | solution.py:103
  141.4 0.1 constant_dynamic-update-slice_fusion.40
  141.6 0.1 constant_dynamic-update-slice_fusion.32
  141.7 2.3 %collective-permute-start.5 = (bf16[16,1024]{1,0:T(8,128)(2,1)S(1)}, bf16[16,1024]{1,0:T(8,128)(2,1)S(1)}, u32[]{:S(2)}, u32[]{:S(2)}) collective-permute-start(bf16[16,1024]{1,0:T(8,128)(2,1)S(1)} %get-tuple-element.29), channel_id=1, source_target_pairs={{0,80},{8,88},{16,96},{24,104},{32,112},{40,120},{48,0},{56,8},{64... | collective-permute-start | bytes 98312 | tf_op jit(solution)/shard_map/ppermute | solution.py:103
  144.1 0.8 collective-permute-start.7
  144.9 1.9 collective-permute-start.8
  146.8 0.7 collective-permute-start.9
  147.5 1.4 collective-permute-start.10
  148.9 1.7 collective-permute-start.11
  150.6 2.1 %collective-permute-start.12 = (bf16[16,1024]{1,0:T(8,128)(2,1)S(1)}, bf16[16,1024]{1,0:T(8,128)(2,1)S(1)}, u32[]{:S(2)}, u32[]{:S(2)}) collective-permute-start(bf16[16,1024]{1,0:T(8,128)(2,1)S(1)} %get-tuple-element.22), channel_id=1, source_target_pairs={{0,24},{8,32},{16,40},{24,48},{32,56},{40,64},{48,72},{56,80},{64,... | collective-permute-start | bytes 98312 | tf_op jit(solution)/shard_map/ppermute | solution.py:103
  152.8 1.7 collective-permute-start.14
  154.4 2.0 collective-permute-done.12
  156.4 1.2 collective-permute-done.13
  157.9 0.3 fusion.4
  158.2 5.9 %shard_map.153 = (f32[1024,512]{1,0:T(8,128)}, f32[1024,512]{1,0:T(8,128)}, f32[1024,512]{1,0:T(8,128)}, bf16[1024,512]{1,0:T(8,128)(2,1)}) custom-call(f32[8,384,512]{2,1,0:T(8,128)} %all-to-all-done.state_ref, f32[1024,512]{1,0:T(8,128)} %grad_ref.1), custom_call_target="tpu_custom_call" | custom-call | tf_op jit(solution)/shard_map/pallas_call | solution.py:46
  164.1 1.7 fusion.3
  165.7 0.1 pad_maximum_fusion
  165.8 15.3 %all_to_all.20 = f32[16,16,576]{2,1,0:T(8,128)S(1)} all-to-all(f32[16,16,576]{2,1,0:T(8,128)S(1)} %bitcast.84), channel_id=1, replica_groups=mesh['fsdp'=16,'tp'=8] {'fsdp'}, dimensions={0} | all-to-all | bytes 1179648 | tf_op jit(solution)/shard_map/all_to_all | solution.py:82
  181.1 0.1 broadcast_in_dim.7
  181.2 0.7 broadcast_in_dim.8
  181.9 6.1 %all-to-all-start.2 = ((bf16[128,8,128]{2,1,0:T(8,128)(2,1)}), bf16[128,8,128]{2,1,0:T(8,128)(2,1)S(1)}, u32[]{:S(2)}, u32[]{:S(2)}) async-start(bf16[128,8,128]{2,1,0:T(8,128)(2,1)} %broadcast_in_dim.8), calls=%async_computation.2 | async-start | bytes 524288 | tf_op jit(solution)/shard_map/all_to_all | solution.py:78
  188.0 0.6 slice.10
  188.6 10.0 %all-to-all-done.2 = bf16[128,8,128]{2,1,0:T(8,128)(2,1)S(1)} async-done(((bf16[128,8,128]{2,1,0:T(8,128)(2,1)}), bf16[128,8,128]{2,1,0:T(8,128)(2,1)S(1)}, u32[]{:S(2)}, u32[]{:S(2)}) %all-to-all-start.2) | async-done | bytes 262176 | tf_op jit(solution)/shard_map/all_to_all | solution.py:78
  198.6 0.2 reshape.40
  198.8 0.1 copy.20
  199.0 1.0 reshape.41
  (77 shorter events, 0.5 us)
Async XLA Ops:
  5.4 8.4 %copy-start.1 = (f32[128,512]{1,0:T(8,128)S(1)}, f32[128,512]{1,0:T(8,128)}, u32[]{:S(2)}) copy-start(f32[128,512]{1,0:T(8,128)} %param.14) | copy-start | bytes 786436
  5.4 8.4 %copy-start.2 = (f32[128,512]{1,0:T(8,128)S(1)}, f32[128,512]{1,0:T(8,128)}, u32[]{:S(2)}) copy-start(f32[128,512]{1,0:T(8,128)} %param.17) | copy-start | bytes 786436
  5.4 8.4 %copy-start.3 = (f32[128,512]{1,0:T(8,128)S(1)}, f32[128,512]{1,0:T(8,128)}, u32[]{:S(2)}) copy-start(f32[128,512]{1,0:T(8,128)} %param.16) | copy-start | bytes 786436
  5.4 8.4 %copy-start.4 = (f32[128,512]{1,0:T(8,128)S(1)}, f32[128,512]{1,0:T(8,128)}, u32[]{:S(2)}) copy-start(f32[128,512]{1,0:T(8,128)} %param.15) | copy-start | bytes 786436
  5.4 152.8 %all-to-all-start = ((f32[8,384,512]{2,1,0:T(8,128)}), f32[8,384,512]{2,1,0:T(8,128)}, u32[]{:S(2)}, u32[]{:S(2)}) async-start(f32[8,384,512]{2,1,0:T(8,128)} %shard_map.152), calls=%async_computation | async-start | bytes 12582912 | tf_op jit(solution)/shard_map/all_to_all | solution.py:122
  13.7 6.3 %copy-start = (bf16[16,16384]{1,0:T(8,128)(2,1)S(1)}, bf16[16,16384]{1,0:T(8,128)(2,1)}, u32[]{:S(2)}) copy-start(bf16[16,16384]{1,0:T(8,128)(2,1)} %param.9) | copy-start | bytes 1572868
  14.9 41.6 %collective-permute-start.15 = (bf16[128,64]{1,0:T(8,128)(2,1)S(1)}, bf16[128,64]{1,0:T(8,128)(2,1)S(1)}, u32[]{:S(2)}, u32[]{:S(2)}) collective-permute-start(bf16[128,64]{1,0:T(8,128)(2,1)S(1)} %get-tuple-element.41), channel_id=1, source_target_pairs={{0,7},{1,0},{2,1},{3,2},{4,3},{5,4},{6,5},{7,6},{8,15},{9,8},{10,9... | collective-permute-start | bytes 49160 | tf_op jit(solution)/shard_map/ppermute | solution.py:115
  20.0 121.7 %collective-permute-start = (bf16[16,1024]{1,0:T(8,128)(2,1)S(1)}, bf16[16,1024]{1,0:T(8,128)(2,1)S(1)}, u32[]{:S(2)}, u32[]{:S(2)}) collective-permute-start(bf16[16,1024]{1,0:T(8,128)(2,1)S(1)} %get-tuple-element.34), channel_id=1, source_target_pairs={{0,120},{8,0},{16,8},{24,16},{32,24},{40,32},{48,40},{56,48},{64,5... | collective-permute-start | bytes 98312 | tf_op jit(solution)/shard_map/ppermute | solution.py:103
  21.6 122.4 %collective-permute-start.1 = (bf16[16,1024]{1,0:T(8,128)(2,1)S(1)}, bf16[16,1024]{1,0:T(8,128)(2,1)S(1)}, u32[]{:S(2)}, u32[]{:S(2)}) collective-permute-start(bf16[16,1024]{1,0:T(8,128)(2,1)S(1)} %get-tuple-element.33), channel_id=1, source_target_pairs={{0,112},{8,120},{16,0},{24,8},{32,16},{40,24},{48,32},{56,40},{64,... | collective-permute-start | bytes 98312 | tf_op jit(solution)/shard_map/ppermute | solution.py:103
  24.8 119.3 %collective-permute-start.2 = (bf16[16,1024]{1,0:T(8,128)(2,1)S(1)}, bf16[16,1024]{1,0:T(8,128)(2,1)S(1)}, u32[]{:S(2)}, u32[]{:S(2)}) collective-permute-start(bf16[16,1024]{1,0:T(8,128)(2,1)S(1)} %get-tuple-element.32), channel_id=1, source_target_pairs={{0,104},{8,112},{16,120},{24,0},{32,8},{40,16},{48,24},{56,32},{64... | collective-permute-start | bytes 98312 | tf_op jit(solution)/shard_map/ppermute | solution.py:103
  25.5 119.4 %collective-permute-start.3 = (bf16[16,1024]{1,0:T(8,128)(2,1)S(1)}, bf16[16,1024]{1,0:T(8,128)(2,1)S(1)}, u32[]{:S(2)}, u32[]{:S(2)}) collective-permute-start(bf16[16,1024]{1,0:T(8,128)(2,1)S(1)} %get-tuple-element.31), channel_id=1, source_target_pairs={{0,96},{8,104},{16,112},{24,120},{32,0},{40,8},{48,16},{56,24},{64... | collective-permute-start | bytes 98312 | tf_op jit(solution)/shard_map/ppermute | solution.py:103
  56.5 45.0 %collective-permute-start.16 = (bf16[128,64]{1,0:T(8,128)(2,1)S(1)}, bf16[128,64]{1,0:T(8,128)(2,1)S(1)}, u32[]{:S(2)}, u32[]{:S(2)}) collective-permute-start(bf16[128,64]{1,0:T(8,128)(2,1)S(1)} %get-tuple-element.40), channel_id=1, source_target_pairs={{0,6},{1,7},{2,0},{3,1},{4,2},{5,3},{6,4},{7,5},{8,14},{9,15},{10,... | collective-permute-start | bytes 49160 | tf_op jit(solution)/shard_map/ppermute | solution.py:115
  101.5 5.2 %collective-permute-start.17 = (bf16[128,64]{1,0:T(8,128)(2,1)S(1)}, bf16[128,64]{1,0:T(8,128)(2,1)S(1)}, u32[]{:S(2)}, u32[]{:S(2)}) collective-permute-start(bf16[128,64]{1,0:T(8,128)(2,1)S(1)} %get-tuple-element.39), channel_id=1, source_target_pairs={{0,5},{1,6},{2,7},{3,0},{4,1},{5,2},{6,3},{7,4},{8,13},{9,14},{10,... | collective-permute-start | bytes 49160 | tf_op jit(solution)/shard_map/ppermute | solution.py:115
  106.7 4.3 %collective-permute-start.18 = (bf16[128,64]{1,0:T(8,128)(2,1)S(1)}, bf16[128,64]{1,0:T(8,128)(2,1)S(1)}, u32[]{:S(2)}, u32[]{:S(2)}) collective-permute-start(bf16[128,64]{1,0:T(8,128)(2,1)S(1)} %get-tuple-element.38), channel_id=1, source_target_pairs={{0,4},{1,5},{2,6},{3,7},{4,0},{5,1},{6,2},{7,3},{8,12},{9,13},{10,... | collective-permute-start | bytes 49160 | tf_op jit(solution)/shard_map/ppermute | solution.py:115
  111.0 7.0 %collective-permute-start.19 = (bf16[128,64]{1,0:T(8,128)(2,1)S(1)}, bf16[128,64]{1,0:T(8,128)(2,1)S(1)}, u32[]{:S(2)}, u32[]{:S(2)}) collective-permute-start(bf16[128,64]{1,0:T(8,128)(2,1)S(1)} %get-tuple-element.37), channel_id=1, source_target_pairs={{0,3},{1,4},{2,5},{3,6},{4,7},{5,0},{6,1},{7,2},{8,11},{9,12},{10,... | collective-permute-start | bytes 49160 | tf_op jit(solution)/shard_map/ppermute | solution.py:115
  118.0 4.9 %collective-permute-start.20 = (bf16[128,64]{1,0:T(8,128)(2,1)S(1)}, bf16[128,64]{1,0:T(8,128)(2,1)S(1)}, u32[]{:S(2)}, u32[]{:S(2)}) collective-permute-start(bf16[128,64]{1,0:T(8,128)(2,1)S(1)} %get-tuple-element.36), channel_id=1, source_target_pairs={{0,2},{1,3},{2,4},{3,5},{4,6},{5,7},{6,0},{7,1},{8,10},{9,11},{10,... | collective-permute-start | bytes 49160 | tf_op jit(solution)/shard_map/ppermute | solution.py:115
  122.9 6.4 %collective-permute-start.21 = (bf16[128,64]{1,0:T(8,128)(2,1)S(1)}, bf16[128,64]{1,0:T(8,128)(2,1)S(1)}, u32[]{:S(2)}, u32[]{:S(2)}) collective-permute-start(bf16[128,64]{1,0:T(8,128)(2,1)S(1)} %get-tuple-element.35), channel_id=1, source_target_pairs={{0,1},{1,2},{2,3},{3,4},{4,5},{5,6},{6,7},{7,0},{8,9},{9,10},{10,1... | collective-permute-start | bytes 49160 | tf_op jit(solution)/shard_map/ppermute | solution.py:115
  129.3 17.5 %collective-permute-start.4 = (bf16[16,1024]{1,0:T(8,128)(2,1)S(1)}, bf16[16,1024]{1,0:T(8,128)(2,1)S(1)}, u32[]{:S(2)}, u32[]{:S(2)}) collective-permute-start(bf16[16,1024]{1,0:T(8,128)(2,1)S(1)} %get-tuple-element.30), channel_id=1, source_target_pairs={{0,88},{8,96},{16,104},{24,112},{32,120},{40,0},{48,8},{56,16},{64... | collective-permute-start | bytes 98312 | tf_op jit(solution)/shard_map/ppermute | solution.py:103
  141.7 5.8 %collective-permute-start.5 = (bf16[16,1024]{1,0:T(8,128)(2,1)S(1)}, bf16[16,1024]{1,0:T(8,128)(2,1)S(1)}, u32[]{:S(2)}, u32[]{:S(2)}) collective-permute-start(bf16[16,1024]{1,0:T(8,128)(2,1)S(1)} %get-tuple-element.29), channel_id=1, source_target_pairs={{0,80},{8,88},{16,96},{24,104},{32,112},{40,120},{48,0},{56,8},{64... | collective-permute-start | bytes 98312 | tf_op jit(solution)/shard_map/ppermute | solution.py:103
  144.0 4.9 %collective-permute-start.6 = (bf16[16,1024]{1,0:T(8,128)(2,1)S(1)}, bf16[16,1024]{1,0:T(8,128)(2,1)S(1)}, u32[]{:S(2)}, u32[]{:S(2)}) collective-permute-start(bf16[16,1024]{1,0:T(8,128)(2,1)S(1)} %get-tuple-element.28), channel_id=1, source_target_pairs={{0,72},{8,80},{16,88},{24,96},{32,104},{40,112},{48,120},{56,0},{6... | collective-permute-start | bytes 98312 | tf_op jit(solution)/shard_map/ppermute | solution.py:103
  144.1 6.6 %collective-permute-start.7 = (bf16[16,1024]{1,0:T(8,128)(2,1)S(1)}, bf16[16,1024]{1,0:T(8,128)(2,1)S(1)}, u32[]{:S(2)}, u32[]{:S(2)}) collective-permute-start(bf16[16,1024]{1,0:T(8,128)(2,1)S(1)} %get-tuple-element.27), channel_id=1, source_target_pairs={{0,64},{8,72},{16,80},{24,88},{32,96},{40,104},{48,112},{56,120},{... | collective-permute-start | bytes 98312 | tf_op jit(solution)/shard_map/ppermute | solution.py:103
  144.9 7.8 %collective-permute-start.8 = (bf16[16,1024]{1,0:T(8,128)(2,1)S(1)}, bf16[16,1024]{1,0:T(8,128)(2,1)S(1)}, u32[]{:S(2)}, u32[]{:S(2)}) collective-permute-start(bf16[16,1024]{1,0:T(8,128)(2,1)S(1)} %get-tuple-element.26), channel_id=1, source_target_pairs={{0,56},{8,64},{16,72},{24,80},{32,88},{40,96},{48,104},{56,112},{6... | collective-permute-start | bytes 98312 | tf_op jit(solution)/shard_map/ppermute | solution.py:103
  146.8 5.9 %collective-permute-start.9 = (bf16[16,1024]{1,0:T(8,128)(2,1)S(1)}, bf16[16,1024]{1,0:T(8,128)(2,1)S(1)}, u32[]{:S(2)}, u32[]{:S(2)}) collective-permute-start(bf16[16,1024]{1,0:T(8,128)(2,1)S(1)} %get-tuple-element.25), channel_id=1, source_target_pairs={{0,48},{8,56},{16,64},{24,72},{32,80},{40,88},{48,96},{56,104},{64... | collective-permute-start | bytes 98312 | tf_op jit(solution)/shard_map/ppermute | solution.py:103
  147.5 6.9 %collective-permute-start.10 = (bf16[16,1024]{1,0:T(8,128)(2,1)S(1)}, bf16[16,1024]{1,0:T(8,128)(2,1)S(1)}, u32[]{:S(2)}, u32[]{:S(2)}) collective-permute-start(bf16[16,1024]{1,0:T(8,128)(2,1)S(1)} %get-tuple-element.24), channel_id=1, source_target_pairs={{0,40},{8,48},{16,56},{24,64},{32,72},{40,80},{48,88},{56,96},{64,... | collective-permute-start | bytes 98312 | tf_op jit(solution)/shard_map/ppermute | solution.py:103
  148.9 5.5 %collective-permute-start.11 = (bf16[16,1024]{1,0:T(8,128)(2,1)S(1)}, bf16[16,1024]{1,0:T(8,128)(2,1)S(1)}, u32[]{:S(2)}, u32[]{:S(2)}) collective-permute-start(bf16[16,1024]{1,0:T(8,128)(2,1)S(1)} %get-tuple-element.23), channel_id=1, source_target_pairs={{0,32},{8,40},{16,48},{24,56},{32,64},{40,72},{48,80},{56,88},{64,... | collective-permute-start | bytes 98312 | tf_op jit(solution)/shard_map/ppermute | solution.py:103
  150.6 5.8 %collective-permute-start.12 = (bf16[16,1024]{1,0:T(8,128)(2,1)S(1)}, bf16[16,1024]{1,0:T(8,128)(2,1)S(1)}, u32[]{:S(2)}, u32[]{:S(2)}) collective-permute-start(bf16[16,1024]{1,0:T(8,128)(2,1)S(1)} %get-tuple-element.22), channel_id=1, source_target_pairs={{0,24},{8,32},{16,40},{24,48},{32,56},{40,64},{48,72},{56,80},{64,... | collective-permute-start | bytes 98312 | tf_op jit(solution)/shard_map/ppermute | solution.py:103
  152.7 4.9 %collective-permute-start.13 = (bf16[16,1024]{1,0:T(8,128)(2,1)S(1)}, bf16[16,1024]{1,0:T(8,128)(2,1)S(1)}, u32[]{:S(2)}, u32[]{:S(2)}) collective-permute-start(bf16[16,1024]{1,0:T(8,128)(2,1)S(1)} %get-tuple-element.21), channel_id=1, source_target_pairs={{0,16},{8,24},{16,32},{24,40},{32,48},{40,56},{48,64},{56,72},{64,... | collective-permute-start | bytes 98312 | tf_op jit(solution)/shard_map/ppermute | solution.py:103
  152.8 4.8 %collective-permute-start.14 = (bf16[16,1024]{1,0:T(8,128)(2,1)S(1)}, bf16[16,1024]{1,0:T(8,128)(2,1)S(1)}, u32[]{:S(2)}, u32[]{:S(2)}) collective-permute-start(bf16[16,1024]{1,0:T(8,128)(2,1)S(1)} %get-tuple-element.20), channel_id=1, source_target_pairs={{0,8},{8,16},{16,24},{24,32},{32,40},{40,48},{48,56},{56,64},{64,7... | collective-permute-start | bytes 98312 | tf_op jit(solution)/shard_map/ppermute | solution.py:103
  181.9 16.7 %all-to-all-start.2 = ((bf16[128,8,128]{2,1,0:T(8,128)(2,1)}), bf16[128,8,128]{2,1,0:T(8,128)(2,1)S(1)}, u32[]{:S(2)}, u32[]{:S(2)}) async-start(bf16[128,8,128]{2,1,0:T(8,128)(2,1)} %broadcast_in_dim.8), calls=%async_computation.2 | async-start | bytes 524288 | tf_op jit(solution)/shard_map/all_to_all | solution.py:78
